TPU v7x, 1024 devices: a whole 8x8x8 slice. The times are simulated.
1024 devices in a mesh: row: 64 (over z_hi, y, core), col: 16 (over x, z_lo).
Axes of the slice: x: 8, y: 8, z: 8 (z_hi: 4, z_lo: 2; z = z_hi * 2 + z_lo), core: 2. Of those that a mesh axis runs over, the one named last changes fastest.
Arguments:
- a_tiles: float32 [64, 16, 3, 256, 256], P('row', 'col'), may hold values from -0.375 to 0.375
- b_tiles: float32 [64, 16, 3, 256, 256], P('row', 'col'), may hold values from -6 to 6
- a_rows: int32 [64, 16, 3], P('row', 'col'), may hold values from 0 to 7, as said below
- b_cols: int32 [64, 16, 3], P('row', 'col'), may hold values from 0 to 31, as said below
- c_shape: int32 [64, 16, 6, 2], P('row', 'col'), may hold values from 0 to 31, as said below
- pairs: int32 [64, 16, 3, 6, 2], P('row', 'col'), may hold values from 0 to 2, as said below
- pair_count: int32 [64, 16, 3], P('row', 'col'), may hold values from 1 to 6, as said below
Outputs:
- c_tiles: float32 [64, 16, 6, 256, 256], P('row', 'col')
Inputs may be any that keep to these rules, and one draw needn't show every extreme that they name: `a_rows`: in each row block every device's A slots name the same 3 distinct tile rows, each device in its own order. `b_cols`: in each column block every device's B slots name the same 3 distinct tile columns, each device in its own order. `c_shape`: each device's result slots are distinct combinations of its row block's A tile rows and its column block's B tile columns. The first pair_count pairs of a device and step are live; live pairs of one step have distinct targets, and every target appears in c_shape. `pair_count`: some device and step lists all 6 pairs.
All inputs are finite; a program needn't handle non-finite values.
Results may differ from a plain program's by a relative error of at most 0.0003.
Values sent between devices are 32-bit elements; how exact they have to be, the bound alone decides.
No kernel may reach another device: no remote copies, remote signals or barrier semaphores. Data moves between devices by JAX's collectives and lax.ppermute only.
A program may use at most 32 MiB of HBM per device.

v0:
```python
import jax
import jax.numpy as jnp
from jax import lax
from jax.experimental import pallas as pl
from jax.experimental.pallas import tpu as pltpu
from jax.sharding import PartitionSpec as P


STEPS, SLOTS, SIDE, RESULTS = 3, 3, 256, 6
RING, PAIR, PLANES = 8, 2, 4
SHARD = 160
SHARDS = 5
PANEL = SHARD * SHARDS
LIST_ROW = SLOTS * SIDE

HOLDERS = (
    ((0, 0), (0, 1), (7, 0), (6, 0), (5, 0)),
    ((6, 1), (7, 1), (2, 1), (3, 1), (4, 1)),
    ((1, 0), (1, 1), (2, 0), (3, 0), (4, 0)),
)
HOLDER = tuple(tuple(ring * PAIR + pair for ring, pair in panel) for panel in HOLDERS)
SLOT_OF = [STEPS * SHARDS] * (RING * PAIR)
for _s in range(STEPS):
    for _k in range(SHARDS):
        SLOT_OF[HOLDER[_s][_k]] = _s * SHARDS + _k

SCATTER = [
    [(s, HOLDER[s][k]) for s in range(STEPS) if HOLDER[s][k] != s] for k in range(SHARDS)
]


def ring_x():
    columns = RING * PAIR
    pairs = []
    for r in range(PLANES * RING * PAIR):
        for c in range(columns):
            to = (c + (PAIR if r % PAIR == 0 else -PAIR)) % columns
            pairs.append((r * columns + c, r * columns + to))
    return pairs


def ring_y(step):
    pairs = []
    for z in range(PLANES):
        for y in range(RING):
            for core in range(PAIR):
                to = (y + (step if core == 0 else -step)) % RING
                pairs.append(((z * RING + y) * PAIR + core, (z * RING + to) * PAIR + core))
    return pairs


SWAP_Z = [(c, c ^ 1) for c in range(RING * PAIR)]
SWAP_CORE = [(r, r ^ 1) for r in range(PLANES * RING * PAIR)]


def to_plane(z):
    return [(r, z * RING * PAIR + r) for r in range(RING * PAIR)]


def scatter(tiles, listed, axis, index):
    panel = tiles.reshape(SLOTS * SIDE, SIDE)
    spare = jnp.pad(listed.astype(jnp.float32)[None, :], ((0, PANEL - LIST_ROW - 1), (0, SIDE - SLOTS)))
    shards = [panel[k * SHARD : (k + 1) * SHARD] for k in range(SHARDS - 1)]
    shards.append(jnp.concatenate([panel[(SHARDS - 1) * SHARD :], spare]))
    arrived = [lax.ppermute(shards[k], axis, SCATTER[k]) for k in range(SHARDS)]
    keeps = jnp.logical_or(index == HOLDER[0][0], index == HOLDER[2][0])
    return jnp.where(keeps, shards[0], sum(arrived[1:], arrived[0]))


def kernel(ints, *refs):
    a_refs, b_refs = refs[: 2 * RING], refs[2 * RING : 2 * RING + 6]
    out, a_all, b_all, a_sp, b_sp, result, lists, sems, list_sems, out_sems = refs[2 * RING + 6 :]
    col, row = ints[51], ints[52]
    x, z = lax.div(col, 2), lax.rem(col, 2)
    y, core = lax.rem(lax.div(row, 2), RING), lax.rem(row, 2)

    copies = []

    def place(ref, part, dest, origin):
        slot = ints[53 + origin]
        copy = pltpu.make_async_copy(
            ref.at[pl.ds(part * SHARD, SHARD), :],
            dest.at[pl.ds(pl.multiple_of(slot * SHARD, SHARD), SHARD), :],
            sems.at[len(copies)],
        )
        copy.start()
        copies.append(copy)

    for half in range(2):
        core_of = core if half == 0 else 1 - core
        way = 1 - 2 * core_of
        for ref, first, count in zip(b_refs[3 * half : 3 * half + 3], (-4, -1, 2), (3, 3, 2)):
            for part in range(count):
                origin_y = lax.rem(y + way * (first + part) + 2 * RING, RING)
                place(ref, part, b_all, origin_y * PAIR + core_of)
    for hop in range(RING):
        origin_x = lax.rem(x - (1 - 2 * core) * hop + RING, RING)
        place(a_refs[hop], 0, a_all, origin_x * PAIR + z)
        place(a_refs[RING + hop], 0, a_all, origin_x * PAIR + (1 - z))

    def split(source, which, dest, order):
        for copy in copies[which * 2 * RING : (which + 1) * 2 * RING]:
            copy.wait()
        asked = []
        for s in range(STEPS):
            copy = pltpu.make_async_copy(
                source.at[pl.ds(s * PANEL + LIST_ROW, 8), pl.ds(0, 128)],
                lists.at[which * STEPS + s],
                list_sems.at[which * STEPS + s],
            )
            copy.start()
            asked.append(copy)
        for s in range(STEPS):
            for t in range(SLOTS):
                value = source[pl.ds(s * PANEL + t * SIDE, SIDE), :]
                high = value.astype(jnp.bfloat16)
                low = (value - high.astype(jnp.float32)).astype(jnp.bfloat16)
                for part, kind in enumerate(order):
                    piece = low if kind else high
                    if which == 0:
                        dest[s * SLOTS + t, :, part * SIDE : (part + 1) * SIDE] = piece
                    else:
                        dest[s * SLOTS + t, part * SIDE : (part + 1) * SIDE, :] = piece
        return asked

    asked = split(b_all, 1, b_sp, (0, 1, 0)) + split(a_all, 0, a_sp, (0, 0, 1))
    for copy in asked:
        copy.wait()

    done = []
    for l in range(RESULTS):
        c_row, c_col = ints[2 * l], ints[2 * l + 1]
        total = None
        for s in range(STEPS):
            i, j = jnp.int32(0), jnp.int32(0)
            for t in range(SLOTS):
                i = jnp.where(lists[s, 0, t].astype(jnp.int32) == c_row, t, i)
                j = jnp.where(lists[STEPS + s, 0, t].astype(jnp.int32) == c_col, t, j)
            live = jnp.int32(0)
            for p in range(RESULTS):
                at = 12 + (s * RESULTS + p) * 2
                hit = (ints[at] == i) & (ints[at + 1] == j) & (p < ints[48 + s])
                live = jnp.where(hit, 1, live)
            product = jnp.dot(
                a_sp[s * SLOTS + i], b_sp[s * SLOTS + j], preferred_element_type=jnp.float32
            )
            product = product * live.astype(jnp.float32)
            total = product if total is None else total + product
        result[l] = total
        copy = pltpu.make_async_copy(result.at[l], out.at[l], out_sems.at[l])
        copy.start()
        done.append(copy)
    for copy in done:
        copy.wait()


def multiply(ints, a_blocks, b_blocks):
    anywhere = pl.BlockSpec(memory_space=pl.ANY)
    count = len(a_blocks) + len(b_blocks)
    rows = (STEPS * SHARDS + 1) * SHARD
    tiles = STEPS * SLOTS
    return pl.pallas_call(
        kernel,
        out_shape=jax.ShapeDtypeStruct((RESULTS, SIDE, SIDE), jnp.float32),
        in_specs=[pl.BlockSpec(memory_space=pltpu.SMEM)] + [anywhere] * count,
        out_specs=anywhere,
        scratch_shapes=[
            pltpu.VMEM((rows, SIDE), jnp.float32),
            pltpu.VMEM((rows, SIDE), jnp.float32),
            pltpu.VMEM((tiles, SIDE, 3 * SIDE), jnp.bfloat16),
            pltpu.VMEM((tiles, 3 * SIDE, SIDE), jnp.bfloat16),
            pltpu.VMEM((RESULTS, SIDE, SIDE), jnp.float32),
            pltpu.SMEM((2 * STEPS, 8, 128), jnp.float32),
            pltpu.SemaphoreType.DMA((4 * RING,)),
            pltpu.SemaphoreType.DMA((2 * STEPS,)),
            pltpu.SemaphoreType.DMA((RESULTS,)),
        ],
        compiler_params=pltpu.CompilerParams(vmem_limit_bytes=20 << 20),
    )(ints, *a_blocks, *b_blocks)


def program(a_tiles, b_tiles, a_rows, b_cols, c_shape, pairs, pair_count):
    col, row = lax.axis_index("col"), lax.axis_index("row")
    ints = jnp.concatenate(
        [
            c_shape.reshape(-1),
            pairs.reshape(-1),
            pair_count.reshape(-1),
            col.astype(jnp.int32)[None],
            row.astype(jnp.int32)[None],
            jnp.array(SLOT_OF, jnp.int32),
        ]
    )

    b_first = scatter(b_tiles[0, 0], b_cols[0, 0], "row", row)
    b_first, ints = lax.optimization_barrier((b_first, ints))
    a_own = scatter(a_tiles[0, 0], a_rows[0, 0], "col", col)
    b_own = b_first + sum(lax.ppermute(b_first, "row", to_plane(z)) for z in range(1, PLANES))

    near_a, far_a = [a_own], [lax.ppermute(a_own, "col", SWAP_Z)]
    for _ in range(1, RING):
        near_a.append(lax.ppermute(near_a[-1], ("row", "col"), ring_x()))
        far_a.append(lax.ppermute(far_a[-1], ("row", "col"), ring_x()))

    behind = lax.ppermute(b_own, "row", ring_y(1))
    ahead = lax.ppermute(b_own, "row", ring_y(-1))
    near = jnp.concatenate([behind, b_own, ahead])
    back = lax.ppermute(near, "row", ring_y(3))
    front = lax.ppermute(near[SHARD:], "row", ring_y(-2))
    mine = [back, near, front]
    other = [lax.ppermute(part, "row", SWAP_CORE) for part in mine]

    return multiply(ints, near_a + far_a, mine + other)[None, None]


def solution(mesh):
    return jax.shard_map(
        program,
        mesh=mesh,
        in_specs=(
            P("row", "col", None, None, None),
            P("row", "col", None, None, None),
            P("row", "col", None),
            P("row", "col", None),
            P("row", "col", None, None),
            P("row", "col", None, None, None),
            P("row", "col", None),
        ),
        out_specs=P("row", "col", None, None, None),
        check_vma=False,
    )
```

profile of v0, /device:TPU:1, one launch (start us, length us, event | category | flops | bytes accessed | tf_op | source)
XLA Modules:
  0.0 134.2 jit_solution(2867521764716945649)
XLA Ops:
  1.7 7.1 %collective-permute-start.9 = (f32[160,256]{1,0:T(8,128)S(1)}, f32[160,256]{1,0:T(8,128)S(1)}, u32[]{:S(2)}, u32[]{:S(2)}) collective-permute-start(f32[160,256]{1,0:T(8,128)S(1)} %select_maximum_fusion), channel_id=1, source_target_pairs={{0,10},{1,9},{2,8},{16,26},{17,25},{18,24},{32,42},{33,41},{34,40}... | collective-permute-start | bytes 491528 | tf_op jit(solution)/shard_map/ppermute | solution.py:65
  10.0 5.8 %collective-permute-start.6 = (f32[160,256]{1,0:T(8,128)S(1)}, f32[160,256]{1,0:T(8,128)S(1)}, u32[]{:S(2)}, u32[]{:S(2)}) collective-permute-start(f32[160,256]{1,0:T(8,128)S(1)} %get-tuple-element.9), channel_id=1, source_target_pairs={{0,1},{1,15},{2,3},{16,17},{17,31},{18,19},{32,33},{33,47},{34,35}... | collective-permute-start | bytes 491528 | tf_op jit(solution)/shard_map/ppermute | solution.py:65
  15.8 1.3 collective-permute-start.8
  17.1 1.3 collective-permute-start.7
  19.8 7.9 %collective-permute-start.4 = (f32[160,256]{1,0:T(8,128)S(1)}, f32[160,256]{1,0:T(8,128)S(1)}, u32[]{:S(2)}, u32[]{:S(2)}) collective-permute-start(f32[160,256]{1,0:T(8,128)S(1)} %select_maximum_fusion.1), channel_id=1, source_target_pairs={{0,160},{16,144},{32,128},{1,161},{17,145},{33,129},{2,162},{18,14... | collective-permute-start | bytes 491528 | tf_op jit(solution)/shard_map/ppermute | solution.py:65
  27.7 1.9 %collective-permute-start.1 = (f32[160,256]{1,0:T(8,128)S(1)}, f32[160,256]{1,0:T(8,128)S(1)}, u32[]{:S(2)}, u32[]{:S(2)}) collective-permute-start(f32[160,256]{1,0:T(8,128)S(1)} %get-tuple-element.13), channel_id=1, source_target_pairs={{0,16},{16,240},{32,48},{1,17},{17,241},{33,49},{2,18},{18,242},{3... | collective-permute-start | bytes 491528 | tf_op jit(solution)/shard_map/ppermute | solution.py:65
  29.6 1.3 collective-permute-start.3
  34.6 2.5 %collective-permute-start.17 = (f32[160,256]{1,0:T(8,128)S(1)}, f32[160,256]{1,0:T(8,128)S(1)}, u32[]{:S(2)}, u32[]{:S(2)}) collective-permute-start(f32[160,256]{1,0:T(8,128)S(1)} %add_select_fusion.refs_0_), channel_id=1, source_target_pairs={{0,1},{1,0},{2,3},{3,2},{4,5},{5,4},{6,7},{7,6},{8,9},{9,8},{10,11... | collective-permute-start | bytes 491528 | tf_op jit(solution)/shard_map/ppermute | solution.py:200
  37.6 5.5 %collective-permute-start.27 = (f32[160,256]{1,0:T(8,128)S(1)}, f32[160,256]{1,0:T(8,128)S(1)}, u32[]{:S(2)}, u32[]{:S(2)}) collective-permute-start(f32[160,256]{1,0:T(8,128)S(1)} %add_select_fusion.1), channel_id=1, source_target_pairs={{0,768},{16,784},{32,800},{48,816},{64,832},{80,848},{96,864},{112... | collective-permute-start | bytes 491528 | tf_op jit(solution)/shard_map/ppermute | solution.py:198
  45.7 5.0 %collective-permute-start.10 = (f32[160,256]{1,0:T(8,128)S(1)}, f32[160,256]{1,0:T(8,128)S(1)}, u32[]{:S(2)}, u32[]{:S(2)}) collective-permute-start(f32[160,256]{1,0:T(8,128)S(1)} %add_select_fusion.refs_0_), channel_id=1, source_target_pairs={{0,2},{1,3},{2,4},{3,5},{4,6},{5,7},{6,8},{7,9},{8,10},{9,11},{10,... | collective-permute-start | bytes 491528 | tf_op jit(solution)/shard_map/ppermute | solution.py:202
  50.8 1.9 %collective-permute-start.18 = (f32[160,256]{1,0:T(8,128)S(1)}, f32[160,256]{1,0:T(8,128)S(1)}, u32[]{:S(2)}, u32[]{:S(2)}) collective-permute-start(f32[160,256]{1,0:T(8,128)S(1)} %collective-permute-done.17.refs_8_), channel_id=1, source_target_pairs={{0,2},{1,3},{2,4},{3,5},{4,6},{5,7},{6,8},{7,9},{8,10},{9,11},{10,... | collective-permute-start | bytes 491528 | tf_op jit(solution)/shard_map/ppermute | solution.py:203
  53.2 3.3 %collective-permute-start.29 = (f32[160,256]{1,0:T(8,128)S(1)}, f32[160,256]{1,0:T(8,128)S(1)}, u32[]{:S(2)}, u32[]{:S(2)}) collective-permute-start(f32[160,256]{1,0:T(8,128)S(1)} %add_add_fusion), channel_id=1, source_target_pairs={{0,224},{16,48},{32,0},{48,80},{64,32},{80,112},{96,64},{112,144},... | collective-permute-start | bytes 491528 | tf_op jit(solution)/shard_map/ppermute | solution.py:206
  56.5 4.5 %collective-permute-start.28 = (f32[160,256]{1,0:T(8,128)S(1)}, f32[160,256]{1,0:T(8,128)S(1)}, u32[]{:S(2)}, u32[]{:S(2)}) collective-permute-start(f32[160,256]{1,0:T(8,128)S(1)} %add_add_fusion), channel_id=1, source_target_pairs={{0,32},{16,240},{32,64},{48,16},{64,96},{80,48},{96,128},{112,80},... | collective-permute-start | bytes 491528 | tf_op jit(solution)/shard_map/ppermute | solution.py:205
  61.0 4.6 %collective-permute-start.11 = (f32[160,256]{1,0:T(8,128)S(1)}, f32[160,256]{1,0:T(8,128)S(1)}, u32[]{:S(2)}, u32[]{:S(2)}) collective-permute-start(f32[160,256]{1,0:T(8,128)S(1)} %collective-permute-done.10.refs_1_), channel_id=1, source_target_pairs={{0,2},{1,3},{2,4},{3,5},{4,6},{5,7},{6,8},{7,9},{8,10},{9,11},{10,... | collective-permute-start | bytes 491528 | tf_op jit(solution)/shard_map/ppermute | solution.py:202
  65.7 2.8 %collective-permute-start.19 = (f32[160,256]{1,0:T(8,128)S(1)}, f32[160,256]{1,0:T(8,128)S(1)}, u32[]{:S(2)}, u32[]{:S(2)}) collective-permute-start(f32[160,256]{1,0:T(8,128)S(1)} %collective-permute-done.18.refs_9_), channel_id=1, source_target_pairs={{0,2},{1,3},{2,4},{3,5},{4,6},{5,7},{6,8},{7,9},{8,10},{9,11},{10,... | collective-permute-start | bytes 491528 | tf_op jit(solution)/shard_map/ppermute | solution.py:203
  68.6 4.7 %collective-permute-start.30 = (f32[480,256]{1,0:T(8,128)S(1)}, f32[480,256]{1,0:T(8,128)S(1)}, u32[]{:S(2)}, u32[]{:S(2)}) collective-permute-start(f32[480,256]{1,0:T(8,128)S(1)} %pad_maximum_fusion.refs_17_), channel_id=1, source_target_pairs={{0,96},{16,176},{32,128},{48,208},{64,160},{80,240},{96,192},{112,... | collective-permute-start | bytes 1474568 | tf_op jit(solution)/shard_map/ppermute | solution.py:208
  73.3 2.2 %collective-permute-start.12 = (f32[160,256]{1,0:T(8,128)S(1)}, f32[160,256]{1,0:T(8,128)S(1)}, u32[]{:S(2)}, u32[]{:S(2)}) collective-permute-start(f32[160,256]{1,0:T(8,128)S(1)} %collective-permute-done.11.refs_2_), channel_id=1, source_target_pairs={{0,2},{1,3},{2,4},{3,5},{4,6},{5,7},{6,8},{7,9},{8,10},{9,11},{10,... | collective-permute-start | bytes 491528 | tf_op jit(solution)/shard_map/ppermute | solution.py:202
  75.5 2.0 %collective-permute-start.20 = (f32[160,256]{1,0:T(8,128)S(1)}, f32[160,256]{1,0:T(8,128)S(1)}, u32[]{:S(2)}, u32[]{:S(2)}) collective-permute-start(f32[160,256]{1,0:T(8,128)S(1)} %collective-permute-done.19.refs_10_), channel_id=1, source_target_pairs={{0,2},{1,3},{2,4},{3,5},{4,6},{5,7},{6,8},{7,9},{8,10},{9,11},{10,... | collective-permute-start | bytes 491528 | tf_op jit(solution)/shard_map/ppermute | solution.py:203
  77.5 3.1 %collective-permute-start.31 = (f32[320,256]{1,0:T(8,128)S(1)}, f32[320,256]{1,0:T(8,128)S(1)}, u32[]{:S(2)}, u32[]{:S(2)}) collective-permute-start(f32[320,256]{1,0:T(8,128)S(1)} %pad_maximum_fusion.1), channel_id=1, source_target_pairs={{0,192},{16,80},{32,224},{48,112},{64,0},{80,144},{96,32},{112,176... | collective-permute-start | bytes 983048 | tf_op jit(solution)/shard_map/ppermute | solution.py:209
  80.7 2.5 %collective-permute-start.13 = (f32[160,256]{1,0:T(8,128)S(1)}, f32[160,256]{1,0:T(8,128)S(1)}, u32[]{:S(2)}, u32[]{:S(2)}) collective-permute-start(f32[160,256]{1,0:T(8,128)S(1)} %collective-permute-done.12.refs_3_), channel_id=1, source_target_pairs={{0,2},{1,3},{2,4},{3,5},{4,6},{5,7},{6,8},{7,9},{8,10},{9,11},{10,... | collective-permute-start | bytes 491528 | tf_op jit(solution)/shard_map/ppermute | solution.py:202
  83.2 5.0 %collective-permute-start.21 = (f32[160,256]{1,0:T(8,128)S(1)}, f32[160,256]{1,0:T(8,128)S(1)}, u32[]{:S(2)}, u32[]{:S(2)}) collective-permute-start(f32[160,256]{1,0:T(8,128)S(1)} %collective-permute-done.20.refs_11_), channel_id=1, source_target_pairs={{0,2},{1,3},{2,4},{3,5},{4,6},{5,7},{6,8},{7,9},{8,10},{9,11},{10,... | collective-permute-start | bytes 491528 | tf_op jit(solution)/shard_map/ppermute | solution.py:203
  88.2 2.2 %collective-permute-start.33 = (f32[480,256]{1,0:T(8,128)S(1)}, f32[480,256]{1,0:T(8,128)S(1)}, u32[]{:S(2)}, u32[]{:S(2)}) collective-permute-start(f32[480,256]{1,0:T(8,128)S(1)} %pad_maximum_fusion.refs_17_), channel_id=1, source_target_pairs={{0,16},{16,0},{32,48},{48,32},{64,80},{80,64},{96,112},{112,96},{1... | collective-permute-start | bytes 1474568 | tf_op jit(solution)/shard_map/ppermute | solution.py:211
  90.5 4.2 %collective-permute-start.14 = (f32[160,256]{1,0:T(8,128)S(1)}, f32[160,256]{1,0:T(8,128)S(1)}, u32[]{:S(2)}, u32[]{:S(2)}) collective-permute-start(f32[160,256]{1,0:T(8,128)S(1)} %collective-permute-done.13.refs_4_), channel_id=1, source_target_pairs={{0,2},{1,3},{2,4},{3,5},{4,6},{5,7},{6,8},{7,9},{8,10},{9,11},{10,... | collective-permute-start | bytes 491528 | tf_op jit(solution)/shard_map/ppermute | solution.py:202
  94.7 3.2 %collective-permute-start.22 = (f32[160,256]{1,0:T(8,128)S(1)}, f32[160,256]{1,0:T(8,128)S(1)}, u32[]{:S(2)}, u32[]{:S(2)}) collective-permute-start(f32[160,256]{1,0:T(8,128)S(1)} %collective-permute-done.21.refs_12_), channel_id=1, source_target_pairs={{0,2},{1,3},{2,4},{3,5},{4,6},{5,7},{6,8},{7,9},{8,10},{9,11},{10,... | collective-permute-start | bytes 491528 | tf_op jit(solution)/shard_map/ppermute | solution.py:203
  97.8 3.7 %collective-permute-start.32 = (f32[480,256]{1,0:T(8,128)S(1)}, f32[480,256]{1,0:T(8,128)S(1)}, u32[]{:S(2)}, u32[]{:S(2)}) collective-permute-start(f32[480,256]{1,0:T(8,128)S(1)} %collective-permute-done.30.refs_16_), channel_id=1, source_target_pairs={{0,16},{16,0},{32,48},{48,32},{64,80},{80,64},{96,112},{112,96},{1... | collective-permute-start | bytes 1474568 | tf_op jit(solution)/shard_map/ppermute | solution.py:211
  101.6 1.9 %collective-permute-start.34 = (f32[320,256]{1,0:T(8,128)S(1)}, f32[320,256]{1,0:T(8,128)S(1)}, u32[]{:S(2)}, u32[]{:S(2)}) collective-permute-start(f32[320,256]{1,0:T(8,128)S(1)} %collective-permute-done.31.refs_18_), channel_id=1, source_target_pairs={{0,16},{16,0},{32,48},{48,32},{64,80},{80,64},{96,112},{112,96},{1... | collective-permute-start | bytes 983048 | tf_op jit(solution)/shard_map/ppermute | solution.py:211
  103.5 4.6 %collective-permute-start.15 = (f32[160,256]{1,0:T(8,128)S(1)}, f32[160,256]{1,0:T(8,128)S(1)}, u32[]{:S(2)}, u32[]{:S(2)}) collective-permute-start(f32[160,256]{1,0:T(8,128)S(1)} %collective-permute-done.14.refs_5_), channel_id=1, source_target_pairs={{0,2},{1,3},{2,4},{3,5},{4,6},{5,7},{6,8},{7,9},{8,10},{9,11},{10,... | collective-permute-start | bytes 491528 | tf_op jit(solution)/shard_map/ppermute | solution.py:202
  108.1 1.9 %collective-permute-start.23 = (f32[160,256]{1,0:T(8,128)S(1)}, f32[160,256]{1,0:T(8,128)S(1)}, u32[]{:S(2)}, u32[]{:S(2)}) collective-permute-start(f32[160,256]{1,0:T(8,128)S(1)} %collective-permute-done.22.refs_13_), channel_id=1, source_target_pairs={{0,2},{1,3},{2,4},{3,5},{4,6},{5,7},{6,8},{7,9},{8,10},{9,11},{10,... | collective-permute-start | bytes 491528 | tf_op jit(solution)/shard_map/ppermute | solution.py:203
  110.3 5.0 %collective-permute-start.16 = (f32[160,256]{1,0:T(8,128)S(1)}, f32[160,256]{1,0:T(8,128)S(1)}, u32[]{:S(2)}, u32[]{:S(2)}) collective-permute-start(f32[160,256]{1,0:T(8,128)S(1)} %collective-permute-done.15.refs_6_), channel_id=1, source_target_pairs={{0,2},{1,3},{2,4},{3,5},{4,6},{5,7},{6,8},{7,9},{8,10},{9,11},{10,... | collective-permute-start | bytes 491528 | tf_op jit(solution)/shard_map/ppermute | solution.py:202
  115.3 1.9 %collective-permute-start.24 = (f32[160,256]{1,0:T(8,128)S(1)}, f32[160,256]{1,0:T(8,128)S(1)}, u32[]{:S(2)}, u32[]{:S(2)}) collective-permute-start(f32[160,256]{1,0:T(8,128)S(1)} %collective-permute-done.23.refs_14_), channel_id=1, source_target_pairs={{0,2},{1,3},{2,4},{3,5},{4,6},{5,7},{6,8},{7,9},{8,10},{9,11},{10,... | collective-permute-start | bytes 491528 | tf_op jit(solution)/shard_map/ppermute | solution.py:203
  117.6 4.1 %collective-permute-done.24.refs_15_ = f32[160,256]{1,0:T(8,128)S(1)} collective-permute-done((f32[160,256]{1,0:T(8,128)S(1)}, f32[160,256]{1,0:T(8,128)S(1)}, u32[]{:S(2)}, u32[]{:S(2)}) %collective-permute-start.24) | collective-permute-done | bytes 163872 | tf_op jit(solution)/shard_map/ppermute | solution.py:203
  121.7 12.5 %shard_map.82 = f32[6,256,256]{2,1,0:T(8,128)} custom-call(s32[69]{0:T(128)S(1)} %concatenate.16.ints, f32[160,256]{1,0:T(8,128)S(1)} %add_select_fusion.refs_0_, f32[160,256]{1,0:T(8,128)S(1)} %collective-permute-done.10.refs_1_, f32[160,256]{1,0:T(8,128)S(1)} %collective-permute-done.11.refs_2_, f32[160,256]{1,0:T(8,128)S(1)} %collective-permute-done.12.refs_3_, ...), custom_call_target="tpu_custom_call" | custom-call | tf_op jit(solution)/shard_map/pallas_call | solution.py:162
  (69 shorter events, 11.9 us)
Async XLA Ops:
  1.7 18.0 %collective-permute-start.9 = (f32[160,256]{1,0:T(8,128)S(1)}, f32[160,256]{1,0:T(8,128)S(1)}, u32[]{:S(2)}, u32[]{:S(2)}) collective-permute-start(f32[160,256]{1,0:T(8,128)S(1)} %select_maximum_fusion), channel_id=1, source_target_pairs={{0,10},{1,9},{2,8},{16,26},{17,25},{18,24},{32,42},{33,41},{34,40}... | collective-permute-start | bytes 491528 | tf_op jit(solution)/shard_map/ppermute | solution.py:65
  10.0 17.7 %collective-permute-start.6 = (f32[160,256]{1,0:T(8,128)S(1)}, f32[160,256]{1,0:T(8,128)S(1)}, u32[]{:S(2)}, u32[]{:S(2)}) collective-permute-start(f32[160,256]{1,0:T(8,128)S(1)} %get-tuple-element.9), channel_id=1, source_target_pairs={{0,1},{1,15},{2,3},{16,17},{17,31},{18,19},{32,33},{33,47},{34,35}... | collective-permute-start | bytes 491528 | tf_op jit(solution)/shard_map/ppermute | solution.py:65
  15.8 13.8 %collective-permute-start.8 = (f32[160,256]{1,0:T(8,128)S(1)}, f32[160,256]{1,0:T(8,128)S(1)}, u32[]{:S(2)}, u32[]{:S(2)}) collective-permute-start(f32[160,256]{1,0:T(8,128)S(1)} %get-tuple-element.10), channel_id=1, source_target_pairs={{0,12},{1,7},{2,6},{16,28},{17,23},{18,22},{32,44},{33,39},{34,38}... | collective-permute-start | bytes 491528 | tf_op jit(solution)/shard_map/ppermute | solution.py:65
  17.1 13.8 %collective-permute-start.7 = (f32[160,256]{1,0:T(8,128)S(1)}, f32[160,256]{1,0:T(8,128)S(1)}, u32[]{:S(2)}, u32[]{:S(2)}) collective-permute-start(f32[160,256]{1,0:T(8,128)S(1)} %get-tuple-element.11), channel_id=1, source_target_pairs={{0,14},{1,5},{2,4},{16,30},{17,21},{18,20},{32,46},{33,37},{34,36}... | collective-permute-start | bytes 491528 | tf_op jit(solution)/shard_map/ppermute | solution.py:65
  18.4 13.8 %collective-permute-start.5 = (f32[160,256]{1,0:T(8,128)S(1)}, f32[160,256]{1,0:T(8,128)S(1)}, u32[]{:S(2)}, u32[]{:S(2)}) collective-permute-start(f32[160,256]{1,0:T(8,128)S(1)} %get-tuple-element.12), channel_id=1, source_target_pairs={{1,13},{17,29},{33,45},{49,61},{65,77},{81,93},{97,109},{113,125},... | collective-permute-start | bytes 491528 | tf_op jit(solution)/shard_map/ppermute | solution.py:65
  19.8 14.8 %collective-permute-start.4 = (f32[160,256]{1,0:T(8,128)S(1)}, f32[160,256]{1,0:T(8,128)S(1)}, u32[]{:S(2)}, u32[]{:S(2)}) collective-permute-start(f32[160,256]{1,0:T(8,128)S(1)} %select_maximum_fusion.1), channel_id=1, source_target_pairs={{0,160},{16,144},{32,128},{1,161},{17,145},{33,129},{2,162},{18,14... | collective-permute-start | bytes 491528 | tf_op jit(solution)/shard_map/ppermute | solution.py:65
  27.7 9.4 %collective-permute-start.1 = (f32[160,256]{1,0:T(8,128)S(1)}, f32[160,256]{1,0:T(8,128)S(1)}, u32[]{:S(2)}, u32[]{:S(2)}) collective-permute-start(f32[160,256]{1,0:T(8,128)S(1)} %get-tuple-element.13), channel_id=1, source_target_pairs={{0,16},{16,240},{32,48},{1,17},{17,241},{33,49},{2,18},{18,242},{3... | collective-permute-start | bytes 491528 | tf_op jit(solution)/shard_map/ppermute | solution.py:65
  29.6 7.5 %collective-permute-start.3 = (f32[160,256]{1,0:T(8,128)S(1)}, f32[160,256]{1,0:T(8,128)S(1)}, u32[]{:S(2)}, u32[]{:S(2)}) collective-permute-start(f32[160,256]{1,0:T(8,128)S(1)} %get-tuple-element.14), channel_id=1, source_target_pairs={{0,192},{16,112},{32,96},{1,193},{17,113},{33,97},{2,194},{18,114}... | collective-permute-start | bytes 491528 | tf_op jit(solution)/shard_map/ppermute | solution.py:65
  34.6 16.2 %collective-permute-start.17 = (f32[160,256]{1,0:T(8,128)S(1)}, f32[160,256]{1,0:T(8,128)S(1)}, u32[]{:S(2)}, u32[]{:S(2)}) collective-permute-start(f32[160,256]{1,0:T(8,128)S(1)} %add_select_fusion.refs_0_), channel_id=1, source_target_pairs={{0,1},{1,0},{2,3},{3,2},{4,5},{5,4},{6,7},{7,6},{8,9},{9,8},{10,11... | collective-permute-start | bytes 491528 | tf_op jit(solution)/shard_map/ppermute | solution.py:200
  37.6 15.5 %collective-permute-start.27 = (f32[160,256]{1,0:T(8,128)S(1)}, f32[160,256]{1,0:T(8,128)S(1)}, u32[]{:S(2)}, u32[]{:S(2)}) collective-permute-start(f32[160,256]{1,0:T(8,128)S(1)} %add_select_fusion.1), channel_id=1, source_target_pairs={{0,768},{16,784},{32,800},{48,816},{64,832},{80,848},{96,864},{112... | collective-permute-start | bytes 491528 | tf_op jit(solution)/shard_map/ppermute | solution.py:198
  43.1 10.0 %collective-permute-start.26 = (f32[160,256]{1,0:T(8,128)S(1)}, f32[160,256]{1,0:T(8,128)S(1)}, u32[]{:S(2)}, u32[]{:S(2)}) collective-permute-start(f32[160,256]{1,0:T(8,128)S(1)} %add_select_fusion.1), channel_id=1, source_target_pairs={{0,512},{16,528},{32,544},{48,560},{64,576},{80,592},{96,608},{112... | collective-permute-start | bytes 491528 | tf_op jit(solution)/shard_map/ppermute | solution.py:198
  44.4 8.7 %collective-permute-start.25 = (f32[160,256]{1,0:T(8,128)S(1)}, f32[160,256]{1,0:T(8,128)S(1)}, u32[]{:S(2)}, u32[]{:S(2)}) collective-permute-start(f32[160,256]{1,0:T(8,128)S(1)} %add_select_fusion.1), channel_id=1, source_target_pairs={{0,256},{16,272},{32,288},{48,304},{64,320},{80,336},{96,352},{112... | collective-permute-start | bytes 491528 | tf_op jit(solution)/shard_map/ppermute | solution.py:198
  45.7 15.3 %collective-permute-start.10 = (f32[160,256]{1,0:T(8,128)S(1)}, f32[160,256]{1,0:T(8,128)S(1)}, u32[]{:S(2)}, u32[]{:S(2)}) collective-permute-start(f32[160,256]{1,0:T(8,128)S(1)} %add_select_fusion.refs_0_), channel_id=1, source_target_pairs={{0,2},{1,3},{2,4},{3,5},{4,6},{5,7},{6,8},{7,9},{8,10},{9,11},{10,... | collective-permute-start | bytes 491528 | tf_op jit(solution)/shard_map/ppermute | solution.py:202
  50.8 14.9 %collective-permute-start.18 = (f32[160,256]{1,0:T(8,128)S(1)}, f32[160,256]{1,0:T(8,128)S(1)}, u32[]{:S(2)}, u32[]{:S(2)}) collective-permute-start(f32[160,256]{1,0:T(8,128)S(1)} %collective-permute-done.17.refs_8_), channel_id=1, source_target_pairs={{0,2},{1,3},{2,4},{3,5},{4,6},{5,7},{6,8},{7,9},{8,10},{9,11},{10,... | collective-permute-start | bytes 491528 | tf_op jit(solution)/shard_map/ppermute | solution.py:203
  53.2 15.3 %collective-permute-start.29 = (f32[160,256]{1,0:T(8,128)S(1)}, f32[160,256]{1,0:T(8,128)S(1)}, u32[]{:S(2)}, u32[]{:S(2)}) collective-permute-start(f32[160,256]{1,0:T(8,128)S(1)} %add_add_fusion), channel_id=1, source_target_pairs={{0,224},{16,48},{32,0},{48,80},{64,32},{80,112},{96,64},{112,144},... | collective-permute-start | bytes 491528 | tf_op jit(solution)/shard_map/ppermute | solution.py:206
  56.5 12.0 %collective-permute-start.28 = (f32[160,256]{1,0:T(8,128)S(1)}, f32[160,256]{1,0:T(8,128)S(1)}, u32[]{:S(2)}, u32[]{:S(2)}) collective-permute-start(f32[160,256]{1,0:T(8,128)S(1)} %add_add_fusion), channel_id=1, source_target_pairs={{0,32},{16,240},{32,64},{48,16},{64,96},{80,48},{96,128},{112,80},... | collective-permute-start | bytes 491528 | tf_op jit(solution)/shard_map/ppermute | solution.py:205
  61.0 12.3 %collective-permute-start.11 = (f32[160,256]{1,0:T(8,128)S(1)}, f32[160,256]{1,0:T(8,128)S(1)}, u32[]{:S(2)}, u32[]{:S(2)}) collective-permute-start(f32[160,256]{1,0:T(8,128)S(1)} %collective-permute-done.10.refs_1_), channel_id=1, source_target_pairs={{0,2},{1,3},{2,4},{3,5},{4,6},{5,7},{6,8},{7,9},{8,10},{9,11},{10,... | collective-permute-start | bytes 491528 | tf_op jit(solution)/shard_map/ppermute | solution.py:202
  65.7 9.8 %collective-permute-start.19 = (f32[160,256]{1,0:T(8,128)S(1)}, f32[160,256]{1,0:T(8,128)S(1)}, u32[]{:S(2)}, u32[]{:S(2)}) collective-permute-start(f32[160,256]{1,0:T(8,128)S(1)} %collective-permute-done.18.refs_9_), channel_id=1, source_target_pairs={{0,2},{1,3},{2,4},{3,5},{4,6},{5,7},{6,8},{7,9},{8,10},{9,11},{10,... | collective-permute-start | bytes 491528 | tf_op jit(solution)/shard_map/ppermute | solution.py:203
  68.6 29.3 %collective-permute-start.30 = (f32[480,256]{1,0:T(8,128)S(1)}, f32[480,256]{1,0:T(8,128)S(1)}, u32[]{:S(2)}, u32[]{:S(2)}) collective-permute-start(f32[480,256]{1,0:T(8,128)S(1)} %pad_maximum_fusion.refs_17_), channel_id=1, source_target_pairs={{0,96},{16,176},{32,128},{48,208},{64,160},{80,240},{96,192},{112,... | collective-permute-start | bytes 1474568 | tf_op jit(solution)/shard_map/ppermute | solution.py:208
  73.3 7.4 %collective-permute-start.12 = (f32[160,256]{1,0:T(8,128)S(1)}, f32[160,256]{1,0:T(8,128)S(1)}, u32[]{:S(2)}, u32[]{:S(2)}) collective-permute-start(f32[160,256]{1,0:T(8,128)S(1)} %collective-permute-done.11.refs_2_), channel_id=1, source_target_pairs={{0,2},{1,3},{2,4},{3,5},{4,6},{5,7},{6,8},{7,9},{8,10},{9,11},{10,... | collective-permute-start | bytes 491528 | tf_op jit(solution)/shard_map/ppermute | solution.py:202
  75.5 7.7 %collective-permute-start.20 = (f32[160,256]{1,0:T(8,128)S(1)}, f32[160,256]{1,0:T(8,128)S(1)}, u32[]{:S(2)}, u32[]{:S(2)}) collective-permute-start(f32[160,256]{1,0:T(8,128)S(1)} %collective-permute-done.19.refs_10_), channel_id=1, source_target_pairs={{0,2},{1,3},{2,4},{3,5},{4,6},{5,7},{6,8},{7,9},{8,10},{9,11},{10,... | collective-permute-start | bytes 491528 | tf_op jit(solution)/shard_map/ppermute | solution.py:203
  77.5 24.0 %collective-permute-start.31 = (f32[320,256]{1,0:T(8,128)S(1)}, f32[320,256]{1,0:T(8,128)S(1)}, u32[]{:S(2)}, u32[]{:S(2)}) collective-permute-start(f32[320,256]{1,0:T(8,128)S(1)} %pad_maximum_fusion.1), channel_id=1, source_target_pairs={{0,192},{16,80},{32,224},{48,112},{64,0},{80,144},{96,32},{112,176... | collective-permute-start | bytes 983048 | tf_op jit(solution)/shard_map/ppermute | solution.py:209
  80.7 9.8 %collective-permute-start.13 = (f32[160,256]{1,0:T(8,128)S(1)}, f32[160,256]{1,0:T(8,128)S(1)}, u32[]{:S(2)}, u32[]{:S(2)}) collective-permute-start(f32[160,256]{1,0:T(8,128)S(1)} %collective-permute-done.12.refs_3_), channel_id=1, source_target_pairs={{0,2},{1,3},{2,4},{3,5},{4,6},{5,7},{6,8},{7,9},{8,10},{9,11},{10,... | collective-permute-start | bytes 491528 | tf_op jit(solution)/shard_map/ppermute | solution.py:202
  83.2 11.5 %collective-permute-start.21 = (f32[160,256]{1,0:T(8,128)S(1)}, f32[160,256]{1,0:T(8,128)S(1)}, u32[]{:S(2)}, u32[]{:S(2)}) collective-permute-start(f32[160,256]{1,0:T(8,128)S(1)} %collective-permute-done.20.refs_11_), channel_id=1, source_target_pairs={{0,2},{1,3},{2,4},{3,5},{4,6},{5,7},{6,8},{7,9},{8,10},{9,11},{10,... | collective-permute-start | bytes 491528 | tf_op jit(solution)/shard_map/ppermute | solution.py:203
  88.2 29.1 %collective-permute-start.33 = (f32[480,256]{1,0:T(8,128)S(1)}, f32[480,256]{1,0:T(8,128)S(1)}, u32[]{:S(2)}, u32[]{:S(2)}) collective-permute-start(f32[480,256]{1,0:T(8,128)S(1)} %pad_maximum_fusion.refs_17_), channel_id=1, source_target_pairs={{0,16},{16,0},{32,48},{48,32},{64,80},{80,64},{96,112},{112,96},{1... | collective-permute-start | bytes 1474568 | tf_op jit(solution)/shard_map/ppermute | solution.py:211
  90.5 13.0 %collective-permute-start.14 = (f32[160,256]{1,0:T(8,128)S(1)}, f32[160,256]{1,0:T(8,128)S(1)}, u32[]{:S(2)}, u32[]{:S(2)}) collective-permute-start(f32[160,256]{1,0:T(8,128)S(1)} %collective-permute-done.13.refs_4_), channel_id=1, source_target_pairs={{0,2},{1,3},{2,4},{3,5},{4,6},{5,7},{6,8},{7,9},{8,10},{9,11},{10,... | collective-permute-start | bytes 491528 | tf_op jit(solution)/shard_map/ppermute | solution.py:202
  94.7 13.4 %collective-permute-start.22 = (f32[160,256]{1,0:T(8,128)S(1)}, f32[160,256]{1,0:T(8,128)S(1)}, u32[]{:S(2)}, u32[]{:S(2)}) collective-permute-start(f32[160,256]{1,0:T(8,128)S(1)} %collective-permute-done.21.refs_12_), channel_id=1, source_target_pairs={{0,2},{1,3},{2,4},{3,5},{4,6},{5,7},{6,8},{7,9},{8,10},{9,11},{10,... | collective-permute-start | bytes 491528 | tf_op jit(solution)/shard_map/ppermute | solution.py:203
  97.8 23.9 %collective-permute-start.32 = (f32[480,256]{1,0:T(8,128)S(1)}, f32[480,256]{1,0:T(8,128)S(1)}, u32[]{:S(2)}, u32[]{:S(2)}) collective-permute-start(f32[480,256]{1,0:T(8,128)S(1)} %collective-permute-done.30.refs_16_), channel_id=1, source_target_pairs={{0,16},{16,0},{32,48},{48,32},{64,80},{80,64},{96,112},{112,96},{1... | collective-permute-start | bytes 1474568 | tf_op jit(solution)/shard_map/ppermute | solution.py:211
  101.6 15.7 %collective-permute-start.34 = (f32[320,256]{1,0:T(8,128)S(1)}, f32[320,256]{1,0:T(8,128)S(1)}, u32[]{:S(2)}, u32[]{:S(2)}) collective-permute-start(f32[320,256]{1,0:T(8,128)S(1)} %collective-permute-done.31.refs_18_), channel_id=1, source_target_pairs={{0,16},{16,0},{32,48},{48,32},{64,80},{80,64},{96,112},{112,96},{1... | collective-permute-start | bytes 983048 | tf_op jit(solution)/shard_map/ppermute | solution.py:211
  103.5 6.8 %collective-permute-start.15 = (f32[160,256]{1,0:T(8,128)S(1)}, f32[160,256]{1,0:T(8,128)S(1)}, u32[]{:S(2)}, u32[]{:S(2)}) collective-permute-start(f32[160,256]{1,0:T(8,128)S(1)} %collective-permute-done.14.refs_5_), channel_id=1, source_target_pairs={{0,2},{1,3},{2,4},{3,5},{4,6},{5,7},{6,8},{7,9},{8,10},{9,11},{10,... | collective-permute-start | bytes 491528 | tf_op jit(solution)/shard_map/ppermute | solution.py:202
  108.1 7.3 %collective-permute-start.23 = (f32[160,256]{1,0:T(8,128)S(1)}, f32[160,256]{1,0:T(8,128)S(1)}, u32[]{:S(2)}, u32[]{:S(2)}) collective-permute-start(f32[160,256]{1,0:T(8,128)S(1)} %collective-permute-done.22.refs_13_), channel_id=1, source_target_pairs={{0,2},{1,3},{2,4},{3,5},{4,6},{5,7},{6,8},{7,9},{8,10},{9,11},{10,... | collective-permute-start | bytes 491528 | tf_op jit(solution)/shard_map/ppermute | solution.py:203
  110.3 7.3 %collective-permute-start.16 = (f32[160,256]{1,0:T(8,128)S(1)}, f32[160,256]{1,0:T(8,128)S(1)}, u32[]{:S(2)}, u32[]{:S(2)}) collective-permute-start(f32[160,256]{1,0:T(8,128)S(1)} %collective-permute-done.15.refs_6_), channel_id=1, source_target_pairs={{0,2},{1,3},{2,4},{3,5},{4,6},{5,7},{6,8},{7,9},{8,10},{9,11},{10,... | collective-permute-start | bytes 491528 | tf_op jit(solution)/shard_map/ppermute | solution.py:202
  (9 other events, 126.5 us)
where the time goes:
time: 135 us; the launch traced here: 134 us
  starting transfers between devices  111 us (82%)
  Pallas kernels  12.5 us (9%)
  waiting for transfers between devices  5.6 us (4%)
  local copies, waits for them, and re-layouts  2.67 us (2%)
  other arithmetic  1.91 us (1%)
    ppermute x10, starting transfers between devices, scatter(): arrived = [lax.ppermute(shards[k], axis, SCATTER[k]) for k in range(SHARDS)]  29.9 us
    ppermute x7, starting transfers between devices, program(): near_a.append(lax.ppermute(near_a[-1], ('row', 'col'), ring_x()))  28.1 us
    ppermute x7, starting transfers between devices, program(): far_a.append(lax.ppermute(far_a[-1], ('row', 'col'), ring_x()))  18.7 us
    pallas_call x1, Pallas kernels, multiply(): pl.pallas_call(kernel, out_shape=jax.ShapeDtypeStruct((RESULTS, SIDE, SID...  12.5 us
    ppermute x3, starting transfers between devices, program(): lax.ppermute(b_first, 'row', to_plane(z))  8.09 us
    ppermute x3, starting transfers between devices, program(): other = [lax.ppermute(part, 'row', SWAP_CORE) for part in mine]  7.87 us
    ppermute x1, starting transfers between devices, program(): back = lax.ppermute(near, 'row', ring_y(3))  4.7 us
    ppermute x1, starting transfers between devices, program(): behind = lax.ppermute(b_own, 'row', ring_y(1))  4.5 us
  transfers between devices with their start and end apart: 35, of which 5 were waited for; matrix products, arithmetic and copies ran while one was open for 2% of the time, Pallas kernels for 0%

commit v1 on v0

v1 whole, which is shorter than its diff:
```python
import jax
import jax.numpy as jnp
from jax import lax
from jax.experimental import pallas as pl
from jax.experimental.pallas import tpu as pltpu
from jax.sharding import PartitionSpec as P


STEPS, SLOTS, SIDE, RESULTS = 3, 3, 256, 6
RING, PAIR, PLANES = 8, 2, 4
SHARD = 160
SHARDS = 5
PANEL = SHARD * SHARDS
LIST_ROW = SLOTS * SIDE

HOLDERS = (
    ((0, 0), (0, 1), (7, 0), (6, 0), (5, 0)),
    ((6, 1), (7, 1), (2, 1), (3, 1), (4, 1)),
    ((1, 0), (1, 1), (2, 0), (3, 0), (4, 0)),
)
HOLDER = tuple(tuple(ring * PAIR + pair for ring, pair in panel) for panel in HOLDERS)
SLOT_OF = [STEPS * SHARDS] * (RING * PAIR)
for _s in range(STEPS):
    for _k in range(SHARDS):
        SLOT_OF[HOLDER[_s][_k]] = _s * SHARDS + _k

SCATTER = [
    [(s, HOLDER[s][k]) for s in range(STEPS) if HOLDER[s][k] != s] for k in range(SHARDS)
]


def ring_x(step):
    columns = RING * PAIR
    pairs = []
    for r in range(PLANES * RING * PAIR):
        for c in range(columns):
            to = (c + PAIR * (step if r % PAIR == 0 else -step)) % columns
            pairs.append((r * columns + c, r * columns + to))
    return pairs


def ring_y(step):
    pairs = []
    for z in range(PLANES):
        for y in range(RING):
            for core in range(PAIR):
                to = (y + (step if core == 0 else -step)) % RING
                pairs.append(((z * RING + y) * PAIR + core, (z * RING + to) * PAIR + core))
    return pairs


SWAP_Z = [(c, c ^ 1) for c in range(RING * PAIR)]
SWAP_CORE = [(r, r ^ 1) for r in range(PLANES * RING * PAIR)]


def to_plane(z):
    return [(r, z * RING * PAIR + r) for r in range(RING * PAIR)]


def scatter(tiles, listed, axis, index):
    panel = tiles.reshape(SLOTS * SIDE, SIDE)
    spare = jnp.pad(listed.astype(jnp.float32)[None, :], ((0, PANEL - LIST_ROW - 1), (0, SIDE - SLOTS)))
    shards = [panel[k * SHARD : (k + 1) * SHARD] for k in range(SHARDS - 1)]
    shards.append(jnp.concatenate([panel[(SHARDS - 1) * SHARD :], spare]))
    arrived = [lax.ppermute(shards[k], axis, SCATTER[k]) for k in range(SHARDS)]
    keeps = jnp.logical_or(index == HOLDER[0][0], index == HOLDER[2][0])
    return jnp.where(keeps, shards[0], sum(arrived[1:], arrived[0]))


def kernel(ints, *refs):
    a_refs, b_refs = refs[:RING], refs[RING : RING + 6]
    out, a_sp, b_sp, lists, list_sems = refs[RING + 6 :]
    col, row = ints[51], ints[52]
    x, z = lax.div(col, 2), lax.rem(col, 2)
    y, core = lax.rem(lax.div(row, 2), RING), lax.rem(row, 2)

    places = []
    for half in range(2):
        core_of = core if half == 0 else 1 - core
        way = 1 - 2 * core_of
        for ref, first, count in zip(b_refs[3 * half : 3 * half + 3], (-4, -1, 2), (3, 3, 2)):
            for part in range(count):
                origin_y = lax.rem(y + way * (first + part) + 2 * RING, RING)
                places.append((ref, part, b_sp, origin_y * PAIR + core_of))
    way = 1 - 2 * core
    for ref, shift in zip(a_refs, (0, -1, 1, -2, 2, -3, 3, -4)):
        origin_x = lax.rem(x + way * shift + RING, RING)
        places.append((ref, 0, a_sp, origin_x * PAIR + z))
        places.append((ref, 1, a_sp, origin_x * PAIR + (1 - z)))

    asked = []
    for n, (ref, part, dest, origin) in enumerate(places):
        slot = ints[53 + origin] + (0 if dest is a_sp else 2 * RING)
        copy = pltpu.make_async_copy(
            ref.at[pl.ds(part * SHARD + LIST_ROW % SHARD, 8), pl.ds(0, 128)],
            lists.at[slot],
            list_sems.at[n],
        )
        copy.start()
        asked.append(copy)
    for ref, part, dest, origin in places:
        slot = ints[53 + origin]
        value = ref[part * SHARD : (part + 1) * SHARD, :]
        high = value.astype(jnp.bfloat16)
        low = (value - high.astype(jnp.float32)).astype(jnp.bfloat16)
        at = pl.ds(pl.multiple_of(slot * SHARD, SHARD), SHARD)
        dest[at, :SIDE] = high
        dest[at, SIDE:] = low
    for copy in asked:
        copy.wait()

    for l in range(RESULTS):
        c_row, c_col = ints[2 * l], ints[2 * l + 1]
        total = None
        for s in range(STEPS):
            last = s * SHARDS + SHARDS - 1
            i, j = jnp.int32(0), jnp.int32(0)
            for t in range(SLOTS):
                i = jnp.where(lists[last, 0, t].astype(jnp.int32) == c_row, t, i)
                j = jnp.where(lists[2 * RING + last, 0, t].astype(jnp.int32) == c_col, t, j)
            live = jnp.int32(0)
            for p in range(RESULTS):
                at = 12 + (s * RESULTS + p) * 2
                hit = (ints[at] == i) & (ints[at + 1] == j) & (p < ints[48 + s])
                live = jnp.where(hit, 1, live)
            ia = pl.ds(pl.multiple_of(s * PANEL + i * SIDE, 32), SIDE)
            jb = pl.ds(pl.multiple_of(s * PANEL + j * SIDE, 32), SIDE)
            product = (
                jnp.dot(a_sp[ia, :SIDE], b_sp[jb, :SIDE], preferred_element_type=jnp.float32)
                + jnp.dot(a_sp[ia, :SIDE], b_sp[jb, SIDE:], preferred_element_type=jnp.float32)
                + jnp.dot(a_sp[ia, SIDE:], b_sp[jb, :SIDE], preferred_element_type=jnp.float32)
            )
            product = product * live.astype(jnp.float32)
            total = product if total is None else total + product
        out[l] = total


def multiply(ints, a_blocks, b_blocks):
    local = pl.BlockSpec(memory_space=pltpu.VMEM)
    count = len(a_blocks) + len(b_blocks)
    rows = (STEPS * SHARDS + 1) * SHARD
    return pl.pallas_call(
        kernel,
        out_shape=jax.ShapeDtypeStruct((RESULTS, SIDE, SIDE), jnp.float32),
        in_specs=[pl.BlockSpec(memory_space=pltpu.SMEM)] + [local] * count,
        out_specs=local,
        scratch_shapes=[
            pltpu.VMEM((rows, 2 * SIDE), jnp.bfloat16),
            pltpu.VMEM((rows, 2 * SIDE), jnp.bfloat16),
            pltpu.SMEM((4 * RING, 8, 128), jnp.float32),
            pltpu.SemaphoreType.DMA((4 * RING,)),
        ],
        compiler_params=pltpu.CompilerParams(vmem_limit_bytes=24 << 20),
    )(ints, *a_blocks, *b_blocks)


def program(a_tiles, b_tiles, a_rows, b_cols, c_shape, pairs, pair_count):
    col, row = lax.axis_index("col"), lax.axis_index("row")
    ints = jnp.concatenate(
        [
            c_shape.reshape(-1),
            pairs.reshape(-1),
            pair_count.reshape(-1),
            col.astype(jnp.int32)[None],
            row.astype(jnp.int32)[None],
            jnp.array(SLOT_OF, jnp.int32),
        ]
    )

    a_own = scatter(a_tiles[0, 0], a_rows[0, 0], "col", col)
    b_first = scatter(b_tiles[0, 0], b_cols[0, 0], "row", row)
    b_first, ints = lax.optimization_barrier((b_first, ints))
    b_own = b_first + sum(lax.ppermute(b_first, "row", to_plane(z)) for z in range(1, PLANES))

    block = jnp.concatenate([a_own, lax.ppermute(a_own, "col", SWAP_Z)])
    a_blocks, after, before = [block], block, block
    for _ in range(1, RING // 2):
        after = lax.ppermute(after, ("row", "col"), ring_x(1))
        before = lax.ppermute(before, ("row", "col"), ring_x(-1))
        a_blocks += [after, before]
    a_blocks.append(lax.ppermute(after, ("row", "col"), ring_x(1)))

    behind = lax.ppermute(b_own, "row", ring_y(1))
    ahead = lax.ppermute(b_own, "row", ring_y(-1))
    near = jnp.concatenate([behind, b_own, ahead])
    back = lax.ppermute(near, "row", ring_y(3))
    front = lax.ppermute(near[SHARD:], "row", ring_y(-2))
    mine = [back, near, front]
    other = [lax.ppermute(part, "row", SWAP_CORE) for part in mine]

    return multiply(ints, a_blocks, mine + other)[None, None]


def solution(mesh):
    return jax.shard_map(
        program,
        mesh=mesh,
        in_specs=(
            P("row", "col", None, None, None),
            P("row", "col", None, None, None),
            P("row", "col", None),
            P("row", "col", None),
            P("row", "col", None, None),
            P("row", "col", None, None, None),
            P("row", "col", None),
        ),
        out_specs=P("row", "col", None, None, None),
        check_vma=False,
    )
```

time: 135 us -> 124 us (0.919)
  starting transfers between devices: 111 us -> 93.6 us
  waiting for transfers between devices: 5.6 us -> 17.1 us
  Pallas kernels: 12.5 us -> 6.69 us
    ppermute x15 -> x8, starting transfers between devices: 49.4 us -> 27.5 us  [the longest x3 14.7 us: program(): after = lax.ppermute(after, ('row', 'col'), ring_x(1))]
    ppermute x1, waiting for transfers between devices: 0.01 us -> 6.25 us  [program(): back = lax.ppermute(near, 'row', ring_y(3))]
    pallas_call x1, Pallas kernels: 12.5 us -> 6.69 us  [multiply(): pl.pallas_call(kernel, out_shape=jax.ShapeDtypeStruct((RESULTS, SIDE, SID...]
    ppermute x3, starting transfers between devices: 7.87 us -> 11.8 us  [program(): other = [lax.ppermute(part, 'row', SWAP_CORE) for part in mine]]
    ppermute x1, waiting for transfers between devices: 0.01 us -> 2.05 us  [program(): behind = lax.ppermute(b_own, 'row', ring_y(1))]
    ppermute x3, waiting for transfers between devices: 0.41 us -> 2.31 us  [program(): lax.ppermute(b_first, 'row', to_plane(z))]
    ppermute x15 -> x8, waiting for transfers between devices: 4.74 us -> 6.05 us  [the longest x1 3.55 us: program(): a_blocks.append(lax.ppermute(after, ('row', 'col'), ring_x(1)))]
  transfers between devices with their start and end apart: 35 -> 28, of which waited for: 5 -> 6; matrix products, arithmetic and copies ran while one was open for 2% -> 2% of each run, Pallas kernels for 0% -> 0%
where the time goes in v1:
time: 124 us; the launch traced here: 123 us
  starting transfers between devices  93.6 us (75%)
  waiting for transfers between devices  17.1 us (14%)
  Pallas kernels  6.69 us (5%)
  local copies, waits for them, and re-layouts  2.67 us (2%)
  other arithmetic  1.93 us (2%)
    ppermute x10, starting transfers between devices, scatter(): arrived = [lax.ppermute(shards[k], axis, SCATTER[k]) for k in range(SHARDS)]  29.9 us
    ppermute x3, starting transfers between devices, program(): after = lax.ppermute(after, ('row', 'col'), ring_x(1))  14.7 us
    ppermute x3, starting transfers between devices, program(): other = [lax.ppermute(part, 'row', SWAP_CORE) for part in mine]  11.8 us
    ppermute x3, starting transfers between devices, program(): lax.ppermute(b_first, 'row', to_plane(z))  8.09 us
    pallas_call x1, Pallas kernels, multiply(): pl.pallas_call(kernel, out_shape=jax.ShapeDtypeStruct((RESULTS, SIDE, SID...  6.69 us
    ppermute x1, waiting for transfers between devices, program(): back = lax.ppermute(near, 'row', ring_y(3))  6.25 us
    ppermute x3, starting transfers between devices, program(): before = lax.ppermute(before, ('row', 'col'), ring_x(-1))  5.76 us
    ppermute x1, starting transfers between devices, program(): back = lax.ppermute(near, 'row', ring_y(3))  5.37 us
  transfers between devices with their start and end apart: 28, of which 6 were waited for; matrix products, arithmetic and copies ran while one was open for 2% of the time, Pallas kernels for 0%

profile of v1, /device:TPU:1, one launch (start us, length us, event | category | flops | bytes accessed | tf_op | source)
XLA Modules:
  0.0 122.6 jit_solution(12441612970038234035)
XLA Ops:
  1.7 7.1 %collective-permute-start.9 = (f32[160,256]{1,0:T(8,128)S(1)}, f32[160,256]{1,0:T(8,128)S(1)}, u32[]{:S(2)}, u32[]{:S(2)}) collective-permute-start(f32[160,256]{1,0:T(8,128)S(1)} %select_maximum_fusion), channel_id=1, source_target_pairs={{0,10},{1,9},{2,8},{16,26},{17,25},{18,24},{32,42},{33,41},{34,40}... | collective-permute-start | bytes 491528 | tf_op jit(solution)/shard_map/ppermute | solution.py:65
  10.0 5.8 %collective-permute-start.6 = (f32[160,256]{1,0:T(8,128)S(1)}, f32[160,256]{1,0:T(8,128)S(1)}, u32[]{:S(2)}, u32[]{:S(2)}) collective-permute-start(f32[160,256]{1,0:T(8,128)S(1)} %get-tuple-element.9), channel_id=1, source_target_pairs={{0,1},{1,15},{2,3},{16,17},{17,31},{18,19},{32,33},{33,47},{34,35}... | collective-permute-start | bytes 491528 | tf_op jit(solution)/shard_map/ppermute | solution.py:65
  15.8 1.3 %collective-permute-start.8 = (f32[160,256]{1,0:T(8,128)S(1)}, f32[160,256]{1,0:T(8,128)S(1)}, u32[]{:S(2)}, u32[]{:S(2)}) collective-permute-start(f32[160,256]{1,0:T(8,128)S(1)} %get-tuple-element.10), channel_id=1, source_target_pairs={{0,12},{1,7},{2,6},{16,28},{17,23},{18,22},{32,44},{33,39},{34,38}... | collective-permute-start | bytes 491528 | tf_op jit(solution)/shard_map/ppermute | solution.py:65
  17.1 1.3 %collective-permute-start.7 = (f32[160,256]{1,0:T(8,128)S(1)}, f32[160,256]{1,0:T(8,128)S(1)}, u32[]{:S(2)}, u32[]{:S(2)}) collective-permute-start(f32[160,256]{1,0:T(8,128)S(1)} %get-tuple-element.11), channel_id=1, source_target_pairs={{0,14},{1,5},{2,4},{16,30},{17,21},{18,20},{32,46},{33,37},{34,36}... | collective-permute-start | bytes 491528 | tf_op jit(solution)/shard_map/ppermute | solution.py:65
  19.8 7.9 %collective-permute-start.4 = (f32[160,256]{1,0:T(8,128)S(1)}, f32[160,256]{1,0:T(8,128)S(1)}, u32[]{:S(2)}, u32[]{:S(2)}) collective-permute-start(f32[160,256]{1,0:T(8,128)S(1)} %select_maximum_fusion.1), channel_id=1, source_target_pairs={{0,160},{16,144},{32,128},{1,161},{17,145},{33,129},{2,162},{18,14... | collective-permute-start | bytes 491528 | tf_op jit(solution)/shard_map/ppermute | solution.py:65
  27.7 1.9 %collective-permute-start.1 = (f32[160,256]{1,0:T(8,128)S(1)}, f32[160,256]{1,0:T(8,128)S(1)}, u32[]{:S(2)}, u32[]{:S(2)}) collective-permute-start(f32[160,256]{1,0:T(8,128)S(1)} %get-tuple-element.13), channel_id=1, source_target_pairs={{0,16},{16,240},{32,48},{1,17},{17,241},{33,49},{2,18},{18,242},{3... | collective-permute-start | bytes 491528 | tf_op jit(solution)/shard_map/ppermute | solution.py:65
  29.6 1.3 %collective-permute-start.3 = (f32[160,256]{1,0:T(8,128)S(1)}, f32[160,256]{1,0:T(8,128)S(1)}, u32[]{:S(2)}, u32[]{:S(2)}) collective-permute-start(f32[160,256]{1,0:T(8,128)S(1)} %get-tuple-element.14), channel_id=1, source_target_pairs={{0,192},{16,112},{32,96},{1,193},{17,113},{33,97},{2,194},{18,114}... | collective-permute-start | bytes 491528 | tf_op jit(solution)/shard_map/ppermute | solution.py:65
  30.9 1.3 %collective-permute-start.2 = (f32[160,256]{1,0:T(8,128)S(1)}, f32[160,256]{1,0:T(8,128)S(1)}, u32[]{:S(2)}, u32[]{:S(2)}) collective-permute-start(f32[160,256]{1,0:T(8,128)S(1)} %get-tuple-element.15), channel_id=1, source_target_pairs={{0,224},{16,80},{32,64},{1,225},{17,81},{33,65},{2,226},{18,82},{3... | collective-permute-start | bytes 491528 | tf_op jit(solution)/shard_map/ppermute | solution.py:65
  34.6 2.5 %collective-permute-start.10 = (f32[160,256]{1,0:T(8,128)S(1)}, f32[160,256]{1,0:T(8,128)S(1)}, u32[]{:S(2)}, u32[]{:S(2)}) collective-permute-start(f32[160,256]{1,0:T(8,128)S(1)} %add_select_fusion), channel_id=1, source_target_pairs={{0,1},{1,0},{2,3},{3,2},{4,5},{5,4},{6,7},{7,6},{8,9},{9,8},{10,11... | collective-permute-start | bytes 491528 | tf_op jit(solution)/shard_map/ppermute | solution.py:175
  37.6 5.5 %collective-permute-start.20 = (f32[160,256]{1,0:T(8,128)S(1)}, f32[160,256]{1,0:T(8,128)S(1)}, u32[]{:S(2)}, u32[]{:S(2)}) collective-permute-start(f32[160,256]{1,0:T(8,128)S(1)} %add_select_fusion.1), channel_id=1, source_target_pairs={{0,768},{16,784},{32,800},{48,816},{64,832},{80,848},{96,864},{112... | collective-permute-start | bytes 491528 | tf_op jit(solution)/shard_map/ppermute | solution.py:173
  43.1 1.3 %collective-permute-start.19 = (f32[160,256]{1,0:T(8,128)S(1)}, f32[160,256]{1,0:T(8,128)S(1)}, u32[]{:S(2)}, u32[]{:S(2)}) collective-permute-start(f32[160,256]{1,0:T(8,128)S(1)} %add_select_fusion.1), channel_id=1, source_target_pairs={{0,512},{16,528},{32,544},{48,560},{64,576},{80,592},{96,608},{112... | collective-permute-start | bytes 491528 | tf_op jit(solution)/shard_map/ppermute | solution.py:173
  44.4 1.3 %collective-permute-start.18 = (f32[160,256]{1,0:T(8,128)S(1)}, f32[160,256]{1,0:T(8,128)S(1)}, u32[]{:S(2)}, u32[]{:S(2)}) collective-permute-start(f32[160,256]{1,0:T(8,128)S(1)} %add_select_fusion.1), channel_id=1, source_target_pairs={{0,256},{16,272},{32,288},{48,304},{64,320},{80,336},{96,352},{112... | collective-permute-start | bytes 491528 | tf_op jit(solution)/shard_map/ppermute | solution.py:173
  45.8 5.0 %collective-permute-start.11 = (f32[320,256]{1,0:T(8,128)S(1)}, f32[320,256]{1,0:T(8,128)S(1)}, u32[]{:S(2)}, u32[]{:S(2)}) collective-permute-start(f32[320,256]{1,0:T(8,128)S(1)} %pad_maximum_fusion.1.refs_0_), channel_id=1, source_target_pairs={{0,2},{1,3},{2,4},{3,5},{4,6},{5,7},{6,8},{7,9},{8,10},{9,11},{10,... | collective-permute-start | bytes 983048 | tf_op jit(solution)/shard_map/ppermute | solution.py:178
  50.8 2.3 %collective-permute-done.20 = f32[160,256]{1,0:T(8,128)S(1)} collective-permute-done((f32[160,256]{1,0:T(8,128)S(1)}, f32[160,256]{1,0:T(8,128)S(1)}, u32[]{:S(2)}, u32[]{:S(2)}) %collective-permute-start.20) | collective-permute-done | bytes 163872 | tf_op jit(solution)/shard_map/ppermute | solution.py:173
  53.2 3.3 %collective-permute-start.22 = (f32[160,256]{1,0:T(8,128)S(1)}, f32[160,256]{1,0:T(8,128)S(1)}, u32[]{:S(2)}, u32[]{:S(2)}) collective-permute-start(f32[160,256]{1,0:T(8,128)S(1)} %add_add_fusion), channel_id=1, source_target_pairs={{0,224},{16,48},{32,0},{48,80},{64,32},{80,112},{96,64},{112,144},... | collective-permute-start | bytes 491528 | tf_op jit(solution)/shard_map/ppermute | solution.py:184
  56.5 4.5 %collective-permute-start.21 = (f32[160,256]{1,0:T(8,128)S(1)}, f32[160,256]{1,0:T(8,128)S(1)}, u32[]{:S(2)}, u32[]{:S(2)}) collective-permute-start(f32[160,256]{1,0:T(8,128)S(1)} %add_add_fusion), channel_id=1, source_target_pairs={{0,32},{16,240},{32,64},{48,16},{64,96},{80,48},{96,128},{112,80},... | collective-permute-start | bytes 491528 | tf_op jit(solution)/shard_map/ppermute | solution.py:183
  61.0 1.9 %collective-permute-start.12 = (f32[320,256]{1,0:T(8,128)S(1)}, f32[320,256]{1,0:T(8,128)S(1)}, u32[]{:S(2)}, u32[]{:S(2)}) collective-permute-start(f32[320,256]{1,0:T(8,128)S(1)} %pad_maximum_fusion.1.refs_0_), channel_id=1, source_target_pairs={{0,14},{1,15},{2,0},{3,1},{4,2},{5,3},{6,4},{7,5},{8,6},{9,7},{10,... | collective-permute-start | bytes 983048 | tf_op jit(solution)/shard_map/ppermute | solution.py:179
  63.0 2.1 %collective-permute-done.21 = f32[160,256]{1,0:T(8,128)S(1)} collective-permute-done((f32[160,256]{1,0:T(8,128)S(1)}, f32[160,256]{1,0:T(8,128)S(1)}, u32[]{:S(2)}, u32[]{:S(2)}) %collective-permute-start.21) | collective-permute-done | bytes 163872 | tf_op jit(solution)/shard_map/ppermute | solution.py:183
  65.0 5.4 %collective-permute-start.23 = (f32[480,256]{1,0:T(8,128)S(1)}, f32[480,256]{1,0:T(8,128)S(1)}, u32[]{:S(2)}, u32[]{:S(2)}) collective-permute-start(f32[480,256]{1,0:T(8,128)S(1)} %pad_maximum_fusion.refs_9_), channel_id=1, source_target_pairs={{0,96},{16,176},{32,128},{48,208},{64,160},{80,240},{96,192},{112,... | collective-permute-start | bytes 1474568 | tf_op jit(solution)/shard_map/ppermute | solution.py:186
  70.4 5.0 %collective-permute-start.13 = (f32[320,256]{1,0:T(8,128)S(1)}, f32[320,256]{1,0:T(8,128)S(1)}, u32[]{:S(2)}, u32[]{:S(2)}) collective-permute-start(f32[320,256]{1,0:T(8,128)S(1)} %collective-permute-done.11.refs_1_), channel_id=1, source_target_pairs={{0,2},{1,3},{2,4},{3,5},{4,6},{5,7},{6,8},{7,9},{8,10},{9,11},{10,... | collective-permute-start | bytes 983048 | tf_op jit(solution)/shard_map/ppermute | solution.py:178
  75.5 3.2 %collective-permute-start.24 = (f32[320,256]{1,0:T(8,128)S(1)}, f32[320,256]{1,0:T(8,128)S(1)}, u32[]{:S(2)}, u32[]{:S(2)}) collective-permute-start(f32[320,256]{1,0:T(8,128)S(1)} %pad_maximum_fusion.2), channel_id=1, source_target_pairs={{0,192},{16,80},{32,224},{48,112},{64,0},{80,144},{96,32},{112,176... | collective-permute-start | bytes 983048 | tf_op jit(solution)/shard_map/ppermute | solution.py:187
  78.7 1.9 %collective-permute-start.14 = (f32[320,256]{1,0:T(8,128)S(1)}, f32[320,256]{1,0:T(8,128)S(1)}, u32[]{:S(2)}, u32[]{:S(2)}) collective-permute-start(f32[320,256]{1,0:T(8,128)S(1)} %collective-permute-done.12.refs_2_), channel_id=1, source_target_pairs={{0,14},{1,15},{2,0},{3,1},{4,2},{5,3},{6,4},{7,5},{8,6},{9,7},{10,... | collective-permute-start | bytes 983048 | tf_op jit(solution)/shard_map/ppermute | solution.py:179
  80.7 4.6 %collective-permute-start.15 = (f32[320,256]{1,0:T(8,128)S(1)}, f32[320,256]{1,0:T(8,128)S(1)}, u32[]{:S(2)}, u32[]{:S(2)}) collective-permute-start(f32[320,256]{1,0:T(8,128)S(1)} %collective-permute-done.13.refs_3_), channel_id=1, source_target_pairs={{0,2},{1,3},{2,4},{3,5},{4,6},{5,7},{6,8},{7,9},{8,10},{9,11},{10,... | collective-permute-start | bytes 983048 | tf_op jit(solution)/shard_map/ppermute | solution.py:178
  85.2 1.9 %collective-permute-start.26 = (f32[480,256]{1,0:T(8,128)S(1)}, f32[480,256]{1,0:T(8,128)S(1)}, u32[]{:S(2)}, u32[]{:S(2)}) collective-permute-start(f32[480,256]{1,0:T(8,128)S(1)} %pad_maximum_fusion.refs_9_), channel_id=1, source_target_pairs={{0,16},{16,0},{32,48},{48,32},{64,80},{80,64},{96,112},{112,96},{1... | collective-permute-start | bytes 1474568 | tf_op jit(solution)/shard_map/ppermute | solution.py:189
  87.2 6.3 %collective-permute-done.23.refs_8_ = f32[480,256]{1,0:T(8,128)S(1)} collective-permute-done((f32[480,256]{1,0:T(8,128)S(1)}, f32[480,256]{1,0:T(8,128)S(1)}, u32[]{:S(2)}, u32[]{:S(2)}) %collective-permute-start.23) | collective-permute-done | bytes 491552 | tf_op jit(solution)/shard_map/ppermute | solution.py:186
  93.4 7.9 %collective-permute-start.25 = (f32[480,256]{1,0:T(8,128)S(1)}, f32[480,256]{1,0:T(8,128)S(1)}, u32[]{:S(2)}, u32[]{:S(2)}) collective-permute-start(f32[480,256]{1,0:T(8,128)S(1)} %collective-permute-done.23.refs_8_), channel_id=1, source_target_pairs={{0,16},{16,0},{32,48},{48,32},{64,80},{80,64},{96,112},{112,96},{1... | collective-permute-start | bytes 1474568 | tf_op jit(solution)/shard_map/ppermute | solution.py:189
  101.4 1.9 %collective-permute-start.27 = (f32[320,256]{1,0:T(8,128)S(1)}, f32[320,256]{1,0:T(8,128)S(1)}, u32[]{:S(2)}, u32[]{:S(2)}) collective-permute-start(f32[320,256]{1,0:T(8,128)S(1)} %collective-permute-done.24.refs_10_), channel_id=1, source_target_pairs={{0,16},{16,0},{32,48},{48,32},{64,80},{80,64},{96,112},{112,96},{1... | collective-permute-start | bytes 983048 | tf_op jit(solution)/shard_map/ppermute | solution.py:189
  103.3 1.9 %collective-permute-start.16 = (f32[320,256]{1,0:T(8,128)S(1)}, f32[320,256]{1,0:T(8,128)S(1)}, u32[]{:S(2)}, u32[]{:S(2)}) collective-permute-start(f32[320,256]{1,0:T(8,128)S(1)} %collective-permute-done.14.refs_4_), channel_id=1, source_target_pairs={{0,14},{1,15},{2,0},{3,1},{4,2},{5,3},{6,4},{7,5},{8,6},{9,7},{10,... | collective-permute-start | bytes 983048 | tf_op jit(solution)/shard_map/ppermute | solution.py:179
  105.2 4.6 %collective-permute-start.17 = (f32[320,256]{1,0:T(8,128)S(1)}, f32[320,256]{1,0:T(8,128)S(1)}, u32[]{:S(2)}, u32[]{:S(2)}) collective-permute-start(f32[320,256]{1,0:T(8,128)S(1)} %collective-permute-done.15.refs_5_), channel_id=1, source_target_pairs={{0,2},{1,3},{2,4},{3,5},{4,6},{5,7},{6,8},{7,9},{8,10},{9,11},{10,... | collective-permute-start | bytes 983048 | tf_op jit(solution)/shard_map/ppermute | solution.py:181
  109.8 2.5 %collective-permute-done.16.refs_6_ = f32[320,256]{1,0:T(8,128)S(1)} collective-permute-done((f32[320,256]{1,0:T(8,128)S(1)}, f32[320,256]{1,0:T(8,128)S(1)}, u32[]{:S(2)}, u32[]{:S(2)}) %collective-permute-start.16) | collective-permute-done | bytes 327712 | tf_op jit(solution)/shard_map/ppermute | solution.py:179
  112.3 3.5 %collective-permute-done.17.refs_7_ = f32[320,256]{1,0:T(8,128)S(1)} collective-permute-done((f32[320,256]{1,0:T(8,128)S(1)}, f32[320,256]{1,0:T(8,128)S(1)}, u32[]{:S(2)}, u32[]{:S(2)}) %collective-permute-start.17) | collective-permute-done | bytes 327712 | tf_op jit(solution)/shard_map/ppermute | solution.py:181
  115.9 6.7 %shard_map.82 = f32[6,256,256]{2,1,0:T(8,128)} custom-call(s32[69]{0:T(128)S(1)} %concatenate.19.ints, f32[320,256]{1,0:T(8,128)S(1)} %pad_maximum_fusion.1.refs_0_, f32[320,256]{1,0:T(8,128)S(1)} %collective-permute-done.11.refs_1_, f32[320,256]{1,0:T(8,128)S(1)} %collective-permute-done.12.refs_2_, f32[320,256]{1,0:T(8,128)S(1)} %collective-permute-done.13.refs_3_, ...), custom_call_target="tpu_custom_call" | custom-call | tf_op jit(solution)/shard_map/pallas_call | solution.py:142
  (56 shorter events, 7.0 us)
Async XLA Ops:
  0.0 19.1 %copy-start = (f32[1,1,3,256,256]{4,3,2,1,0:T(8,128)S(1)}, f32[1,1,3,256,256]{4,3,2,1,0:T(8,128)}, u32[]{:S(2)}) copy-start(f32[1,1,3,256,256]{4,3,2,1,0:T(8,128)} %param.9) | copy-start | bytes 2359300
  0.7 18.4 %copy-start.5 = (s32[1,1,3]{2,1,0:T(1,128)S(1)}, s32[1,1,3]{2,1,0:T(1,128)}, u32[]{:S(2)}) copy-start(s32[1,1,3]{2,1,0:T(1,128)} %param.11) | copy-start | bytes 40
  1.7 17.9 %copy-start.3 = (s32[1,1,3]{2,1,0:T(1,128)S(1)}, s32[1,1,3]{2,1,0:T(1,128)}, u32[]{:S(2)}) copy-start(s32[1,1,3]{2,1,0:T(1,128)} %param.14) | copy-start | bytes 40
  1.7 17.9 %copy-start.4 = (s32[16]{0:T(128)S(1)}, s32[16]{0:T(128)}, u32[]{:S(2)}) copy-start(s32[16]{0:T(128)} %constant.17.clone) | copy-start | bytes 196
  1.7 18.0 %collective-permute-start.9 = (f32[160,256]{1,0:T(8,128)S(1)}, f32[160,256]{1,0:T(8,128)S(1)}, u32[]{:S(2)}, u32[]{:S(2)}) collective-permute-start(f32[160,256]{1,0:T(8,128)S(1)} %select_maximum_fusion), channel_id=1, source_target_pairs={{0,10},{1,9},{2,8},{16,26},{17,25},{18,24},{32,42},{33,41},{34,40}... | collective-permute-start | bytes 491528 | tf_op jit(solution)/shard_map/ppermute | solution.py:65
  10.0 17.7 %collective-permute-start.6 = (f32[160,256]{1,0:T(8,128)S(1)}, f32[160,256]{1,0:T(8,128)S(1)}, u32[]{:S(2)}, u32[]{:S(2)}) collective-permute-start(f32[160,256]{1,0:T(8,128)S(1)} %get-tuple-element.9), channel_id=1, source_target_pairs={{0,1},{1,15},{2,3},{16,17},{17,31},{18,19},{32,33},{33,47},{34,35}... | collective-permute-start | bytes 491528 | tf_op jit(solution)/shard_map/ppermute | solution.py:65
  15.8 13.8 %collective-permute-start.8 = (f32[160,256]{1,0:T(8,128)S(1)}, f32[160,256]{1,0:T(8,128)S(1)}, u32[]{:S(2)}, u32[]{:S(2)}) collective-permute-start(f32[160,256]{1,0:T(8,128)S(1)} %get-tuple-element.10), channel_id=1, source_target_pairs={{0,12},{1,7},{2,6},{16,28},{17,23},{18,22},{32,44},{33,39},{34,38}... | collective-permute-start | bytes 491528 | tf_op jit(solution)/shard_map/ppermute | solution.py:65
  17.1 13.8 %collective-permute-start.7 = (f32[160,256]{1,0:T(8,128)S(1)}, f32[160,256]{1,0:T(8,128)S(1)}, u32[]{:S(2)}, u32[]{:S(2)}) collective-permute-start(f32[160,256]{1,0:T(8,128)S(1)} %get-tuple-element.11), channel_id=1, source_target_pairs={{0,14},{1,5},{2,4},{16,30},{17,21},{18,20},{32,46},{33,37},{34,36}... | collective-permute-start | bytes 491528 | tf_op jit(solution)/shard_map/ppermute | solution.py:65
  18.4 13.8 %collective-permute-start.5 = (f32[160,256]{1,0:T(8,128)S(1)}, f32[160,256]{1,0:T(8,128)S(1)}, u32[]{:S(2)}, u32[]{:S(2)}) collective-permute-start(f32[160,256]{1,0:T(8,128)S(1)} %get-tuple-element.12), channel_id=1, source_target_pairs={{1,13},{17,29},{33,45},{49,61},{65,77},{81,93},{97,109},{113,125},... | collective-permute-start | bytes 491528 | tf_op jit(solution)/shard_map/ppermute | solution.py:65
  19.8 14.8 %collective-permute-start.4 = (f32[160,256]{1,0:T(8,128)S(1)}, f32[160,256]{1,0:T(8,128)S(1)}, u32[]{:S(2)}, u32[]{:S(2)}) collective-permute-start(f32[160,256]{1,0:T(8,128)S(1)} %select_maximum_fusion.1), channel_id=1, source_target_pairs={{0,160},{16,144},{32,128},{1,161},{17,145},{33,129},{2,162},{18,14... | collective-permute-start | bytes 491528 | tf_op jit(solution)/shard_map/ppermute | solution.py:65
  27.7 9.4 %collective-permute-start.1 = (f32[160,256]{1,0:T(8,128)S(1)}, f32[160,256]{1,0:T(8,128)S(1)}, u32[]{:S(2)}, u32[]{:S(2)}) collective-permute-start(f32[160,256]{1,0:T(8,128)S(1)} %get-tuple-element.13), channel_id=1, source_target_pairs={{0,16},{16,240},{32,48},{1,17},{17,241},{33,49},{2,18},{18,242},{3... | collective-permute-start | bytes 491528 | tf_op jit(solution)/shard_map/ppermute | solution.py:65
  29.6 7.5 %collective-permute-start.3 = (f32[160,256]{1,0:T(8,128)S(1)}, f32[160,256]{1,0:T(8,128)S(1)}, u32[]{:S(2)}, u32[]{:S(2)}) collective-permute-start(f32[160,256]{1,0:T(8,128)S(1)} %get-tuple-element.14), channel_id=1, source_target_pairs={{0,192},{16,112},{32,96},{1,193},{17,113},{33,97},{2,194},{18,114}... | collective-permute-start | bytes 491528 | tf_op jit(solution)/shard_map/ppermute | solution.py:65
  30.9 6.2 %collective-permute-start.2 = (f32[160,256]{1,0:T(8,128)S(1)}, f32[160,256]{1,0:T(8,128)S(1)}, u32[]{:S(2)}, u32[]{:S(2)}) collective-permute-start(f32[160,256]{1,0:T(8,128)S(1)} %get-tuple-element.15), channel_id=1, source_target_pairs={{0,224},{16,80},{32,64},{1,225},{17,81},{33,65},{2,226},{18,82},{3... | collective-permute-start | bytes 491528 | tf_op jit(solution)/shard_map/ppermute | solution.py:65
  32.3 5.3 %collective-permute-start = (f32[160,256]{1,0:T(8,128)S(1)}, f32[160,256]{1,0:T(8,128)S(1)}, u32[]{:S(2)}, u32[]{:S(2)}) collective-permute-start(f32[160,256]{1,0:T(8,128)S(1)} %get-tuple-element.16), channel_id=1, source_target_pairs={{16,208},{17,209},{18,210},{19,211},{20,212},{21,213},{22,214},{23... | collective-permute-start | bytes 491528 | tf_op jit(solution)/shard_map/ppermute | solution.py:65
  34.6 11.2 %collective-permute-start.10 = (f32[160,256]{1,0:T(8,128)S(1)}, f32[160,256]{1,0:T(8,128)S(1)}, u32[]{:S(2)}, u32[]{:S(2)}) collective-permute-start(f32[160,256]{1,0:T(8,128)S(1)} %add_select_fusion), channel_id=1, source_target_pairs={{0,1},{1,0},{2,3},{3,2},{4,5},{5,4},{6,7},{7,6},{8,9},{9,8},{10,11... | collective-permute-start | bytes 491528 | tf_op jit(solution)/shard_map/ppermute | solution.py:175
  37.6 15.5 %collective-permute-start.20 = (f32[160,256]{1,0:T(8,128)S(1)}, f32[160,256]{1,0:T(8,128)S(1)}, u32[]{:S(2)}, u32[]{:S(2)}) collective-permute-start(f32[160,256]{1,0:T(8,128)S(1)} %add_select_fusion.1), channel_id=1, source_target_pairs={{0,768},{16,784},{32,800},{48,816},{64,832},{80,848},{96,864},{112... | collective-permute-start | bytes 491528 | tf_op jit(solution)/shard_map/ppermute | solution.py:173
  43.1 10.0 %collective-permute-start.19 = (f32[160,256]{1,0:T(8,128)S(1)}, f32[160,256]{1,0:T(8,128)S(1)}, u32[]{:S(2)}, u32[]{:S(2)}) collective-permute-start(f32[160,256]{1,0:T(8,128)S(1)} %add_select_fusion.1), channel_id=1, source_target_pairs={{0,512},{16,528},{32,544},{48,560},{64,576},{80,592},{96,608},{112... | collective-permute-start | bytes 491528 | tf_op jit(solution)/shard_map/ppermute | solution.py:173
  44.4 8.7 %collective-permute-start.18 = (f32[160,256]{1,0:T(8,128)S(1)}, f32[160,256]{1,0:T(8,128)S(1)}, u32[]{:S(2)}, u32[]{:S(2)}) collective-permute-start(f32[160,256]{1,0:T(8,128)S(1)} %add_select_fusion.1), channel_id=1, source_target_pairs={{0,256},{16,272},{32,288},{48,304},{64,320},{80,336},{96,352},{112... | collective-permute-start | bytes 491528 | tf_op jit(solution)/shard_map/ppermute | solution.py:173
  45.8 24.7 %collective-permute-start.11 = (f32[320,256]{1,0:T(8,128)S(1)}, f32[320,256]{1,0:T(8,128)S(1)}, u32[]{:S(2)}, u32[]{:S(2)}) collective-permute-start(f32[320,256]{1,0:T(8,128)S(1)} %pad_maximum_fusion.1.refs_0_), channel_id=1, source_target_pairs={{0,2},{1,3},{2,4},{3,5},{4,6},{5,7},{6,8},{7,9},{8,10},{9,11},{10,... | collective-permute-start | bytes 983048 | tf_op jit(solution)/shard_map/ppermute | solution.py:178
  53.2 9.8 %collective-permute-start.22 = (f32[160,256]{1,0:T(8,128)S(1)}, f32[160,256]{1,0:T(8,128)S(1)}, u32[]{:S(2)}, u32[]{:S(2)}) collective-permute-start(f32[160,256]{1,0:T(8,128)S(1)} %add_add_fusion), channel_id=1, source_target_pairs={{0,224},{16,48},{32,0},{48,80},{64,32},{80,112},{96,64},{112,144},... | collective-permute-start | bytes 491528 | tf_op jit(solution)/shard_map/ppermute | solution.py:184
  56.5 8.5 %collective-permute-start.21 = (f32[160,256]{1,0:T(8,128)S(1)}, f32[160,256]{1,0:T(8,128)S(1)}, u32[]{:S(2)}, u32[]{:S(2)}) collective-permute-start(f32[160,256]{1,0:T(8,128)S(1)} %add_add_fusion), channel_id=1, source_target_pairs={{0,32},{16,240},{32,64},{48,16},{64,96},{80,48},{96,128},{112,80},... | collective-permute-start | bytes 491528 | tf_op jit(solution)/shard_map/ppermute | solution.py:183
  61.0 17.7 %collective-permute-start.12 = (f32[320,256]{1,0:T(8,128)S(1)}, f32[320,256]{1,0:T(8,128)S(1)}, u32[]{:S(2)}, u32[]{:S(2)}) collective-permute-start(f32[320,256]{1,0:T(8,128)S(1)} %pad_maximum_fusion.1.refs_0_), channel_id=1, source_target_pairs={{0,14},{1,15},{2,0},{3,1},{4,2},{5,3},{6,4},{7,5},{8,6},{9,7},{10,... | collective-permute-start | bytes 983048 | tf_op jit(solution)/shard_map/ppermute | solution.py:179
  65.0 28.4 %collective-permute-start.23 = (f32[480,256]{1,0:T(8,128)S(1)}, f32[480,256]{1,0:T(8,128)S(1)}, u32[]{:S(2)}, u32[]{:S(2)}) collective-permute-start(f32[480,256]{1,0:T(8,128)S(1)} %pad_maximum_fusion.refs_9_), channel_id=1, source_target_pairs={{0,96},{16,176},{32,128},{48,208},{64,160},{80,240},{96,192},{112,... | collective-permute-start | bytes 1474568 | tf_op jit(solution)/shard_map/ppermute | solution.py:186
  70.4 10.2 %collective-permute-start.13 = (f32[320,256]{1,0:T(8,128)S(1)}, f32[320,256]{1,0:T(8,128)S(1)}, u32[]{:S(2)}, u32[]{:S(2)}) collective-permute-start(f32[320,256]{1,0:T(8,128)S(1)} %collective-permute-done.11.refs_1_), channel_id=1, source_target_pairs={{0,2},{1,3},{2,4},{3,5},{4,6},{5,7},{6,8},{7,9},{8,10},{9,11},{10,... | collective-permute-start | bytes 983048 | tf_op jit(solution)/shard_map/ppermute | solution.py:178
  75.5 25.8 %collective-permute-start.24 = (f32[320,256]{1,0:T(8,128)S(1)}, f32[320,256]{1,0:T(8,128)S(1)}, u32[]{:S(2)}, u32[]{:S(2)}) collective-permute-start(f32[320,256]{1,0:T(8,128)S(1)} %pad_maximum_fusion.2), channel_id=1, source_target_pairs={{0,192},{16,80},{32,224},{48,112},{64,0},{80,144},{96,32},{112,176... | collective-permute-start | bytes 983048 | tf_op jit(solution)/shard_map/ppermute | solution.py:187
  78.7 24.6 %collective-permute-start.14 = (f32[320,256]{1,0:T(8,128)S(1)}, f32[320,256]{1,0:T(8,128)S(1)}, u32[]{:S(2)}, u32[]{:S(2)}) collective-permute-start(f32[320,256]{1,0:T(8,128)S(1)} %collective-permute-done.12.refs_2_), channel_id=1, source_target_pairs={{0,14},{1,15},{2,0},{3,1},{4,2},{5,3},{6,4},{7,5},{8,6},{9,7},{10,... | collective-permute-start | bytes 983048 | tf_op jit(solution)/shard_map/ppermute | solution.py:179
  80.7 24.6 %collective-permute-start.15 = (f32[320,256]{1,0:T(8,128)S(1)}, f32[320,256]{1,0:T(8,128)S(1)}, u32[]{:S(2)}, u32[]{:S(2)}) collective-permute-start(f32[320,256]{1,0:T(8,128)S(1)} %collective-permute-done.13.refs_3_), channel_id=1, source_target_pairs={{0,2},{1,3},{2,4},{3,5},{4,6},{5,7},{6,8},{7,9},{8,10},{9,11},{10,... | collective-permute-start | bytes 983048 | tf_op jit(solution)/shard_map/ppermute | solution.py:178
  85.2 24.6 %collective-permute-start.26 = (f32[480,256]{1,0:T(8,128)S(1)}, f32[480,256]{1,0:T(8,128)S(1)}, u32[]{:S(2)}, u32[]{:S(2)}) collective-permute-start(f32[480,256]{1,0:T(8,128)S(1)} %pad_maximum_fusion.refs_9_), channel_id=1, source_target_pairs={{0,16},{16,0},{32,48},{48,32},{64,80},{80,64},{96,112},{112,96},{1... | collective-permute-start | bytes 1474568 | tf_op jit(solution)/shard_map/ppermute | solution.py:189
  93.4 18.9 %collective-permute-start.25 = (f32[480,256]{1,0:T(8,128)S(1)}, f32[480,256]{1,0:T(8,128)S(1)}, u32[]{:S(2)}, u32[]{:S(2)}) collective-permute-start(f32[480,256]{1,0:T(8,128)S(1)} %collective-permute-done.23.refs_8_), channel_id=1, source_target_pairs={{0,16},{16,0},{32,48},{48,32},{64,80},{80,64},{96,112},{112,96},{1... | collective-permute-start | bytes 1474568 | tf_op jit(solution)/shard_map/ppermute | solution.py:189
  101.4 8.5 %collective-permute-start.27 = (f32[320,256]{1,0:T(8,128)S(1)}, f32[320,256]{1,0:T(8,128)S(1)}, u32[]{:S(2)}, u32[]{:S(2)}) collective-permute-start(f32[320,256]{1,0:T(8,128)S(1)} %collective-permute-done.24.refs_10_), channel_id=1, source_target_pairs={{0,16},{16,0},{32,48},{48,32},{64,80},{80,64},{96,112},{112,96},{1... | collective-permute-start | bytes 983048 | tf_op jit(solution)/shard_map/ppermute | solution.py:189
  103.3 9.0 %collective-permute-start.16 = (f32[320,256]{1,0:T(8,128)S(1)}, f32[320,256]{1,0:T(8,128)S(1)}, u32[]{:S(2)}, u32[]{:S(2)}) collective-permute-start(f32[320,256]{1,0:T(8,128)S(1)} %collective-permute-done.14.refs_4_), channel_id=1, source_target_pairs={{0,14},{1,15},{2,0},{3,1},{4,2},{5,3},{6,4},{7,5},{8,6},{9,7},{10,... | collective-permute-start | bytes 983048 | tf_op jit(solution)/shard_map/ppermute | solution.py:179
  105.2 10.6 %collective-permute-start.17 = (f32[320,256]{1,0:T(8,128)S(1)}, f32[320,256]{1,0:T(8,128)S(1)}, u32[]{:S(2)}, u32[]{:S(2)}) collective-permute-start(f32[320,256]{1,0:T(8,128)S(1)} %collective-permute-done.15.refs_5_), channel_id=1, source_target_pairs={{0,2},{1,3},{2,4},{3,5},{4,6},{5,7},{6,8},{7,9},{8,10},{9,11},{10,... | collective-permute-start | bytes 983048 | tf_op jit(solution)/shard_map/ppermute | solution.py:181
  (2 other events, 35.3 us)

commit v2 on v1

--- a/solution.py
+++ b/solution.py
@@ -10,8 +10,8 @@
 RING, PAIR, PLANES = 8, 2, 4
 SHARD = 160
 SHARDS = 5
-PANEL = SHARD * SHARDS
-LIST_ROW = SLOTS * SIDE
+PANEL = SLOTS * SIDE
+LIST = SHARDS * SHARD - PANEL
 
 HOLDERS = (
     ((0, 0), (0, 1), (7, 0), (6, 0), (5, 0)),
@@ -19,10 +19,14 @@
     ((1, 0), (1, 1), (2, 0), (3, 0), (4, 0)),
 )
 HOLDER = tuple(tuple(ring * PAIR + pair for ring, pair in panel) for panel in HOLDERS)
-SLOT_OF = [STEPS * SHARDS] * (RING * PAIR)
+HEAD_AT = [STEPS * PANEL] * (RING * PAIR)
+REST_AT = [STEPS * PANEL + LIST] * (RING * PAIR)
 for _s in range(STEPS):
     for _k in range(SHARDS):
-        SLOT_OF[HOLDER[_s][_k]] = _s * SHARDS + _k
+        _at = _s * PANEL + min(_k * SHARD, PANEL - SHARD)
+        REST_AT[HOLDER[_s][_k]] = _at + LIST
+        if _k < SHARDS - 1:
+            HEAD_AT[HOLDER[_s][_k]] = _at
 
 SCATTER = [
     [(s, HOLDER[s][k]) for s in range(STEPS) if HOLDER[s][k] != s] for k in range(SHARDS)
@@ -59,9 +63,10 @@
 
 def scatter(tiles, listed, axis, index):
     panel = tiles.reshape(SLOTS * SIDE, SIDE)
-    spare = jnp.pad(listed.astype(jnp.float32)[None, :], ((0, PANEL - LIST_ROW - 1), (0, SIDE - SLOTS)))
     shards = [panel[k * SHARD : (k + 1) * SHARD] for k in range(SHARDS - 1)]
-    shards.append(jnp.concatenate([panel[(SHARDS - 1) * SHARD :], spare]))
+    spare = jnp.pad(listed[None, :], ((0, SHARD - 1), (0, SIDE - SLOTS))).astype(jnp.float32)
+    rows = lax.broadcasted_iota(jnp.int32, (SHARD, SIDE), 0)
+    shards.append(jnp.where(rows < LIST, spare, panel[PANEL - SHARD :]))
     arrived = [lax.ppermute(shards[k], axis, SCATTER[k]) for k in range(SHARDS)]
     keeps = jnp.logical_or(index == HOLDER[0][0], index == HOLDER[2][0])
     return jnp.where(keeps, shards[0], sum(arrived[1:], arrived[0]))
@@ -90,22 +95,23 @@
 
     asked = []
     for n, (ref, part, dest, origin) in enumerate(places):
-        slot = ints[53 + origin] + (0 if dest is a_sp else 2 * RING)
         copy = pltpu.make_async_copy(
-            ref.at[pl.ds(part * SHARD + LIST_ROW % SHARD, 8), pl.ds(0, 128)],
-            lists.at[slot],
+            ref.at[pl.ds(part * SHARD, 8), pl.ds(0, 128)],
+            lists.at[origin + (0 if dest is a_sp else 2 * RING)],
             list_sems.at[n],
         )
         copy.start()
         asked.append(copy)
     for ref, part, dest, origin in places:
-        slot = ints[53 + origin]
         value = ref[part * SHARD : (part + 1) * SHARD, :]
         high = value.astype(jnp.bfloat16)
         low = (value - high.astype(jnp.float32)).astype(jnp.bfloat16)
-        at = pl.ds(pl.multiple_of(slot * SHARD, SHARD), SHARD)
-        dest[at, :SIDE] = high
-        dest[at, SIDE:] = low
+        head = pl.ds(pl.multiple_of(ints[53 + origin], LIST), LIST)
+        rest = pl.ds(pl.multiple_of(ints[53 + 2 * RING + origin], LIST), SHARD - LIST)
+        dest[head, :SIDE] = high[:LIST]
+        dest[head, SIDE:] = low[:LIST]
+        dest[rest, :SIDE] = high[LIST:]
+        dest[rest, SIDE:] = low[LIST:]
     for copy in asked:
         copy.wait()
 
@@ -113,7 +119,7 @@
         c_row, c_col = ints[2 * l], ints[2 * l + 1]
         total = None
         for s in range(STEPS):
-            last = s * SHARDS + SHARDS - 1
+            last = HOLDER[s][SHARDS - 1]
             i, j = jnp.int32(0), jnp.int32(0)
             for t in range(SLOTS):
                 i = jnp.where(lists[last, 0, t].astype(jnp.int32) == c_row, t, i)
@@ -138,7 +144,7 @@
 def multiply(ints, a_blocks, b_blocks):
     local = pl.BlockSpec(memory_space=pltpu.VMEM)
     count = len(a_blocks) + len(b_blocks)
-    rows = (STEPS * SHARDS + 1) * SHARD
+    rows = STEPS * PANEL + SHARD
     return pl.pallas_call(
         kernel,
         out_shape=jax.ShapeDtypeStruct((RESULTS, SIDE, SIDE), jnp.float32),
@@ -163,7 +169,7 @@
             pair_count.reshape(-1),
             col.astype(jnp.int32)[None],
             row.astype(jnp.int32)[None],
-            jnp.array(SLOT_OF, jnp.int32),
+            jnp.array(HEAD_AT + REST_AT, jnp.int32),
         ]
     )
 

time: 124 us -> 122 us (0.984)
  local copies, waits for them, and re-layouts: 2.67 us -> 0.48 us
  other arithmetic: 1.93 us -> 3.77 us
    ppermute x3, starting transfers between devices: 14.7 us -> 8.56 us  [program(): after = lax.ppermute(after, ('row', 'col'), ring_x(1))]
    ppermute x3, waiting for transfers between devices: 2.31 us -> 5.63 us  [program(): lax.ppermute(b_first, 'row', to_plane(z))]
    ppermute x1, starting transfers between devices: 2.54 us -> 5.78 us  [program(): block = jnp.concatenate([a_own, lax.ppermute(a_own, 'col', SWAP_Z)])]
    ppermute x10, starting transfers between devices: 29.9 us -> 26.8 us  [scatter(): arrived = [lax.ppermute(shards[k], axis, SCATTER[k]) for k in range(SHARDS)]]
    ppermute x3, starting transfers between devices: 11.8 us -> 14.3 us  [program(): other = [lax.ppermute(part, 'row', SWAP_CORE) for part in mine]]
    slice x4 -> x0, local copies, waits for them, and re-layouts: 2.18 us -> none  [the longest x2 1.25 us: scatter(): shards = [panel[k * SHARD:(k + 1) * SHARD] for k in range(SHARDS - 1)]]
    ppermute x1, waiting for transfers between devices: 6.25 us -> 4.3 us  [program(): back = lax.ppermute(near, 'row', ring_y(3))]
    ppermute x3, starting transfers between devices: 5.76 us -> 7.57 us  [program(): before = lax.ppermute(before, ('row', 'col'), ring_x(-1))]
  transfers between devices with their start and end apart: 28 -> 28, of which waited for: 6 -> 5; matrix products, arithmetic and copies ran while one was open for 2% -> 2% of each run, Pallas kernels for 0% -> 0%
where the time goes in v2:
time: 122 us; the launch traced here: 121 us
  starting transfers between devices  92.6 us (76%)
  waiting for transfers between devices  17.1 us (14%)
  Pallas kernels  6.68 us (5%)
  other arithmetic  3.77 us (3%)
    ppermute x10, starting transfers between devices, scatter(): arrived = [lax.ppermute(shards[k], axis, SCATTER[k]) for k in range(SHARDS)]  26.8 us
    ppermute x3, starting transfers between devices, program(): other = [lax.ppermute(part, 'row', SWAP_CORE) for part in mine]  14.3 us
    ppermute x3, starting transfers between devices, program(): lax.ppermute(b_first, 'row', to_plane(z))  9.33 us
    ppermute x3, starting transfers between devices, program(): after = lax.ppermute(after, ('row', 'col'), ring_x(1))  8.56 us
    ppermute x3, starting transfers between devices, program(): before = lax.ppermute(before, ('row', 'col'), ring_x(-1))  7.57 us
    pallas_call x1, Pallas kernels, multiply(): pl.pallas_call(kernel, out_shape=jax.ShapeDtypeStruct((RESULTS, SIDE, SID...  6.68 us
    ppermute x1, starting transfers between devices, program(): block = jnp.concatenate([a_own, lax.ppermute(a_own, 'col', SWAP_Z)])  5.78 us
    ppermute x3, waiting for transfers between devices, program(): lax.ppermute(b_first, 'row', to_plane(z))  5.63 us
  transfers between devices with their start and end apart: 28, of which 5 were waited for; matrix products, arithmetic and copies ran while one was open for 2% of the time, Pallas kernels for 0%

profile of v2, /device:TPU:1, one launch (start us, length us, event | category | flops | bytes accessed | tf_op | source)
XLA Modules:
  0.0 121.1 jit_solution(1165281193954237173)
XLA Ops:
  0.0 1.7 %fusion = (f32[160,256]{1,0:T(8,128)S(1)}, f32[160,256]{1,0:T(8,128)S(1)}, f32[160,256]{1,0:T(8,128)S(1)}, f32[160,256]{1,0:T(8,128)S(1)}, f32[160,256]{1,0:T(8,...) fusion(f32[768,256]{1,0:T(8,128)} %bitcast.8, ...), kind=kLoop, calls=%fused_computation.9 | loop fusion | flops 163840 | bytes 3276984 | tf_op jit(solution)/shard_map/slice | solution.py:66
  1.7 5.7 %collective-permute-start.6 = (f32[160,256]{1,0:T(8,128)S(1)}, f32[160,256]{1,0:T(8,128)S(1)}, u32[]{:S(2)}, u32[]{:S(2)}) collective-permute-start(f32[160,256]{1,0:T(8,128)S(1)} %get-tuple-element.9), channel_id=1, source_target_pairs={{0,1},{1,15},{2,3},{16,17},{17,31},{18,19},{32,33},{33,47},{34,35}... | collective-permute-start | bytes 491528 | tf_op jit(solution)/shard_map/ppermute | solution.py:70
  7.5 2.0 %collective-permute-start.9 = (f32[160,256]{1,0:T(8,128)S(1)}, f32[160,256]{1,0:T(8,128)S(1)}, u32[]{:S(2)}, u32[]{:S(2)}) collective-permute-start(f32[160,256]{1,0:T(8,128)S(1)} %get-tuple-element.10), channel_id=1, source_target_pairs={{0,10},{1,9},{2,8},{16,26},{17,25},{18,24},{32,42},{33,41},{34,40}... | collective-permute-start | bytes 491528 | tf_op jit(solution)/shard_map/ppermute | solution.py:70
  9.5 1.3 %collective-permute-start.8 = (f32[160,256]{1,0:T(8,128)S(1)}, f32[160,256]{1,0:T(8,128)S(1)}, u32[]{:S(2)}, u32[]{:S(2)}) collective-permute-start(f32[160,256]{1,0:T(8,128)S(1)} %get-tuple-element.11), channel_id=1, source_target_pairs={{0,12},{1,7},{2,6},{16,28},{17,23},{18,22},{32,44},{33,39},{34,38}... | collective-permute-start | bytes 491528 | tf_op jit(solution)/shard_map/ppermute | solution.py:70
  10.8 1.3 %collective-permute-start.7 = (f32[160,256]{1,0:T(8,128)S(1)}, f32[160,256]{1,0:T(8,128)S(1)}, u32[]{:S(2)}, u32[]{:S(2)}) collective-permute-start(f32[160,256]{1,0:T(8,128)S(1)} %get-tuple-element.12), channel_id=1, source_target_pairs={{0,14},{1,5},{2,4},{16,30},{17,21},{18,20},{32,46},{33,37},{34,36}... | collective-permute-start | bytes 491528 | tf_op jit(solution)/shard_map/ppermute | solution.py:70
  13.3 6.6 %collective-permute-start = (f32[160,256]{1,0:T(8,128)S(1)}, f32[160,256]{1,0:T(8,128)S(1)}, u32[]{:S(2)}, u32[]{:S(2)}) collective-permute-start(f32[160,256]{1,0:T(8,128)S(1)} %get-tuple-element.19), channel_id=1, source_target_pairs={{16,208},{17,209},{18,210},{19,211},{20,212},{21,213},{22,214},{23... | collective-permute-start | bytes 491528 | tf_op jit(solution)/shard_map/ppermute | solution.py:70
  19.9 1.3 %collective-permute-start.2 = (f32[160,256]{1,0:T(8,128)S(1)}, f32[160,256]{1,0:T(8,128)S(1)}, u32[]{:S(2)}, u32[]{:S(2)}) collective-permute-start(f32[160,256]{1,0:T(8,128)S(1)} %get-tuple-element.20), channel_id=1, source_target_pairs={{0,224},{16,80},{32,64},{1,225},{17,81},{33,65},{2,226},{18,82},{3... | collective-permute-start | bytes 491528 | tf_op jit(solution)/shard_map/ppermute | solution.py:70
  21.2 1.3 %collective-permute-start.3 = (f32[160,256]{1,0:T(8,128)S(1)}, f32[160,256]{1,0:T(8,128)S(1)}, u32[]{:S(2)}, u32[]{:S(2)}) collective-permute-start(f32[160,256]{1,0:T(8,128)S(1)} %get-tuple-element.21), channel_id=1, source_target_pairs={{0,192},{16,112},{32,96},{1,193},{17,113},{33,97},{2,194},{18,114}... | collective-permute-start | bytes 491528 | tf_op jit(solution)/shard_map/ppermute | solution.py:70
  22.5 4.8 %collective-permute-start.4 = (f32[160,256]{1,0:T(8,128)S(1)}, f32[160,256]{1,0:T(8,128)S(1)}, u32[]{:S(2)}, u32[]{:S(2)}) collective-permute-start(f32[160,256]{1,0:T(8,128)S(1)} %get-tuple-element.22), channel_id=1, source_target_pairs={{0,160},{16,144},{32,128},{1,161},{17,145},{33,129},{2,162},{18,14... | collective-permute-start | bytes 491528 | tf_op jit(solution)/shard_map/ppermute | solution.py:70
  27.3 1.9 %collective-permute-start.1 = (f32[160,256]{1,0:T(8,128)S(1)}, f32[160,256]{1,0:T(8,128)S(1)}, u32[]{:S(2)}, u32[]{:S(2)}) collective-permute-start(f32[160,256]{1,0:T(8,128)S(1)} %get-tuple-element.23), channel_id=1, source_target_pairs={{0,16},{16,240},{32,48},{1,17},{17,241},{33,49},{2,18},{18,242},{3... | collective-permute-start | bytes 491528 | tf_op jit(solution)/shard_map/ppermute | solution.py:70
  30.2 5.8 %collective-permute-start.10 = (f32[160,256]{1,0:T(8,128)S(1)}, f32[160,256]{1,0:T(8,128)S(1)}, u32[]{:S(2)}, u32[]{:S(2)}) collective-permute-start(f32[160,256]{1,0:T(8,128)S(1)} %add_select_fusion), channel_id=1, source_target_pairs={{0,1},{1,0},{2,3},{3,2},{4,5},{5,4},{6,7},{7,6},{8,9},{9,8},{10,11... | collective-permute-start | bytes 491528 | tf_op jit(solution)/shard_map/ppermute | solution.py:181
  37.0 6.7 %collective-permute-start.20 = (f32[160,256]{1,0:T(8,128)S(1)}, f32[160,256]{1,0:T(8,128)S(1)}, u32[]{:S(2)}, u32[]{:S(2)}) collective-permute-start(f32[160,256]{1,0:T(8,128)S(1)} %add_select_fusion.1), channel_id=1, source_target_pairs={{0,768},{16,784},{32,800},{48,816},{64,832},{80,848},{96,864},{112... | collective-permute-start | bytes 491528 | tf_op jit(solution)/shard_map/ppermute | solution.py:179
  43.8 1.3 %collective-permute-start.19 = (f32[160,256]{1,0:T(8,128)S(1)}, f32[160,256]{1,0:T(8,128)S(1)}, u32[]{:S(2)}, u32[]{:S(2)}) collective-permute-start(f32[160,256]{1,0:T(8,128)S(1)} %add_select_fusion.1), channel_id=1, source_target_pairs={{0,512},{16,528},{32,544},{48,560},{64,576},{80,592},{96,608},{112... | collective-permute-start | bytes 491528 | tf_op jit(solution)/shard_map/ppermute | solution.py:179
  46.4 2.4 %collective-permute-start.11 = (f32[320,256]{1,0:T(8,128)S(1)}, f32[320,256]{1,0:T(8,128)S(1)}, u32[]{:S(2)}, u32[]{:S(2)}) collective-permute-start(f32[320,256]{1,0:T(8,128)S(1)} %pad_maximum_fusion.1.refs_0_), channel_id=1, source_target_pairs={{0,2},{1,3},{2,4},{3,5},{4,6},{5,7},{6,8},{7,9},{8,10},{9,11},{10,... | collective-permute-start | bytes 983048 | tf_op jit(solution)/shard_map/ppermute | solution.py:184
  48.8 5.6 %collective-permute-done.20 = f32[160,256]{1,0:T(8,128)S(1)} collective-permute-done((f32[160,256]{1,0:T(8,128)S(1)}, f32[160,256]{1,0:T(8,128)S(1)}, u32[]{:S(2)}, u32[]{:S(2)}) %collective-permute-start.20) | collective-permute-done | bytes 163872 | tf_op jit(solution)/shard_map/ppermute | solution.py:179
  54.5 3.3 %collective-permute-start.22 = (f32[160,256]{1,0:T(8,128)S(1)}, f32[160,256]{1,0:T(8,128)S(1)}, u32[]{:S(2)}, u32[]{:S(2)}) collective-permute-start(f32[160,256]{1,0:T(8,128)S(1)} %add_add_fusion), channel_id=1, source_target_pairs={{0,224},{16,48},{32,0},{48,80},{64,32},{80,112},{96,64},{112,144},... | collective-permute-start | bytes 491528 | tf_op jit(solution)/shard_map/ppermute | solution.py:190
  57.8 4.5 %collective-permute-start.21 = (f32[160,256]{1,0:T(8,128)S(1)}, f32[160,256]{1,0:T(8,128)S(1)}, u32[]{:S(2)}, u32[]{:S(2)}) collective-permute-start(f32[160,256]{1,0:T(8,128)S(1)} %add_add_fusion), channel_id=1, source_target_pairs={{0,32},{16,240},{32,64},{48,16},{64,96},{80,48},{96,128},{112,80},... | collective-permute-start | bytes 491528 | tf_op jit(solution)/shard_map/ppermute | solution.py:189
  62.3 1.9 %collective-permute-start.12 = (f32[320,256]{1,0:T(8,128)S(1)}, f32[320,256]{1,0:T(8,128)S(1)}, u32[]{:S(2)}, u32[]{:S(2)}) collective-permute-start(f32[320,256]{1,0:T(8,128)S(1)} %pad_maximum_fusion.1.refs_0_), channel_id=1, source_target_pairs={{0,14},{1,15},{2,0},{3,1},{4,2},{5,3},{6,4},{7,5},{8,6},{9,7},{10,... | collective-permute-start | bytes 983048 | tf_op jit(solution)/shard_map/ppermute | solution.py:185
  65.3 5.5 %collective-permute-start.23 = (f32[480,256]{1,0:T(8,128)S(1)}, f32[480,256]{1,0:T(8,128)S(1)}, u32[]{:S(2)}, u32[]{:S(2)}) collective-permute-start(f32[480,256]{1,0:T(8,128)S(1)} %pad_maximum_fusion.refs_9_), channel_id=1, source_target_pairs={{0,96},{16,176},{32,128},{48,208},{64,160},{80,240},{96,192},{112,... | collective-permute-start | bytes 1474568 | tf_op jit(solution)/shard_map/ppermute | solution.py:192
  70.8 2.8 %collective-permute-start.13 = (f32[320,256]{1,0:T(8,128)S(1)}, f32[320,256]{1,0:T(8,128)S(1)}, u32[]{:S(2)}, u32[]{:S(2)}) collective-permute-start(f32[320,256]{1,0:T(8,128)S(1)} %collective-permute-done.11.refs_1_), channel_id=1, source_target_pairs={{0,2},{1,3},{2,4},{3,5},{4,6},{5,7},{6,8},{7,9},{8,10},{9,11},{10,... | collective-permute-start | bytes 983048 | tf_op jit(solution)/shard_map/ppermute | solution.py:184
  73.6 3.0 %collective-permute-start.24 = (f32[320,256]{1,0:T(8,128)S(1)}, f32[320,256]{1,0:T(8,128)S(1)}, u32[]{:S(2)}, u32[]{:S(2)}) collective-permute-start(f32[320,256]{1,0:T(8,128)S(1)} %pad_maximum_fusion.2), channel_id=1, source_target_pairs={{0,192},{16,80},{32,224},{48,112},{64,0},{80,144},{96,32},{112,176... | collective-permute-start | bytes 983048 | tf_op jit(solution)/shard_map/ppermute | solution.py:193
  76.7 3.1 %collective-permute-start.14 = (f32[320,256]{1,0:T(8,128)S(1)}, f32[320,256]{1,0:T(8,128)S(1)}, u32[]{:S(2)}, u32[]{:S(2)}) collective-permute-start(f32[320,256]{1,0:T(8,128)S(1)} %collective-permute-done.12.refs_2_), channel_id=1, source_target_pairs={{0,14},{1,15},{2,0},{3,1},{4,2},{5,3},{6,4},{7,5},{8,6},{9,7},{10,... | collective-permute-start | bytes 983048 | tf_op jit(solution)/shard_map/ppermute | solution.py:185
  79.7 3.4 %collective-permute-start.15 = (f32[320,256]{1,0:T(8,128)S(1)}, f32[320,256]{1,0:T(8,128)S(1)}, u32[]{:S(2)}, u32[]{:S(2)}) collective-permute-start(f32[320,256]{1,0:T(8,128)S(1)} %collective-permute-done.13.refs_3_), channel_id=1, source_target_pairs={{0,2},{1,3},{2,4},{3,5},{4,6},{5,7},{6,8},{7,9},{8,10},{9,11},{10,... | collective-permute-start | bytes 983048 | tf_op jit(solution)/shard_map/ppermute | solution.py:184
  83.2 4.3 %collective-permute-start.26 = (f32[480,256]{1,0:T(8,128)S(1)}, f32[480,256]{1,0:T(8,128)S(1)}, u32[]{:S(2)}, u32[]{:S(2)}) collective-permute-start(f32[480,256]{1,0:T(8,128)S(1)} %pad_maximum_fusion.refs_9_), channel_id=1, source_target_pairs={{0,16},{16,0},{32,48},{48,32},{64,80},{80,64},{96,112},{112,96},{1... | collective-permute-start | bytes 1474568 | tf_op jit(solution)/shard_map/ppermute | solution.py:195
  87.5 4.3 %collective-permute-done.23.refs_8_ = f32[480,256]{1,0:T(8,128)S(1)} collective-permute-done((f32[480,256]{1,0:T(8,128)S(1)}, f32[480,256]{1,0:T(8,128)S(1)}, u32[]{:S(2)}, u32[]{:S(2)}) %collective-permute-start.23) | collective-permute-done | bytes 491552 | tf_op jit(solution)/shard_map/ppermute | solution.py:192
  91.8 8.1 %collective-permute-start.25 = (f32[480,256]{1,0:T(8,128)S(1)}, f32[480,256]{1,0:T(8,128)S(1)}, u32[]{:S(2)}, u32[]{:S(2)}) collective-permute-start(f32[480,256]{1,0:T(8,128)S(1)} %collective-permute-done.23.refs_8_), channel_id=1, source_target_pairs={{0,16},{16,0},{32,48},{48,32},{64,80},{80,64},{96,112},{112,96},{1... | collective-permute-start | bytes 1474568 | tf_op jit(solution)/shard_map/ppermute | solution.py:195
  99.9 1.9 %collective-permute-start.27 = (f32[320,256]{1,0:T(8,128)S(1)}, f32[320,256]{1,0:T(8,128)S(1)}, u32[]{:S(2)}, u32[]{:S(2)}) collective-permute-start(f32[320,256]{1,0:T(8,128)S(1)} %collective-permute-done.24.refs_10_), channel_id=1, source_target_pairs={{0,16},{16,0},{32,48},{48,32},{64,80},{80,64},{96,112},{112,96},{1... | collective-permute-start | bytes 983048 | tf_op jit(solution)/shard_map/ppermute | solution.py:195
  101.8 2.6 %collective-permute-start.16 = (f32[320,256]{1,0:T(8,128)S(1)}, f32[320,256]{1,0:T(8,128)S(1)}, u32[]{:S(2)}, u32[]{:S(2)}) collective-permute-start(f32[320,256]{1,0:T(8,128)S(1)} %collective-permute-done.14.refs_4_), channel_id=1, source_target_pairs={{0,14},{1,15},{2,0},{3,1},{4,2},{5,3},{6,4},{7,5},{8,6},{9,7},{10,... | collective-permute-start | bytes 983048 | tf_op jit(solution)/shard_map/ppermute | solution.py:185
  104.4 3.9 %collective-permute-start.17 = (f32[320,256]{1,0:T(8,128)S(1)}, f32[320,256]{1,0:T(8,128)S(1)}, u32[]{:S(2)}, u32[]{:S(2)}) collective-permute-start(f32[320,256]{1,0:T(8,128)S(1)} %collective-permute-done.15.refs_5_), channel_id=1, source_target_pairs={{0,2},{1,3},{2,4},{3,5},{4,6},{5,7},{6,8},{7,9},{8,10},{9,11},{10,... | collective-permute-start | bytes 983048 | tf_op jit(solution)/shard_map/ppermute | solution.py:187
  108.4 2.5 %collective-permute-done.16.refs_6_ = f32[320,256]{1,0:T(8,128)S(1)} collective-permute-done((f32[320,256]{1,0:T(8,128)S(1)}, f32[320,256]{1,0:T(8,128)S(1)}, u32[]{:S(2)}, u32[]{:S(2)}) %collective-permute-start.16) | collective-permute-done | bytes 327712 | tf_op jit(solution)/shard_map/ppermute | solution.py:185
  110.9 3.5 %collective-permute-done.17.refs_7_ = f32[320,256]{1,0:T(8,128)S(1)} collective-permute-done((f32[320,256]{1,0:T(8,128)S(1)}, f32[320,256]{1,0:T(8,128)S(1)}, u32[]{:S(2)}, u32[]{:S(2)}) %collective-permute-start.17) | collective-permute-done | bytes 327712 | tf_op jit(solution)/shard_map/ppermute | solution.py:187
  114.4 6.7 %shard_map.82 = f32[6,256,256]{2,1,0:T(8,128)} custom-call(s32[85]{0:T(128)S(1)} %concatenate.12.ints, f32[320,256]{1,0:T(8,128)S(1)} %pad_maximum_fusion.1.refs_0_, f32[320,256]{1,0:T(8,128)S(1)} %collective-permute-done.11.refs_1_, f32[320,256]{1,0:T(8,128)S(1)} %collective-permute-done.12.refs_2_, f32[320,256]{1,0:T(8,128)S(1)} %collective-permute-done.13.refs_3_, ...), custom_call_target="tpu_custom_call" | custom-call | tf_op jit(solution)/shard_map/pallas_call | solution.py:148
  (46 shorter events, 5.7 us)
Async XLA Ops:
  0.0 12.8 %copy-start.1 = (s32[1,1,6,2]{2,3,1,0:T(2,128)S(1)}, s32[1,1,6,2]{2,3,1,0:T(2,128)}, u32[]{:S(2)}) copy-start(s32[1,1,6,2]{2,3,1,0:T(2,128)} %param.12) | copy-start | bytes 148
  0.0 13.0 %copy-start = (s32[1,1,3,6,2]{3,4,2,1,0:T(2,128)S(1)}, s32[1,1,3,6,2]{3,4,2,1,0:T(2,128)}, u32[]{:S(2)}) copy-start(s32[1,1,3,6,2]{3,4,2,1,0:T(2,128)} %param.13) | copy-start | bytes 436
  0.0 13.2 %copy-start.2 = (s32[1,1,3]{2,1,0:T(1,128)S(1)}, s32[1,1,3]{2,1,0:T(1,128)}, u32[]{:S(2)}) copy-start(s32[1,1,3]{2,1,0:T(1,128)} %param.14) | copy-start | bytes 40
  0.0 13.2 %copy-start.3 = (s32[32]{0:T(128)S(1)}, s32[32]{0:T(128)}, u32[]{:S(2)}) copy-start(s32[32]{0:T(128)} %constant.17.clone) | copy-start | bytes 388
  1.7 11.6 %collective-permute-start.6 = (f32[160,256]{1,0:T(8,128)S(1)}, f32[160,256]{1,0:T(8,128)S(1)}, u32[]{:S(2)}, u32[]{:S(2)}) collective-permute-start(f32[160,256]{1,0:T(8,128)S(1)} %get-tuple-element.9), channel_id=1, source_target_pairs={{0,1},{1,15},{2,3},{16,17},{17,31},{18,19},{32,33},{33,47},{34,35}... | collective-permute-start | bytes 491528 | tf_op jit(solution)/shard_map/ppermute | solution.py:70
  7.5 12.4 %collective-permute-start.9 = (f32[160,256]{1,0:T(8,128)S(1)}, f32[160,256]{1,0:T(8,128)S(1)}, u32[]{:S(2)}, u32[]{:S(2)}) collective-permute-start(f32[160,256]{1,0:T(8,128)S(1)} %get-tuple-element.10), channel_id=1, source_target_pairs={{0,10},{1,9},{2,8},{16,26},{17,25},{18,24},{32,42},{33,41},{34,40}... | collective-permute-start | bytes 491528 | tf_op jit(solution)/shard_map/ppermute | solution.py:70
  9.5 11.7 %collective-permute-start.8 = (f32[160,256]{1,0:T(8,128)S(1)}, f32[160,256]{1,0:T(8,128)S(1)}, u32[]{:S(2)}, u32[]{:S(2)}) collective-permute-start(f32[160,256]{1,0:T(8,128)S(1)} %get-tuple-element.11), channel_id=1, source_target_pairs={{0,12},{1,7},{2,6},{16,28},{17,23},{18,22},{32,44},{33,39},{34,38}... | collective-permute-start | bytes 491528 | tf_op jit(solution)/shard_map/ppermute | solution.py:70
  10.8 11.7 %collective-permute-start.7 = (f32[160,256]{1,0:T(8,128)S(1)}, f32[160,256]{1,0:T(8,128)S(1)}, u32[]{:S(2)}, u32[]{:S(2)}) collective-permute-start(f32[160,256]{1,0:T(8,128)S(1)} %get-tuple-element.12), channel_id=1, source_target_pairs={{0,14},{1,5},{2,4},{16,30},{17,21},{18,20},{32,46},{33,37},{34,36}... | collective-permute-start | bytes 491528 | tf_op jit(solution)/shard_map/ppermute | solution.py:70
  12.1 15.2 %collective-permute-start.5 = (f32[160,256]{1,0:T(8,128)S(1)}, f32[160,256]{1,0:T(8,128)S(1)}, u32[]{:S(2)}, u32[]{:S(2)}) collective-permute-start(f32[160,256]{1,0:T(8,128)S(1)} %get-tuple-element.13), channel_id=1, source_target_pairs={{1,13},{17,29},{33,45},{49,61},{65,77},{81,93},{97,109},{113,125},... | collective-permute-start | bytes 491528 | tf_op jit(solution)/shard_map/ppermute | solution.py:70
  13.3 16.9 %collective-permute-start = (f32[160,256]{1,0:T(8,128)S(1)}, f32[160,256]{1,0:T(8,128)S(1)}, u32[]{:S(2)}, u32[]{:S(2)}) collective-permute-start(f32[160,256]{1,0:T(8,128)S(1)} %get-tuple-element.19), channel_id=1, source_target_pairs={{16,208},{17,209},{18,210},{19,211},{20,212},{21,213},{22,214},{23... | collective-permute-start | bytes 491528 | tf_op jit(solution)/shard_map/ppermute | solution.py:70
  19.9 16.1 %collective-permute-start.2 = (f32[160,256]{1,0:T(8,128)S(1)}, f32[160,256]{1,0:T(8,128)S(1)}, u32[]{:S(2)}, u32[]{:S(2)}) collective-permute-start(f32[160,256]{1,0:T(8,128)S(1)} %get-tuple-element.20), channel_id=1, source_target_pairs={{0,224},{16,80},{32,64},{1,225},{17,81},{33,65},{2,226},{18,82},{3... | collective-permute-start | bytes 491528 | tf_op jit(solution)/shard_map/ppermute | solution.py:70
  21.2 14.8 %collective-permute-start.3 = (f32[160,256]{1,0:T(8,128)S(1)}, f32[160,256]{1,0:T(8,128)S(1)}, u32[]{:S(2)}, u32[]{:S(2)}) collective-permute-start(f32[160,256]{1,0:T(8,128)S(1)} %get-tuple-element.21), channel_id=1, source_target_pairs={{0,192},{16,112},{32,96},{1,193},{17,113},{33,97},{2,194},{18,114}... | collective-permute-start | bytes 491528 | tf_op jit(solution)/shard_map/ppermute | solution.py:70
  22.5 13.5 %collective-permute-start.4 = (f32[160,256]{1,0:T(8,128)S(1)}, f32[160,256]{1,0:T(8,128)S(1)}, u32[]{:S(2)}, u32[]{:S(2)}) collective-permute-start(f32[160,256]{1,0:T(8,128)S(1)} %get-tuple-element.22), channel_id=1, source_target_pairs={{0,160},{16,144},{32,128},{1,161},{17,145},{33,129},{2,162},{18,14... | collective-permute-start | bytes 491528 | tf_op jit(solution)/shard_map/ppermute | solution.py:70
  27.3 8.8 %collective-permute-start.1 = (f32[160,256]{1,0:T(8,128)S(1)}, f32[160,256]{1,0:T(8,128)S(1)}, u32[]{:S(2)}, u32[]{:S(2)}) collective-permute-start(f32[160,256]{1,0:T(8,128)S(1)} %get-tuple-element.23), channel_id=1, source_target_pairs={{0,16},{16,240},{32,48},{1,17},{17,241},{33,49},{2,18},{18,242},{3... | collective-permute-start | bytes 491528 | tf_op jit(solution)/shard_map/ppermute | solution.py:70
  30.2 16.2 %collective-permute-start.10 = (f32[160,256]{1,0:T(8,128)S(1)}, f32[160,256]{1,0:T(8,128)S(1)}, u32[]{:S(2)}, u32[]{:S(2)}) collective-permute-start(f32[160,256]{1,0:T(8,128)S(1)} %add_select_fusion), channel_id=1, source_target_pairs={{0,1},{1,0},{2,3},{3,2},{4,5},{5,4},{6,7},{7,6},{8,9},{9,8},{10,11... | collective-permute-start | bytes 491528 | tf_op jit(solution)/shard_map/ppermute | solution.py:181
  37.0 17.4 %collective-permute-start.20 = (f32[160,256]{1,0:T(8,128)S(1)}, f32[160,256]{1,0:T(8,128)S(1)}, u32[]{:S(2)}, u32[]{:S(2)}) collective-permute-start(f32[160,256]{1,0:T(8,128)S(1)} %add_select_fusion.1), channel_id=1, source_target_pairs={{0,768},{16,784},{32,800},{48,816},{64,832},{80,848},{96,864},{112... | collective-permute-start | bytes 491528 | tf_op jit(solution)/shard_map/ppermute | solution.py:179
  43.8 10.6 %collective-permute-start.19 = (f32[160,256]{1,0:T(8,128)S(1)}, f32[160,256]{1,0:T(8,128)S(1)}, u32[]{:S(2)}, u32[]{:S(2)}) collective-permute-start(f32[160,256]{1,0:T(8,128)S(1)} %add_select_fusion.1), channel_id=1, source_target_pairs={{0,512},{16,528},{32,544},{48,560},{64,576},{80,592},{96,608},{112... | collective-permute-start | bytes 491528 | tf_op jit(solution)/shard_map/ppermute | solution.py:179
  45.1 9.3 %collective-permute-start.18 = (f32[160,256]{1,0:T(8,128)S(1)}, f32[160,256]{1,0:T(8,128)S(1)}, u32[]{:S(2)}, u32[]{:S(2)}) collective-permute-start(f32[160,256]{1,0:T(8,128)S(1)} %add_select_fusion.1), channel_id=1, source_target_pairs={{0,256},{16,272},{32,288},{48,304},{64,320},{80,336},{96,352},{112... | collective-permute-start | bytes 491528 | tf_op jit(solution)/shard_map/ppermute | solution.py:179
  46.4 24.4 %collective-permute-start.11 = (f32[320,256]{1,0:T(8,128)S(1)}, f32[320,256]{1,0:T(8,128)S(1)}, u32[]{:S(2)}, u32[]{:S(2)}) collective-permute-start(f32[320,256]{1,0:T(8,128)S(1)} %pad_maximum_fusion.1.refs_0_), channel_id=1, source_target_pairs={{0,2},{1,3},{2,4},{3,5},{4,6},{5,7},{6,8},{7,9},{8,10},{9,11},{10,... | collective-permute-start | bytes 983048 | tf_op jit(solution)/shard_map/ppermute | solution.py:184
  54.5 9.8 %collective-permute-start.22 = (f32[160,256]{1,0:T(8,128)S(1)}, f32[160,256]{1,0:T(8,128)S(1)}, u32[]{:S(2)}, u32[]{:S(2)}) collective-permute-start(f32[160,256]{1,0:T(8,128)S(1)} %add_add_fusion), channel_id=1, source_target_pairs={{0,224},{16,48},{32,0},{48,80},{64,32},{80,112},{96,64},{112,144},... | collective-permute-start | bytes 491528 | tf_op jit(solution)/shard_map/ppermute | solution.py:190
  57.8 7.5 %collective-permute-start.21 = (f32[160,256]{1,0:T(8,128)S(1)}, f32[160,256]{1,0:T(8,128)S(1)}, u32[]{:S(2)}, u32[]{:S(2)}) collective-permute-start(f32[160,256]{1,0:T(8,128)S(1)} %add_add_fusion), channel_id=1, source_target_pairs={{0,32},{16,240},{32,64},{48,16},{64,96},{80,48},{96,128},{112,80},... | collective-permute-start | bytes 491528 | tf_op jit(solution)/shard_map/ppermute | solution.py:189
  62.3 14.4 %collective-permute-start.12 = (f32[320,256]{1,0:T(8,128)S(1)}, f32[320,256]{1,0:T(8,128)S(1)}, u32[]{:S(2)}, u32[]{:S(2)}) collective-permute-start(f32[320,256]{1,0:T(8,128)S(1)} %pad_maximum_fusion.1.refs_0_), channel_id=1, source_target_pairs={{0,14},{1,15},{2,0},{3,1},{4,2},{5,3},{6,4},{7,5},{8,6},{9,7},{10,... | collective-permute-start | bytes 983048 | tf_op jit(solution)/shard_map/ppermute | solution.py:185
  65.3 26.4 %collective-permute-start.23 = (f32[480,256]{1,0:T(8,128)S(1)}, f32[480,256]{1,0:T(8,128)S(1)}, u32[]{:S(2)}, u32[]{:S(2)}) collective-permute-start(f32[480,256]{1,0:T(8,128)S(1)} %pad_maximum_fusion.refs_9_), channel_id=1, source_target_pairs={{0,96},{16,176},{32,128},{48,208},{64,160},{80,240},{96,192},{112,... | collective-permute-start | bytes 1474568 | tf_op jit(solution)/shard_map/ppermute | solution.py:192
  70.8 8.9 %collective-permute-start.13 = (f32[320,256]{1,0:T(8,128)S(1)}, f32[320,256]{1,0:T(8,128)S(1)}, u32[]{:S(2)}, u32[]{:S(2)}) collective-permute-start(f32[320,256]{1,0:T(8,128)S(1)} %collective-permute-done.11.refs_1_), channel_id=1, source_target_pairs={{0,2},{1,3},{2,4},{3,5},{4,6},{5,7},{6,8},{7,9},{8,10},{9,11},{10,... | collective-permute-start | bytes 983048 | tf_op jit(solution)/shard_map/ppermute | solution.py:184
  73.6 26.3 %collective-permute-start.24 = (f32[320,256]{1,0:T(8,128)S(1)}, f32[320,256]{1,0:T(8,128)S(1)}, u32[]{:S(2)}, u32[]{:S(2)}) collective-permute-start(f32[320,256]{1,0:T(8,128)S(1)} %pad_maximum_fusion.2), channel_id=1, source_target_pairs={{0,192},{16,80},{32,224},{48,112},{64,0},{80,144},{96,32},{112,176... | collective-permute-start | bytes 983048 | tf_op jit(solution)/shard_map/ppermute | solution.py:193
  76.7 25.2 %collective-permute-start.14 = (f32[320,256]{1,0:T(8,128)S(1)}, f32[320,256]{1,0:T(8,128)S(1)}, u32[]{:S(2)}, u32[]{:S(2)}) collective-permute-start(f32[320,256]{1,0:T(8,128)S(1)} %collective-permute-done.12.refs_2_), channel_id=1, source_target_pairs={{0,14},{1,15},{2,0},{3,1},{4,2},{5,3},{6,4},{7,5},{8,6},{9,7},{10,... | collective-permute-start | bytes 983048 | tf_op jit(solution)/shard_map/ppermute | solution.py:185
  79.7 24.7 %collective-permute-start.15 = (f32[320,256]{1,0:T(8,128)S(1)}, f32[320,256]{1,0:T(8,128)S(1)}, u32[]{:S(2)}, u32[]{:S(2)}) collective-permute-start(f32[320,256]{1,0:T(8,128)S(1)} %collective-permute-done.13.refs_3_), channel_id=1, source_target_pairs={{0,2},{1,3},{2,4},{3,5},{4,6},{5,7},{6,8},{7,9},{8,10},{9,11},{10,... | collective-permute-start | bytes 983048 | tf_op jit(solution)/shard_map/ppermute | solution.py:184
  83.2 25.2 %collective-permute-start.26 = (f32[480,256]{1,0:T(8,128)S(1)}, f32[480,256]{1,0:T(8,128)S(1)}, u32[]{:S(2)}, u32[]{:S(2)}) collective-permute-start(f32[480,256]{1,0:T(8,128)S(1)} %pad_maximum_fusion.refs_9_), channel_id=1, source_target_pairs={{0,16},{16,0},{32,48},{48,32},{64,80},{80,64},{96,112},{112,96},{1... | collective-permute-start | bytes 1474568 | tf_op jit(solution)/shard_map/ppermute | solution.py:195
  91.8 19.1 %collective-permute-start.25 = (f32[480,256]{1,0:T(8,128)S(1)}, f32[480,256]{1,0:T(8,128)S(1)}, u32[]{:S(2)}, u32[]{:S(2)}) collective-permute-start(f32[480,256]{1,0:T(8,128)S(1)} %collective-permute-done.23.refs_8_), channel_id=1, source_target_pairs={{0,16},{16,0},{32,48},{48,32},{64,80},{80,64},{96,112},{112,96},{1... | collective-permute-start | bytes 1474568 | tf_op jit(solution)/shard_map/ppermute | solution.py:195
  99.9 8.5 %collective-permute-start.27 = (f32[320,256]{1,0:T(8,128)S(1)}, f32[320,256]{1,0:T(8,128)S(1)}, u32[]{:S(2)}, u32[]{:S(2)}) collective-permute-start(f32[320,256]{1,0:T(8,128)S(1)} %collective-permute-done.24.refs_10_), channel_id=1, source_target_pairs={{0,16},{16,0},{32,48},{48,32},{64,80},{80,64},{96,112},{112,96},{1... | collective-permute-start | bytes 983048 | tf_op jit(solution)/shard_map/ppermute | solution.py:195
  101.8 9.0 %collective-permute-start.16 = (f32[320,256]{1,0:T(8,128)S(1)}, f32[320,256]{1,0:T(8,128)S(1)}, u32[]{:S(2)}, u32[]{:S(2)}) collective-permute-start(f32[320,256]{1,0:T(8,128)S(1)} %collective-permute-done.14.refs_4_), channel_id=1, source_target_pairs={{0,14},{1,15},{2,0},{3,1},{4,2},{5,3},{6,4},{7,5},{8,6},{9,7},{10,... | collective-permute-start | bytes 983048 | tf_op jit(solution)/shard_map/ppermute | solution.py:185
  104.4 10.0 %collective-permute-start.17 = (f32[320,256]{1,0:T(8,128)S(1)}, f32[320,256]{1,0:T(8,128)S(1)}, u32[]{:S(2)}, u32[]{:S(2)}) collective-permute-start(f32[320,256]{1,0:T(8,128)S(1)} %collective-permute-done.15.refs_5_), channel_id=1, source_target_pairs={{0,2},{1,3},{2,4},{3,5},{4,6},{5,7},{6,8},{7,9},{8,10},{9,11},{10,... | collective-permute-start | bytes 983048 | tf_op jit(solution)/shard_map/ppermute | solution.py:187

commit v3 on v2

--- a/solution.py
+++ b/solution.py
@@ -15,7 +15,7 @@
 
 HOLDERS = (
     ((0, 0), (0, 1), (7, 0), (6, 0), (5, 0)),
-    ((6, 1), (7, 1), (2, 1), (3, 1), (4, 1)),
+    ((7, 1), (6, 1), (2, 1), (3, 1), (4, 1)),
     ((1, 0), (1, 1), (2, 0), (3, 0), (4, 0)),
 )
 HOLDER = tuple(tuple(ring * PAIR + pair for ring, pair in panel) for panel in HOLDERS)
@@ -72,37 +72,32 @@
     return jnp.where(keeps, shards[0], sum(arrived[1:], arrived[0]))
 
 
-def kernel(ints, *refs):
-    a_refs, b_refs = refs[:RING], refs[RING : RING + 6]
-    out, a_sp, b_sp, lists, list_sems = refs[RING + 6 :]
+EARLY_A, EARLY_B = 5, (1, 4)
+
+
+def placements(ints, a_refs, b_refs, a_sp, b_sp):
     col, row = ints[51], ints[52]
     x, z = lax.div(col, 2), lax.rem(col, 2)
     y, core = lax.rem(lax.div(row, 2), RING), lax.rem(row, 2)
-
     places = []
     for half in range(2):
         core_of = core if half == 0 else 1 - core
         way = 1 - 2 * core_of
-        for ref, first, count in zip(b_refs[3 * half : 3 * half + 3], (-4, -1, 2), (3, 3, 2)):
+        for i, (first, count) in enumerate(zip((-4, -1, 2), (3, 3, 2))):
+            at = 3 * half + i
             for part in range(count):
                 origin_y = lax.rem(y + way * (first + part) + 2 * RING, RING)
-                places.append((ref, part, b_sp, origin_y * PAIR + core_of))
+                places.append((b_refs[at], part, b_sp, origin_y * PAIR + core_of, at in EARLY_B))
     way = 1 - 2 * core
-    for ref, shift in zip(a_refs, (0, -1, 1, -2, 2, -3, 3, -4)):
+    for i, shift in enumerate((0, -1, 1, -2, 2, -3, 3, -4)):
         origin_x = lax.rem(x + way * shift + RING, RING)
-        places.append((ref, 0, a_sp, origin_x * PAIR + z))
-        places.append((ref, 1, a_sp, origin_x * PAIR + (1 - z)))
-
-    asked = []
-    for n, (ref, part, dest, origin) in enumerate(places):
-        copy = pltpu.make_async_copy(
-            ref.at[pl.ds(part * SHARD, 8), pl.ds(0, 128)],
-            lists.at[origin + (0 if dest is a_sp else 2 * RING)],
-            list_sems.at[n],
-        )
-        copy.start()
-        asked.append(copy)
-    for ref, part, dest, origin in places:
+        places.append((a_refs[i], 0, a_sp, origin_x * PAIR + z, i < EARLY_A))
+        places.append((a_refs[i], 1, a_sp, origin_x * PAIR + (1 - z), i < EARLY_A))
+    return places
+
+
+def split(ints, places):
+    for ref, part, dest, origin, _ in places:
         value = ref[part * SHARD : (part + 1) * SHARD, :]
         high = value.astype(jnp.bfloat16)
         low = (value - high.astype(jnp.float32)).astype(jnp.bfloat16)
@@ -112,6 +107,32 @@
         dest[head, SIDE:] = low[:LIST]
         dest[rest, :SIDE] = high[LIST:]
         dest[rest, SIDE:] = low[LIST:]
+
+
+def early_kernel(ints, *refs):
+    a_refs = list(refs[:EARLY_A]) + [None] * (RING - EARLY_A)
+    b_refs = [None] * 6
+    for at, ref in zip(EARLY_B, refs[EARLY_A : EARLY_A + len(EARLY_B)]):
+        b_refs[at] = ref
+    places = placements(ints, a_refs, b_refs, *refs[EARLY_A + len(EARLY_B) :])
+    split(ints, [place for place in places if place[4]])
+
+
+def kernel(ints, *refs):
+    a_refs, b_refs = refs[:RING], refs[RING : RING + 6]
+    out, a_sp, b_sp, lists, list_sems = refs[RING + 8 :]
+    places = placements(ints, a_refs, b_refs, a_sp, b_sp)
+
+    asked = []
+    for n, (ref, part, dest, origin, _) in enumerate(places):
+        copy = pltpu.make_async_copy(
+            ref.at[pl.ds(part * SHARD, 8), pl.ds(0, 128)],
+            lists.at[origin + (0 if dest is a_sp else 2 * RING)],
+            list_sems.at[n],
+        )
+        copy.start()
+        asked.append(copy)
+    split(ints, [place for place in places if not place[4]])
     for copy in asked:
         copy.wait()
 
@@ -143,21 +164,31 @@
 
 def multiply(ints, a_blocks, b_blocks):
     local = pl.BlockSpec(memory_space=pltpu.VMEM)
+    scalars = pl.BlockSpec(memory_space=pltpu.SMEM)
+    halves = jax.ShapeDtypeStruct((STEPS * PANEL + SHARD, 2 * SIDE), jnp.bfloat16)
+    early = list(a_blocks[:EARLY_A]) + [b_blocks[at] for at in EARLY_B]
+    a_sp, b_sp = pl.pallas_call(
+        early_kernel,
+        out_shape=(halves, halves),
+        in_specs=[scalars] + [local] * len(early),
+        out_specs=(local, local),
+        compiler_params=pltpu.CompilerParams(vmem_limit_bytes=24 << 20),
+        name="early",
+    )(ints, *early)
     count = len(a_blocks) + len(b_blocks)
-    rows = STEPS * PANEL + SHARD
     return pl.pallas_call(
         kernel,
-        out_shape=jax.ShapeDtypeStruct((RESULTS, SIDE, SIDE), jnp.float32),
-        in_specs=[pl.BlockSpec(memory_space=pltpu.SMEM)] + [local] * count,
-        out_specs=local,
+        out_shape=(jax.ShapeDtypeStruct((RESULTS, SIDE, SIDE), jnp.float32), halves, halves),
+        in_specs=[scalars] + [local] * (count + 2),
+        out_specs=(local, local, local),
+        input_output_aliases={count + 1: 1, count + 2: 2},
         scratch_shapes=[
-            pltpu.VMEM((rows, 2 * SIDE), jnp.bfloat16),
-            pltpu.VMEM((rows, 2 * SIDE), jnp.bfloat16),
             pltpu.SMEM((4 * RING, 8, 128), jnp.float32),
             pltpu.SemaphoreType.DMA((4 * RING,)),
         ],
         compiler_params=pltpu.CompilerParams(vmem_limit_bytes=24 << 20),
-    )(ints, *a_blocks, *b_blocks)
+        name="multiply",
+    )(ints, *a_blocks, *b_blocks, a_sp, b_sp)[0]
 
 
 def program(a_tiles, b_tiles, a_rows, b_cols, c_shape, pairs, pair_count):

time: 122 us -> 122 us (level)
    pallas_call x1 -> x2, Pallas kernels: 6.68 us -> 7.57 us  [the longest x1 6.71 us: multiply(): pl.pallas_call(kernel, out_shape=(jax.ShapeDtypeStruct((RESULTS, SIDE, SI...]
  transfers between devices with their start and end apart: 28 -> 28, of which waited for: 5 -> 5; matrix products, arithmetic and copies ran while one was open for 2% -> 2% of each run, Pallas kernels for 0% -> 1%
where the time goes in v3:
time: 122 us; the launch traced here: 121 us
  starting transfers between devices  92.5 us (76%)
  waiting for transfers between devices  16.3 us (13%)
  Pallas kernels  7.57 us (6%)
  other arithmetic  3.76 us (3%)
    ppermute x10, starting transfers between devices, scatter(): arrived = [lax.ppermute(shards[k], axis, SCATTER[k]) for k in range(SHARDS)]  26.8 us
    ppermute x3, starting transfers between devices, program(): other = [lax.ppermute(part, 'row', SWAP_CORE) for part in mine]  14.2 us
    ppermute x3, starting transfers between devices, program(): lax.ppermute(b_first, 'row', to_plane(z))  9.32 us
    ppermute x3, starting transfers between devices, program(): after = lax.ppermute(after, ('row', 'col'), ring_x(1))  8.58 us
    ppermute x3, starting transfers between devices, program(): before = lax.ppermute(before, ('row', 'col'), ring_x(-1))  7.53 us
    pallas_call x1, Pallas kernels, multiply(): pl.pallas_call(kernel, out_shape=(jax.ShapeDtypeStruct((RESULTS, SIDE, SI...  6.71 us
    ppermute x1, starting transfers between devices, program(): block = jnp.concatenate([a_own, lax.ppermute(a_own, 'col', SWAP_Z)])  5.78 us
    ppermute x3, waiting for transfers between devices, program(): lax.ppermute(b_first, 'row', to_plane(z))  5.62 us
  transfers between devices with their start and end apart: 28, of which 5 were waited for; matrix products, arithmetic and copies ran while one was open for 2% of the time, Pallas kernels for 1%

profile of v3, /device:TPU:1, one launch (start us, length us, event | category | flops | bytes accessed | tf_op | source)
XLA Modules:
  0.0 121.1 jit_solution(1160229497420642008)
XLA Ops:
  0.0 1.7 %fusion = (f32[160,256]{1,0:T(8,128)S(1)}, f32[160,256]{1,0:T(8,128)S(1)}, f32[160,256]{1,0:T(8,128)S(1)}, f32[160,256]{1,0:T(8,128)S(1)}, f32[160,256]{1,0:T(8,...) fusion(f32[768,256]{1,0:T(8,128)} %bitcast.8, ...), kind=kLoop, calls=%fused_computation.9 | loop fusion | flops 163840 | bytes 3276984 | tf_op jit(solution)/shard_map/slice | solution.py:66
  1.7 5.7 %collective-permute-start.6 = (f32[160,256]{1,0:T(8,128)S(1)}, f32[160,256]{1,0:T(8,128)S(1)}, u32[]{:S(2)}, u32[]{:S(2)}) collective-permute-start(f32[160,256]{1,0:T(8,128)S(1)} %get-tuple-element.15), channel_id=1, source_target_pairs={{0,1},{1,13},{2,3},{16,17},{17,29},{18,19},{32,33},{33,45},{34,35}... | collective-permute-start | bytes 491528 | tf_op jit(solution)/shard_map/ppermute | solution.py:70
  7.4 2.0 %collective-permute-start.9 = (f32[160,256]{1,0:T(8,128)S(1)}, f32[160,256]{1,0:T(8,128)S(1)}, u32[]{:S(2)}, u32[]{:S(2)}) collective-permute-start(f32[160,256]{1,0:T(8,128)S(1)} %get-tuple-element.16), channel_id=1, source_target_pairs={{0,10},{1,9},{2,8},{16,26},{17,25},{18,24},{32,42},{33,41},{34,40}... | collective-permute-start | bytes 491528 | tf_op jit(solution)/shard_map/ppermute | solution.py:70
  9.4 1.3 %collective-permute-start.8 = (f32[160,256]{1,0:T(8,128)S(1)}, f32[160,256]{1,0:T(8,128)S(1)}, u32[]{:S(2)}, u32[]{:S(2)}) collective-permute-start(f32[160,256]{1,0:T(8,128)S(1)} %get-tuple-element.17), channel_id=1, source_target_pairs={{0,12},{1,7},{2,6},{16,28},{17,23},{18,22},{32,44},{33,39},{34,38}... | collective-permute-start | bytes 491528 | tf_op jit(solution)/shard_map/ppermute | solution.py:70
  10.8 1.3 %collective-permute-start.7 = (f32[160,256]{1,0:T(8,128)S(1)}, f32[160,256]{1,0:T(8,128)S(1)}, u32[]{:S(2)}, u32[]{:S(2)}) collective-permute-start(f32[160,256]{1,0:T(8,128)S(1)} %get-tuple-element.18), channel_id=1, source_target_pairs={{0,14},{1,5},{2,4},{16,30},{17,21},{18,20},{32,46},{33,37},{34,36}... | collective-permute-start | bytes 491528 | tf_op jit(solution)/shard_map/ppermute | solution.py:70
  13.3 5.9 %collective-permute-start = (f32[160,256]{1,0:T(8,128)S(1)}, f32[160,256]{1,0:T(8,128)S(1)}, u32[]{:S(2)}, u32[]{:S(2)}) collective-permute-start(f32[160,256]{1,0:T(8,128)S(1)} %get-tuple-element.25), channel_id=1, source_target_pairs={{16,240},{17,241},{18,242},{19,243},{20,244},{21,245},{22,246},{23... | collective-permute-start | bytes 491528 | tf_op jit(solution)/shard_map/ppermute | solution.py:70
  19.2 1.3 %collective-permute-start.2 = (f32[160,256]{1,0:T(8,128)S(1)}, f32[160,256]{1,0:T(8,128)S(1)}, u32[]{:S(2)}, u32[]{:S(2)}) collective-permute-start(f32[160,256]{1,0:T(8,128)S(1)} %get-tuple-element.26), channel_id=1, source_target_pairs={{0,224},{16,80},{32,64},{1,225},{17,81},{33,65},{2,226},{18,82},{3... | collective-permute-start | bytes 491528 | tf_op jit(solution)/shard_map/ppermute | solution.py:70
  20.5 1.3 %collective-permute-start.3 = (f32[160,256]{1,0:T(8,128)S(1)}, f32[160,256]{1,0:T(8,128)S(1)}, u32[]{:S(2)}, u32[]{:S(2)}) collective-permute-start(f32[160,256]{1,0:T(8,128)S(1)} %get-tuple-element.27), channel_id=1, source_target_pairs={{0,192},{16,112},{32,96},{1,193},{17,113},{33,97},{2,194},{18,114}... | collective-permute-start | bytes 491528 | tf_op jit(solution)/shard_map/ppermute | solution.py:70
  21.8 5.4 %collective-permute-start.4 = (f32[160,256]{1,0:T(8,128)S(1)}, f32[160,256]{1,0:T(8,128)S(1)}, u32[]{:S(2)}, u32[]{:S(2)}) collective-permute-start(f32[160,256]{1,0:T(8,128)S(1)} %get-tuple-element.28), channel_id=1, source_target_pairs={{0,160},{16,144},{32,128},{1,161},{17,145},{33,129},{2,162},{18,14... | collective-permute-start | bytes 491528 | tf_op jit(solution)/shard_map/ppermute | solution.py:70
  27.2 1.9 %collective-permute-start.1 = (f32[160,256]{1,0:T(8,128)S(1)}, f32[160,256]{1,0:T(8,128)S(1)}, u32[]{:S(2)}, u32[]{:S(2)}) collective-permute-start(f32[160,256]{1,0:T(8,128)S(1)} %get-tuple-element.29), channel_id=1, source_target_pairs={{0,16},{16,208},{32,48},{1,17},{17,209},{33,49},{2,18},{18,210},{3... | collective-permute-start | bytes 491528 | tf_op jit(solution)/shard_map/ppermute | solution.py:70
  30.2 5.8 %collective-permute-start.10 = (f32[160,256]{1,0:T(8,128)S(1)}, f32[160,256]{1,0:T(8,128)S(1)}, u32[]{:S(2)}, u32[]{:S(2)}) collective-permute-start(f32[160,256]{1,0:T(8,128)S(1)} %add_select_fusion), channel_id=1, source_target_pairs={{0,1},{1,0},{2,3},{3,2},{4,5},{5,4},{6,7},{7,6},{8,9},{9,8},{10,11... | collective-permute-start | bytes 491528 | tf_op jit(solution)/shard_map/ppermute | solution.py:212
  37.0 6.7 %collective-permute-start.20 = (f32[160,256]{1,0:T(8,128)S(1)}, f32[160,256]{1,0:T(8,128)S(1)}, u32[]{:S(2)}, u32[]{:S(2)}) collective-permute-start(f32[160,256]{1,0:T(8,128)S(1)} %add_select_fusion.1), channel_id=1, source_target_pairs={{0,768},{16,784},{32,800},{48,816},{64,832},{80,848},{96,864},{112... | collective-permute-start | bytes 491528 | tf_op jit(solution)/shard_map/ppermute | solution.py:210
  45.0 1.3 %collective-permute-start.18 = (f32[160,256]{1,0:T(8,128)S(1)}, f32[160,256]{1,0:T(8,128)S(1)}, u32[]{:S(2)}, u32[]{:S(2)}) collective-permute-start(f32[160,256]{1,0:T(8,128)S(1)} %add_select_fusion.1), channel_id=1, source_target_pairs={{0,256},{16,272},{32,288},{48,304},{64,320},{80,336},{96,352},{112... | collective-permute-start | bytes 491528 | tf_op jit(solution)/shard_map/ppermute | solution.py:210
  46.4 2.4 %collective-permute-start.11 = (f32[320,256]{1,0:T(8,128)S(1)}, f32[320,256]{1,0:T(8,128)S(1)}, u32[]{:S(2)}, u32[]{:S(2)}) collective-permute-start(f32[320,256]{1,0:T(8,128)S(1)} %pad_maximum_fusion.1.refs_0_), channel_id=1, source_target_pairs={{0,2},{1,3},{2,4},{3,5},{4,6},{5,7},{6,8},{7,9},{8,10},{9,11},{10,... | collective-permute-start | bytes 983048 | tf_op jit(solution)/shard_map/ppermute | solution.py:215
  48.8 5.6 %collective-permute-done.20 = f32[160,256]{1,0:T(8,128)S(1)} collective-permute-done((f32[160,256]{1,0:T(8,128)S(1)}, f32[160,256]{1,0:T(8,128)S(1)}, u32[]{:S(2)}, u32[]{:S(2)}) %collective-permute-start.20) | collective-permute-done | bytes 163872 | tf_op jit(solution)/shard_map/ppermute | solution.py:210
  54.4 3.3 %collective-permute-start.22 = (f32[160,256]{1,0:T(8,128)S(1)}, f32[160,256]{1,0:T(8,128)S(1)}, u32[]{:S(2)}, u32[]{:S(2)}) collective-permute-start(f32[160,256]{1,0:T(8,128)S(1)} %add_add_fusion), channel_id=1, source_target_pairs={{0,224},{16,48},{32,0},{48,80},{64,32},{80,112},{96,64},{112,144},... | collective-permute-start | bytes 491528 | tf_op jit(solution)/shard_map/ppermute | solution.py:221
  57.8 4.5 %collective-permute-start.21 = (f32[160,256]{1,0:T(8,128)S(1)}, f32[160,256]{1,0:T(8,128)S(1)}, u32[]{:S(2)}, u32[]{:S(2)}) collective-permute-start(f32[160,256]{1,0:T(8,128)S(1)} %add_add_fusion), channel_id=1, source_target_pairs={{0,32},{16,240},{32,64},{48,16},{64,96},{80,48},{96,128},{112,80},... | collective-permute-start | bytes 491528 | tf_op jit(solution)/shard_map/ppermute | solution.py:220
  62.3 1.9 %collective-permute-start.12 = (f32[320,256]{1,0:T(8,128)S(1)}, f32[320,256]{1,0:T(8,128)S(1)}, u32[]{:S(2)}, u32[]{:S(2)}) collective-permute-start(f32[320,256]{1,0:T(8,128)S(1)} %pad_maximum_fusion.1.refs_0_), channel_id=1, source_target_pairs={{0,14},{1,15},{2,0},{3,1},{4,2},{5,3},{6,4},{7,5},{8,6},{9,7},{10,... | collective-permute-start | bytes 983048 | tf_op jit(solution)/shard_map/ppermute | solution.py:216
  65.3 5.5 %collective-permute-start.23 = (f32[480,256]{1,0:T(8,128)S(1)}, f32[480,256]{1,0:T(8,128)S(1)}, u32[]{:S(2)}, u32[]{:S(2)}) collective-permute-start(f32[480,256]{1,0:T(8,128)S(1)} %pad_maximum_fusion.refs_5_.refs_9_), channel_id=1, source_target_pairs={{0,96},{16,176},{32,128},{48,208},{64,160},{80,240},{96,192},{112,... | collective-permute-start | bytes 1474568 | tf_op jit(solution)/shard_map/ppermute | solution.py:223
  70.8 2.8 %collective-permute-start.13 = (f32[320,256]{1,0:T(8,128)S(1)}, f32[320,256]{1,0:T(8,128)S(1)}, u32[]{:S(2)}, u32[]{:S(2)}) collective-permute-start(f32[320,256]{1,0:T(8,128)S(1)} %collective-permute-done.11.refs_1_), channel_id=1, source_target_pairs={{0,2},{1,3},{2,4},{3,5},{4,6},{5,7},{6,8},{7,9},{8,10},{9,11},{10,... | collective-permute-start | bytes 983048 | tf_op jit(solution)/shard_map/ppermute | solution.py:215
  73.6 3.1 %collective-permute-start.24 = (f32[320,256]{1,0:T(8,128)S(1)}, f32[320,256]{1,0:T(8,128)S(1)}, u32[]{:S(2)}, u32[]{:S(2)}) collective-permute-start(f32[320,256]{1,0:T(8,128)S(1)} %pad_maximum_fusion.2), channel_id=1, source_target_pairs={{0,192},{16,80},{32,224},{48,112},{64,0},{80,144},{96,32},{112,176... | collective-permute-start | bytes 983048 | tf_op jit(solution)/shard_map/ppermute | solution.py:224
  76.7 3.0 %collective-permute-start.14 = (f32[320,256]{1,0:T(8,128)S(1)}, f32[320,256]{1,0:T(8,128)S(1)}, u32[]{:S(2)}, u32[]{:S(2)}) collective-permute-start(f32[320,256]{1,0:T(8,128)S(1)} %collective-permute-done.12.refs_2_), channel_id=1, source_target_pairs={{0,14},{1,15},{2,0},{3,1},{4,2},{5,3},{6,4},{7,5},{8,6},{9,7},{10,... | collective-permute-start | bytes 983048 | tf_op jit(solution)/shard_map/ppermute | solution.py:216
  79.7 3.5 %collective-permute-start.15 = (f32[320,256]{1,0:T(8,128)S(1)}, f32[320,256]{1,0:T(8,128)S(1)}, u32[]{:S(2)}, u32[]{:S(2)}) collective-permute-start(f32[320,256]{1,0:T(8,128)S(1)} %collective-permute-done.13.refs_3_), channel_id=1, source_target_pairs={{0,2},{1,3},{2,4},{3,5},{4,6},{5,7},{6,8},{7,9},{8,10},{9,11},{10,... | collective-permute-start | bytes 983048 | tf_op jit(solution)/shard_map/ppermute | solution.py:215
  83.2 4.3 %collective-permute-start.26 = (f32[480,256]{1,0:T(8,128)S(1)}, f32[480,256]{1,0:T(8,128)S(1)}, u32[]{:S(2)}, u32[]{:S(2)}) collective-permute-start(f32[480,256]{1,0:T(8,128)S(1)} %pad_maximum_fusion.refs_5_.refs_9_), channel_id=1, source_target_pairs={{0,16},{16,0},{32,48},{48,32},{64,80},{80,64},{96,112},{112,96},{1... | collective-permute-start | bytes 1474568 | tf_op jit(solution)/shard_map/ppermute | solution.py:226
  87.5 4.4 %collective-permute-done.23.refs_8_ = f32[480,256]{1,0:T(8,128)S(1)} collective-permute-done((f32[480,256]{1,0:T(8,128)S(1)}, f32[480,256]{1,0:T(8,128)S(1)}, u32[]{:S(2)}, u32[]{:S(2)}) %collective-permute-start.23) | collective-permute-done | bytes 491552 | tf_op jit(solution)/shard_map/ppermute | solution.py:223
  91.8 8.1 %collective-permute-start.25 = (f32[480,256]{1,0:T(8,128)S(1)}, f32[480,256]{1,0:T(8,128)S(1)}, u32[]{:S(2)}, u32[]{:S(2)}) collective-permute-start(f32[480,256]{1,0:T(8,128)S(1)} %collective-permute-done.23.refs_8_), channel_id=1, source_target_pairs={{0,16},{16,0},{32,48},{48,32},{64,80},{80,64},{96,112},{112,96},{1... | collective-permute-start | bytes 1474568 | tf_op jit(solution)/shard_map/ppermute | solution.py:226
  99.9 1.9 %collective-permute-start.27 = (f32[320,256]{1,0:T(8,128)S(1)}, f32[320,256]{1,0:T(8,128)S(1)}, u32[]{:S(2)}, u32[]{:S(2)}) collective-permute-start(f32[320,256]{1,0:T(8,128)S(1)} %collective-permute-done.24.refs_10_), channel_id=1, source_target_pairs={{0,16},{16,0},{32,48},{48,32},{64,80},{80,64},{96,112},{112,96},{1... | collective-permute-start | bytes 983048 | tf_op jit(solution)/shard_map/ppermute | solution.py:226
  101.8 2.6 %collective-permute-start.16 = (f32[320,256]{1,0:T(8,128)S(1)}, f32[320,256]{1,0:T(8,128)S(1)}, u32[]{:S(2)}, u32[]{:S(2)}) collective-permute-start(f32[320,256]{1,0:T(8,128)S(1)} %collective-permute-done.14.refs_4_), channel_id=1, source_target_pairs={{0,14},{1,15},{2,0},{3,1},{4,2},{5,3},{6,4},{7,5},{8,6},{9,7},{10,... | collective-permute-start | bytes 983048 | tf_op jit(solution)/shard_map/ppermute | solution.py:216
  104.4 3.9 %collective-permute-start.17 = (f32[320,256]{1,0:T(8,128)S(1)}, f32[320,256]{1,0:T(8,128)S(1)}, u32[]{:S(2)}, u32[]{:S(2)}) collective-permute-start(f32[320,256]{1,0:T(8,128)S(1)} %collective-permute-done.15.refs_5_), channel_id=1, source_target_pairs={{0,2},{1,3},{2,4},{3,5},{4,6},{5,7},{6,8},{7,9},{8,10},{9,11},{10,... | collective-permute-start | bytes 983048 | tf_op jit(solution)/shard_map/ppermute | solution.py:218
  109.2 1.6 %collective-permute-done.16.refs_6_ = f32[320,256]{1,0:T(8,128)S(1)} collective-permute-done((f32[320,256]{1,0:T(8,128)S(1)}, f32[320,256]{1,0:T(8,128)S(1)}, u32[]{:S(2)}, u32[]{:S(2)}) %collective-permute-start.16) | collective-permute-done | bytes 327712 | tf_op jit(solution)/shard_map/ppermute | solution.py:216
  110.9 3.5 %collective-permute-done.17.refs_7_ = f32[320,256]{1,0:T(8,128)S(1)} collective-permute-done((f32[320,256]{1,0:T(8,128)S(1)}, f32[320,256]{1,0:T(8,128)S(1)}, u32[]{:S(2)}, u32[]{:S(2)}) %collective-permute-start.17) | collective-permute-done | bytes 327712 | tf_op jit(solution)/shard_map/ppermute | solution.py:218
  114.4 6.7 %multiply.1 = (f32[6,256,256]{2,1,0:T(8,128)}, bf16[2464,512]{1,0:T(8,128)(2,1)S(1)}, bf16[2464,512]{1,0:T(8,128)(2,1)S(1)}) custom-call(s32[85]{0:T(128)S(1)} %concatenate.12.ints, f32[320,256]{1,0:T(8,128)S(1)} %pad_maximum_fusion.1.refs_0_, f32[320,256]{1,0:T(8,128)S(1)} %collective-permute-done.11.refs_1_, ...), custom_call_target="tpu_custom_call", output_to_operand_aliasing={{1}: (15, {}), {2}: (16, {})} | custom-call | tf_op jit(solution)/shard_map/multiply/pallas_call | solution.py:179
  (47 shorter events, 6.6 us)
Async XLA Ops:
  0.0 13.2 %copy-start.3 = (s32[32]{0:T(128)S(1)}, s32[32]{0:T(128)}, u32[]{:S(2)}) copy-start(s32[32]{0:T(128)} %constant.17.clone) | copy-start | bytes 388
  0.0 12.8 %copy-start.1 = (s32[1,1,6,2]{2,3,1,0:T(2,128)S(1)}, s32[1,1,6,2]{2,3,1,0:T(2,128)}, u32[]{:S(2)}) copy-start(s32[1,1,6,2]{2,3,1,0:T(2,128)} %param.12) | copy-start | bytes 148
  0.0 12.9 %copy-start = (s32[1,1,3,6,2]{3,4,2,1,0:T(2,128)S(1)}, s32[1,1,3,6,2]{3,4,2,1,0:T(2,128)}, u32[]{:S(2)}) copy-start(s32[1,1,3,6,2]{3,4,2,1,0:T(2,128)} %param.13) | copy-start | bytes 436
  0.0 13.2 %copy-start.2 = (s32[1,1,3]{2,1,0:T(1,128)S(1)}, s32[1,1,3]{2,1,0:T(1,128)}, u32[]{:S(2)}) copy-start(s32[1,1,3]{2,1,0:T(1,128)} %param.14) | copy-start | bytes 40
  1.7 11.6 %collective-permute-start.6 = (f32[160,256]{1,0:T(8,128)S(1)}, f32[160,256]{1,0:T(8,128)S(1)}, u32[]{:S(2)}, u32[]{:S(2)}) collective-permute-start(f32[160,256]{1,0:T(8,128)S(1)} %get-tuple-element.15), channel_id=1, source_target_pairs={{0,1},{1,13},{2,3},{16,17},{17,29},{18,19},{32,33},{33,45},{34,35}... | collective-permute-start | bytes 491528 | tf_op jit(solution)/shard_map/ppermute | solution.py:70
  7.4 11.7 %collective-permute-start.9 = (f32[160,256]{1,0:T(8,128)S(1)}, f32[160,256]{1,0:T(8,128)S(1)}, u32[]{:S(2)}, u32[]{:S(2)}) collective-permute-start(f32[160,256]{1,0:T(8,128)S(1)} %get-tuple-element.16), channel_id=1, source_target_pairs={{0,10},{1,9},{2,8},{16,26},{17,25},{18,24},{32,42},{33,41},{34,40}... | collective-permute-start | bytes 491528 | tf_op jit(solution)/shard_map/ppermute | solution.py:70
  9.4 11.0 %collective-permute-start.8 = (f32[160,256]{1,0:T(8,128)S(1)}, f32[160,256]{1,0:T(8,128)S(1)}, u32[]{:S(2)}, u32[]{:S(2)}) collective-permute-start(f32[160,256]{1,0:T(8,128)S(1)} %get-tuple-element.17), channel_id=1, source_target_pairs={{0,12},{1,7},{2,6},{16,28},{17,23},{18,22},{32,44},{33,39},{34,38}... | collective-permute-start | bytes 491528 | tf_op jit(solution)/shard_map/ppermute | solution.py:70
  10.8 11.0 %collective-permute-start.7 = (f32[160,256]{1,0:T(8,128)S(1)}, f32[160,256]{1,0:T(8,128)S(1)}, u32[]{:S(2)}, u32[]{:S(2)}) collective-permute-start(f32[160,256]{1,0:T(8,128)S(1)} %get-tuple-element.18), channel_id=1, source_target_pairs={{0,14},{1,5},{2,4},{16,30},{17,21},{18,20},{32,46},{33,37},{34,36}... | collective-permute-start | bytes 491528 | tf_op jit(solution)/shard_map/ppermute | solution.py:70
  12.1 15.2 %collective-permute-start.5 = (f32[160,256]{1,0:T(8,128)S(1)}, f32[160,256]{1,0:T(8,128)S(1)}, u32[]{:S(2)}, u32[]{:S(2)}) collective-permute-start(f32[160,256]{1,0:T(8,128)S(1)} %get-tuple-element.19), channel_id=1, source_target_pairs={{1,15},{17,31},{33,47},{49,63},{65,79},{81,95},{97,111},{113,127},... | collective-permute-start | bytes 491528 | tf_op jit(solution)/shard_map/ppermute | solution.py:70
  13.3 16.9 %collective-permute-start = (f32[160,256]{1,0:T(8,128)S(1)}, f32[160,256]{1,0:T(8,128)S(1)}, u32[]{:S(2)}, u32[]{:S(2)}) collective-permute-start(f32[160,256]{1,0:T(8,128)S(1)} %get-tuple-element.25), channel_id=1, source_target_pairs={{16,240},{17,241},{18,242},{19,243},{20,244},{21,245},{22,246},{23... | collective-permute-start | bytes 491528 | tf_op jit(solution)/shard_map/ppermute | solution.py:70
  19.2 16.8 %collective-permute-start.2 = (f32[160,256]{1,0:T(8,128)S(1)}, f32[160,256]{1,0:T(8,128)S(1)}, u32[]{:S(2)}, u32[]{:S(2)}) collective-permute-start(f32[160,256]{1,0:T(8,128)S(1)} %get-tuple-element.26), channel_id=1, source_target_pairs={{0,224},{16,80},{32,64},{1,225},{17,81},{33,65},{2,226},{18,82},{3... | collective-permute-start | bytes 491528 | tf_op jit(solution)/shard_map/ppermute | solution.py:70
  20.5 15.5 %collective-permute-start.3 = (f32[160,256]{1,0:T(8,128)S(1)}, f32[160,256]{1,0:T(8,128)S(1)}, u32[]{:S(2)}, u32[]{:S(2)}) collective-permute-start(f32[160,256]{1,0:T(8,128)S(1)} %get-tuple-element.27), channel_id=1, source_target_pairs={{0,192},{16,112},{32,96},{1,193},{17,113},{33,97},{2,194},{18,114}... | collective-permute-start | bytes 491528 | tf_op jit(solution)/shard_map/ppermute | solution.py:70
  21.8 14.2 %collective-permute-start.4 = (f32[160,256]{1,0:T(8,128)S(1)}, f32[160,256]{1,0:T(8,128)S(1)}, u32[]{:S(2)}, u32[]{:S(2)}) collective-permute-start(f32[160,256]{1,0:T(8,128)S(1)} %get-tuple-element.28), channel_id=1, source_target_pairs={{0,160},{16,144},{32,128},{1,161},{17,145},{33,129},{2,162},{18,14... | collective-permute-start | bytes 491528 | tf_op jit(solution)/shard_map/ppermute | solution.py:70
  27.2 8.8 %collective-permute-start.1 = (f32[160,256]{1,0:T(8,128)S(1)}, f32[160,256]{1,0:T(8,128)S(1)}, u32[]{:S(2)}, u32[]{:S(2)}) collective-permute-start(f32[160,256]{1,0:T(8,128)S(1)} %get-tuple-element.29), channel_id=1, source_target_pairs={{0,16},{16,208},{32,48},{1,17},{17,209},{33,49},{2,18},{18,210},{3... | collective-permute-start | bytes 491528 | tf_op jit(solution)/shard_map/ppermute | solution.py:70
  30.2 16.2 %collective-permute-start.10 = (f32[160,256]{1,0:T(8,128)S(1)}, f32[160,256]{1,0:T(8,128)S(1)}, u32[]{:S(2)}, u32[]{:S(2)}) collective-permute-start(f32[160,256]{1,0:T(8,128)S(1)} %add_select_fusion), channel_id=1, source_target_pairs={{0,1},{1,0},{2,3},{3,2},{4,5},{5,4},{6,7},{7,6},{8,9},{9,8},{10,11... | collective-permute-start | bytes 491528 | tf_op jit(solution)/shard_map/ppermute | solution.py:212
  37.0 17.4 %collective-permute-start.20 = (f32[160,256]{1,0:T(8,128)S(1)}, f32[160,256]{1,0:T(8,128)S(1)}, u32[]{:S(2)}, u32[]{:S(2)}) collective-permute-start(f32[160,256]{1,0:T(8,128)S(1)} %add_select_fusion.1), channel_id=1, source_target_pairs={{0,768},{16,784},{32,800},{48,816},{64,832},{80,848},{96,864},{112... | collective-permute-start | bytes 491528 | tf_op jit(solution)/shard_map/ppermute | solution.py:210
  43.7 10.6 %collective-permute-start.19 = (f32[160,256]{1,0:T(8,128)S(1)}, f32[160,256]{1,0:T(8,128)S(1)}, u32[]{:S(2)}, u32[]{:S(2)}) collective-permute-start(f32[160,256]{1,0:T(8,128)S(1)} %add_select_fusion.1), channel_id=1, source_target_pairs={{0,512},{16,528},{32,544},{48,560},{64,576},{80,592},{96,608},{112... | collective-permute-start | bytes 491528 | tf_op jit(solution)/shard_map/ppermute | solution.py:210
  45.0 9.3 %collective-permute-start.18 = (f32[160,256]{1,0:T(8,128)S(1)}, f32[160,256]{1,0:T(8,128)S(1)}, u32[]{:S(2)}, u32[]{:S(2)}) collective-permute-start(f32[160,256]{1,0:T(8,128)S(1)} %add_select_fusion.1), channel_id=1, source_target_pairs={{0,256},{16,272},{32,288},{48,304},{64,320},{80,336},{96,352},{112... | collective-permute-start | bytes 491528 | tf_op jit(solution)/shard_map/ppermute | solution.py:210
  46.4 24.4 %collective-permute-start.11 = (f32[320,256]{1,0:T(8,128)S(1)}, f32[320,256]{1,0:T(8,128)S(1)}, u32[]{:S(2)}, u32[]{:S(2)}) collective-permute-start(f32[320,256]{1,0:T(8,128)S(1)} %pad_maximum_fusion.1.refs_0_), channel_id=1, source_target_pairs={{0,2},{1,3},{2,4},{3,5},{4,6},{5,7},{6,8},{7,9},{8,10},{9,11},{10,... | collective-permute-start | bytes 983048 | tf_op jit(solution)/shard_map/ppermute | solution.py:215
  54.4 9.8 %collective-permute-start.22 = (f32[160,256]{1,0:T(8,128)S(1)}, f32[160,256]{1,0:T(8,128)S(1)}, u32[]{:S(2)}, u32[]{:S(2)}) collective-permute-start(f32[160,256]{1,0:T(8,128)S(1)} %add_add_fusion), channel_id=1, source_target_pairs={{0,224},{16,48},{32,0},{48,80},{64,32},{80,112},{96,64},{112,144},... | collective-permute-start | bytes 491528 | tf_op jit(solution)/shard_map/ppermute | solution.py:221
  57.8 7.5 %collective-permute-start.21 = (f32[160,256]{1,0:T(8,128)S(1)}, f32[160,256]{1,0:T(8,128)S(1)}, u32[]{:S(2)}, u32[]{:S(2)}) collective-permute-start(f32[160,256]{1,0:T(8,128)S(1)} %add_add_fusion), channel_id=1, source_target_pairs={{0,32},{16,240},{32,64},{48,16},{64,96},{80,48},{96,128},{112,80},... | collective-permute-start | bytes 491528 | tf_op jit(solution)/shard_map/ppermute | solution.py:220
  62.3 14.4 %collective-permute-start.12 = (f32[320,256]{1,0:T(8,128)S(1)}, f32[320,256]{1,0:T(8,128)S(1)}, u32[]{:S(2)}, u32[]{:S(2)}) collective-permute-start(f32[320,256]{1,0:T(8,128)S(1)} %pad_maximum_fusion.1.refs_0_), channel_id=1, source_target_pairs={{0,14},{1,15},{2,0},{3,1},{4,2},{5,3},{6,4},{7,5},{8,6},{9,7},{10,... | collective-permute-start | bytes 983048 | tf_op jit(solution)/shard_map/ppermute | solution.py:216
  65.3 26.5 %collective-permute-start.23 = (f32[480,256]{1,0:T(8,128)S(1)}, f32[480,256]{1,0:T(8,128)S(1)}, u32[]{:S(2)}, u32[]{:S(2)}) collective-permute-start(f32[480,256]{1,0:T(8,128)S(1)} %pad_maximum_fusion.refs_5_.refs_9_), channel_id=1, source_target_pairs={{0,96},{16,176},{32,128},{48,208},{64,160},{80,240},{96,192},{112,... | collective-permute-start | bytes 1474568 | tf_op jit(solution)/shard_map/ppermute | solution.py:223
  70.8 8.9 %collective-permute-start.13 = (f32[320,256]{1,0:T(8,128)S(1)}, f32[320,256]{1,0:T(8,128)S(1)}, u32[]{:S(2)}, u32[]{:S(2)}) collective-permute-start(f32[320,256]{1,0:T(8,128)S(1)} %collective-permute-done.11.refs_1_), channel_id=1, source_target_pairs={{0,2},{1,3},{2,4},{3,5},{4,6},{5,7},{6,8},{7,9},{8,10},{9,11},{10,... | collective-permute-start | bytes 983048 | tf_op jit(solution)/shard_map/ppermute | solution.py:215
  73.6 26.3 %collective-permute-start.24 = (f32[320,256]{1,0:T(8,128)S(1)}, f32[320,256]{1,0:T(8,128)S(1)}, u32[]{:S(2)}, u32[]{:S(2)}) collective-permute-start(f32[320,256]{1,0:T(8,128)S(1)} %pad_maximum_fusion.2), channel_id=1, source_target_pairs={{0,192},{16,80},{32,224},{48,112},{64,0},{80,144},{96,32},{112,176... | collective-permute-start | bytes 983048 | tf_op jit(solution)/shard_map/ppermute | solution.py:224
  76.7 25.2 %collective-permute-start.14 = (f32[320,256]{1,0:T(8,128)S(1)}, f32[320,256]{1,0:T(8,128)S(1)}, u32[]{:S(2)}, u32[]{:S(2)}) collective-permute-start(f32[320,256]{1,0:T(8,128)S(1)} %collective-permute-done.12.refs_2_), channel_id=1, source_target_pairs={{0,14},{1,15},{2,0},{3,1},{4,2},{5,3},{6,4},{7,5},{8,6},{9,7},{10,... | collective-permute-start | bytes 983048 | tf_op jit(solution)/shard_map/ppermute | solution.py:216
  79.7 24.7 %collective-permute-start.15 = (f32[320,256]{1,0:T(8,128)S(1)}, f32[320,256]{1,0:T(8,128)S(1)}, u32[]{:S(2)}, u32[]{:S(2)}) collective-permute-start(f32[320,256]{1,0:T(8,128)S(1)} %collective-permute-done.13.refs_3_), channel_id=1, source_target_pairs={{0,2},{1,3},{2,4},{3,5},{4,6},{5,7},{6,8},{7,9},{8,10},{9,11},{10,... | collective-permute-start | bytes 983048 | tf_op jit(solution)/shard_map/ppermute | solution.py:215
  83.2 25.2 %collective-permute-start.26 = (f32[480,256]{1,0:T(8,128)S(1)}, f32[480,256]{1,0:T(8,128)S(1)}, u32[]{:S(2)}, u32[]{:S(2)}) collective-permute-start(f32[480,256]{1,0:T(8,128)S(1)} %pad_maximum_fusion.refs_5_.refs_9_), channel_id=1, source_target_pairs={{0,16},{16,0},{32,48},{48,32},{64,80},{80,64},{96,112},{112,96},{1... | collective-permute-start | bytes 1474568 | tf_op jit(solution)/shard_map/ppermute | solution.py:226
  91.8 19.0 %collective-permute-start.25 = (f32[480,256]{1,0:T(8,128)S(1)}, f32[480,256]{1,0:T(8,128)S(1)}, u32[]{:S(2)}, u32[]{:S(2)}) collective-permute-start(f32[480,256]{1,0:T(8,128)S(1)} %collective-permute-done.23.refs_8_), channel_id=1, source_target_pairs={{0,16},{16,0},{32,48},{48,32},{64,80},{80,64},{96,112},{112,96},{1... | collective-permute-start | bytes 1474568 | tf_op jit(solution)/shard_map/ppermute | solution.py:226
  99.9 9.3 %collective-permute-start.27 = (f32[320,256]{1,0:T(8,128)S(1)}, f32[320,256]{1,0:T(8,128)S(1)}, u32[]{:S(2)}, u32[]{:S(2)}) collective-permute-start(f32[320,256]{1,0:T(8,128)S(1)} %collective-permute-done.24.refs_10_), channel_id=1, source_target_pairs={{0,16},{16,0},{32,48},{48,32},{64,80},{80,64},{96,112},{112,96},{1... | collective-permute-start | bytes 983048 | tf_op jit(solution)/shard_map/ppermute | solution.py:226
  101.8 9.0 %collective-permute-start.16 = (f32[320,256]{1,0:T(8,128)S(1)}, f32[320,256]{1,0:T(8,128)S(1)}, u32[]{:S(2)}, u32[]{:S(2)}) collective-permute-start(f32[320,256]{1,0:T(8,128)S(1)} %collective-permute-done.14.refs_4_), channel_id=1, source_target_pairs={{0,14},{1,15},{2,0},{3,1},{4,2},{5,3},{6,4},{7,5},{8,6},{9,7},{10,... | collective-permute-start | bytes 983048 | tf_op jit(solution)/shard_map/ppermute | solution.py:216
  104.4 10.0 %collective-permute-start.17 = (f32[320,256]{1,0:T(8,128)S(1)}, f32[320,256]{1,0:T(8,128)S(1)}, u32[]{:S(2)}, u32[]{:S(2)}) collective-permute-start(f32[320,256]{1,0:T(8,128)S(1)} %collective-permute-done.15.refs_5_), channel_id=1, source_target_pairs={{0,2},{1,3},{2,4},{3,5},{4,6},{5,7},{6,8},{7,9},{8,10},{9,11},{10,... | collective-permute-start | bytes 983048 | tf_op jit(solution)/shard_map/ppermute | solution.py:218

commit v4 on v3

--- a/solution.py
+++ b/solution.py
@@ -120,36 +120,40 @@
 
 def kernel(ints, *refs):
     a_refs, b_refs = refs[:RING], refs[RING : RING + 6]
-    out, a_sp, b_sp, lists, list_sems = refs[RING + 8 :]
+    out, a_sp, b_sp, lists, live, sized, list_sem = refs[RING + 8 :]
     places = placements(ints, a_refs, b_refs, a_sp, b_sp)
 
-    asked = []
-    for n, (ref, part, dest, origin, _) in enumerate(places):
-        copy = pltpu.make_async_copy(
+    for ref, part, dest, origin, _ in places:
+        pltpu.make_async_copy(
             ref.at[pl.ds(part * SHARD, 8), pl.ds(0, 128)],
             lists.at[origin + (0 if dest is a_sp else 2 * RING)],
-            list_sems.at[n],
-        )
-        copy.start()
-        asked.append(copy)
+            list_sem,
+        ).start()
     split(ints, [place for place in places if not place[4]])
-    for copy in asked:
-        copy.wait()
+    for at in range(STEPS * SLOTS * SLOTS):
+        live[at] = 0.0
+    for s in range(STEPS):
+        for p in range(RESULTS):
+            at = 12 + (s * RESULTS + p) * 2
+            cell = s * SLOTS * SLOTS + ints[at] * SLOTS + ints[at + 1]
+            live[cell] = jnp.where(p < ints[48 + s], 1.0, live[cell])
+
+    pltpu.make_async_copy(sized, lists, list_sem).wait()
+    known_rows, known_cols = [], []
+    for s in range(STEPS):
+        last = HOLDER[s][SHARDS - 1]
+        known_rows.append([lists[last, 0, t].astype(jnp.int32) for t in range(1, SLOTS)])
+        known_cols.append([lists[2 * RING + last, 0, t].astype(jnp.int32) for t in range(1, SLOTS)])
 
     for l in range(RESULTS):
         c_row, c_col = ints[2 * l], ints[2 * l + 1]
         total = None
         for s in range(STEPS):
-            last = HOLDER[s][SHARDS - 1]
             i, j = jnp.int32(0), jnp.int32(0)
-            for t in range(SLOTS):
-                i = jnp.where(lists[last, 0, t].astype(jnp.int32) == c_row, t, i)
-                j = jnp.where(lists[2 * RING + last, 0, t].astype(jnp.int32) == c_col, t, j)
-            live = jnp.int32(0)
-            for p in range(RESULTS):
-                at = 12 + (s * RESULTS + p) * 2
-                hit = (ints[at] == i) & (ints[at + 1] == j) & (p < ints[48 + s])
-                live = jnp.where(hit, 1, live)
+            for t in range(1, SLOTS):
+                i = jnp.where(known_rows[s][t - 1] == c_row, t, i)
+                j = jnp.where(known_cols[s][t - 1] == c_col, t, j)
+            weight = live[s * SLOTS * SLOTS + i * SLOTS + j]
             ia = pl.ds(pl.multiple_of(s * PANEL + i * SIDE, 32), SIDE)
             jb = pl.ds(pl.multiple_of(s * PANEL + j * SIDE, 32), SIDE)
             product = (
@@ -157,7 +161,7 @@
                 + jnp.dot(a_sp[ia, :SIDE], b_sp[jb, SIDE:], preferred_element_type=jnp.float32)
                 + jnp.dot(a_sp[ia, SIDE:], b_sp[jb, :SIDE], preferred_element_type=jnp.float32)
             )
-            product = product * live.astype(jnp.float32)
+            product = product * weight
             total = product if total is None else total + product
         out[l] = total
 
@@ -184,7 +188,9 @@
         input_output_aliases={count + 1: 1, count + 2: 2},
         scratch_shapes=[
             pltpu.SMEM((4 * RING, 8, 128), jnp.float32),
-            pltpu.SemaphoreType.DMA((4 * RING,)),
+            pltpu.SMEM((STEPS * SLOTS * SLOTS,), jnp.float32),
+            pltpu.VMEM((4 * RING, 8, 128), jnp.float32),
+            pltpu.SemaphoreType.DMA,
         ],
         compiler_params=pltpu.CompilerParams(vmem_limit_bytes=24 << 20),
         name="multiply",

time: 122 us -> 122 us (level)
  no operation moved by 1% of the time
where the time goes in v4:
time: 122 us; the launch traced here: 121 us
  starting transfers between devices  92.5 us (76%)
  waiting for transfers between devices  16.3 us (13%)
  Pallas kernels  7.3 us (6%)
  other arithmetic  3.76 us (3%)
    ppermute x10, starting transfers between devices, scatter(): arrived = [lax.ppermute(shards[k], axis, SCATTER[k]) for k in range(SHARDS)]  26.8 us
    ppermute x3, starting transfers between devices, program(): other = [lax.ppermute(part, 'row', SWAP_CORE) for part in mine]  14.2 us
    ppermute x3, starting transfers between devices, program(): lax.ppermute(b_first, 'row', to_plane(z))  9.32 us
    ppermute x3, starting transfers between devices, program(): after = lax.ppermute(after, ('row', 'col'), ring_x(1))  8.58 us
    ppermute x3, starting transfers between devices, program(): before = lax.ppermute(before, ('row', 'col'), ring_x(-1))  7.53 us
    pallas_call x1, Pallas kernels, multiply(): pl.pallas_call(kernel, out_shape=(jax.ShapeDtypeStruct((RESULTS, SIDE, SI...  6.44 us
    ppermute x1, starting transfers between devices, program(): block = jnp.concatenate([a_own, lax.ppermute(a_own, 'col', SWAP_Z)])  5.78 us
    ppermute x3, waiting for transfers between devices, program(): lax.ppermute(b_first, 'row', to_plane(z))  5.62 us
  transfers between devices with their start and end apart: 28, of which 5 were waited for; matrix products, arithmetic and copies ran while one was open for 2% of the time, Pallas kernels for 1%

profile of v4, /device:TPU:1, one launch (start us, length us, event | category | flops | bytes accessed | tf_op | source)
XLA Modules:
  0.0 120.9 jit_solution(12959185694513729478)
XLA Ops:
  0.0 1.7 %fusion = (f32[160,256]{1,0:T(8,128)S(1)}, f32[160,256]{1,0:T(8,128)S(1)}, f32[160,256]{1,0:T(8,128)S(1)}, f32[160,256]{1,0:T(8,128)S(1)}, f32[160,256]{1,0:T(8,...) fusion(f32[768,256]{1,0:T(8,128)} %bitcast.8, ...), kind=kLoop, calls=%fused_computation.9 | loop fusion | flops 163840 | bytes 3276984 | tf_op jit(solution)/shard_map/slice | solution.py:66
  1.7 5.7 %collective-permute-start.6 = (f32[160,256]{1,0:T(8,128)S(1)}, f32[160,256]{1,0:T(8,128)S(1)}, u32[]{:S(2)}, u32[]{:S(2)}) collective-permute-start(f32[160,256]{1,0:T(8,128)S(1)} %get-tuple-element.15), channel_id=1, source_target_pairs={{0,1},{1,13},{2,3},{16,17},{17,29},{18,19},{32,33},{33,45},{34,35}... | collective-permute-start | bytes 491528 | tf_op jit(solution)/shard_map/ppermute | solution.py:70
  7.4 2.0 %collective-permute-start.9 = (f32[160,256]{1,0:T(8,128)S(1)}, f32[160,256]{1,0:T(8,128)S(1)}, u32[]{:S(2)}, u32[]{:S(2)}) collective-permute-start(f32[160,256]{1,0:T(8,128)S(1)} %get-tuple-element.16), channel_id=1, source_target_pairs={{0,10},{1,9},{2,8},{16,26},{17,25},{18,24},{32,42},{33,41},{34,40}... | collective-permute-start | bytes 491528 | tf_op jit(solution)/shard_map/ppermute | solution.py:70
  9.4 1.3 %collective-permute-start.8 = (f32[160,256]{1,0:T(8,128)S(1)}, f32[160,256]{1,0:T(8,128)S(1)}, u32[]{:S(2)}, u32[]{:S(2)}) collective-permute-start(f32[160,256]{1,0:T(8,128)S(1)} %get-tuple-element.17), channel_id=1, source_target_pairs={{0,12},{1,7},{2,6},{16,28},{17,23},{18,22},{32,44},{33,39},{34,38}... | collective-permute-start | bytes 491528 | tf_op jit(solution)/shard_map/ppermute | solution.py:70
  10.8 1.3 %collective-permute-start.7 = (f32[160,256]{1,0:T(8,128)S(1)}, f32[160,256]{1,0:T(8,128)S(1)}, u32[]{:S(2)}, u32[]{:S(2)}) collective-permute-start(f32[160,256]{1,0:T(8,128)S(1)} %get-tuple-element.18), channel_id=1, source_target_pairs={{0,14},{1,5},{2,4},{16,30},{17,21},{18,20},{32,46},{33,37},{34,36}... | collective-permute-start | bytes 491528 | tf_op jit(solution)/shard_map/ppermute | solution.py:70
  13.3 5.9 %collective-permute-start = (f32[160,256]{1,0:T(8,128)S(1)}, f32[160,256]{1,0:T(8,128)S(1)}, u32[]{:S(2)}, u32[]{:S(2)}) collective-permute-start(f32[160,256]{1,0:T(8,128)S(1)} %get-tuple-element.25), channel_id=1, source_target_pairs={{16,240},{17,241},{18,242},{19,243},{20,244},{21,245},{22,246},{23... | collective-permute-start | bytes 491528 | tf_op jit(solution)/shard_map/ppermute | solution.py:70
  19.2 1.3 %collective-permute-start.2 = (f32[160,256]{1,0:T(8,128)S(1)}, f32[160,256]{1,0:T(8,128)S(1)}, u32[]{:S(2)}, u32[]{:S(2)}) collective-permute-start(f32[160,256]{1,0:T(8,128)S(1)} %get-tuple-element.26), channel_id=1, source_target_pairs={{0,224},{16,80},{32,64},{1,225},{17,81},{33,65},{2,226},{18,82},{3... | collective-permute-start | bytes 491528 | tf_op jit(solution)/shard_map/ppermute | solution.py:70
  20.5 1.3 %collective-permute-start.3 = (f32[160,256]{1,0:T(8,128)S(1)}, f32[160,256]{1,0:T(8,128)S(1)}, u32[]{:S(2)}, u32[]{:S(2)}) collective-permute-start(f32[160,256]{1,0:T(8,128)S(1)} %get-tuple-element.27), channel_id=1, source_target_pairs={{0,192},{16,112},{32,96},{1,193},{17,113},{33,97},{2,194},{18,114}... | collective-permute-start | bytes 491528 | tf_op jit(solution)/shard_map/ppermute | solution.py:70
  21.8 5.4 %collective-permute-start.4 = (f32[160,256]{1,0:T(8,128)S(1)}, f32[160,256]{1,0:T(8,128)S(1)}, u32[]{:S(2)}, u32[]{:S(2)}) collective-permute-start(f32[160,256]{1,0:T(8,128)S(1)} %get-tuple-element.28), channel_id=1, source_target_pairs={{0,160},{16,144},{32,128},{1,161},{17,145},{33,129},{2,162},{18,14... | collective-permute-start | bytes 491528 | tf_op jit(solution)/shard_map/ppermute | solution.py:70
  27.2 1.9 %collective-permute-start.1 = (f32[160,256]{1,0:T(8,128)S(1)}, f32[160,256]{1,0:T(8,128)S(1)}, u32[]{:S(2)}, u32[]{:S(2)}) collective-permute-start(f32[160,256]{1,0:T(8,128)S(1)} %get-tuple-element.29), channel_id=1, source_target_pairs={{0,16},{16,208},{32,48},{1,17},{17,209},{33,49},{2,18},{18,210},{3... | collective-permute-start | bytes 491528 | tf_op jit(solution)/shard_map/ppermute | solution.py:70
  30.2 5.8 %collective-permute-start.10 = (f32[160,256]{1,0:T(8,128)S(1)}, f32[160,256]{1,0:T(8,128)S(1)}, u32[]{:S(2)}, u32[]{:S(2)}) collective-permute-start(f32[160,256]{1,0:T(8,128)S(1)} %add_select_fusion), channel_id=1, source_target_pairs={{0,1},{1,0},{2,3},{3,2},{4,5},{5,4},{6,7},{7,6},{8,9},{9,8},{10,11... | collective-permute-start | bytes 491528 | tf_op jit(solution)/shard_map/ppermute | solution.py:218
  37.0 6.7 %collective-permute-start.20 = (f32[160,256]{1,0:T(8,128)S(1)}, f32[160,256]{1,0:T(8,128)S(1)}, u32[]{:S(2)}, u32[]{:S(2)}) collective-permute-start(f32[160,256]{1,0:T(8,128)S(1)} %add_select_fusion.1), channel_id=1, source_target_pairs={{0,768},{16,784},{32,800},{48,816},{64,832},{80,848},{96,864},{112... | collective-permute-start | bytes 491528 | tf_op jit(solution)/shard_map/ppermute | solution.py:216
  45.0 1.3 %collective-permute-start.18 = (f32[160,256]{1,0:T(8,128)S(1)}, f32[160,256]{1,0:T(8,128)S(1)}, u32[]{:S(2)}, u32[]{:S(2)}) collective-permute-start(f32[160,256]{1,0:T(8,128)S(1)} %add_select_fusion.1), channel_id=1, source_target_pairs={{0,256},{16,272},{32,288},{48,304},{64,320},{80,336},{96,352},{112... | collective-permute-start | bytes 491528 | tf_op jit(solution)/shard_map/ppermute | solution.py:216
  46.4 2.4 %collective-permute-start.11 = (f32[320,256]{1,0:T(8,128)S(1)}, f32[320,256]{1,0:T(8,128)S(1)}, u32[]{:S(2)}, u32[]{:S(2)}) collective-permute-start(f32[320,256]{1,0:T(8,128)S(1)} %pad_maximum_fusion.1.refs_0_), channel_id=1, source_target_pairs={{0,2},{1,3},{2,4},{3,5},{4,6},{5,7},{6,8},{7,9},{8,10},{9,11},{10,... | collective-permute-start | bytes 983048 | tf_op jit(solution)/shard_map/ppermute | solution.py:221
  48.8 5.6 %collective-permute-done.20 = f32[160,256]{1,0:T(8,128)S(1)} collective-permute-done((f32[160,256]{1,0:T(8,128)S(1)}, f32[160,256]{1,0:T(8,128)S(1)}, u32[]{:S(2)}, u32[]{:S(2)}) %collective-permute-start.20) | collective-permute-done | bytes 163872 | tf_op jit(solution)/shard_map/ppermute | solution.py:216
  54.4 3.3 %collective-permute-start.22 = (f32[160,256]{1,0:T(8,128)S(1)}, f32[160,256]{1,0:T(8,128)S(1)}, u32[]{:S(2)}, u32[]{:S(2)}) collective-permute-start(f32[160,256]{1,0:T(8,128)S(1)} %add_add_fusion), channel_id=1, source_target_pairs={{0,224},{16,48},{32,0},{48,80},{64,32},{80,112},{96,64},{112,144},... | collective-permute-start | bytes 491528 | tf_op jit(solution)/shard_map/ppermute | solution.py:227
  57.8 4.5 %collective-permute-start.21 = (f32[160,256]{1,0:T(8,128)S(1)}, f32[160,256]{1,0:T(8,128)S(1)}, u32[]{:S(2)}, u32[]{:S(2)}) collective-permute-start(f32[160,256]{1,0:T(8,128)S(1)} %add_add_fusion), channel_id=1, source_target_pairs={{0,32},{16,240},{32,64},{48,16},{64,96},{80,48},{96,128},{112,80},... | collective-permute-start | bytes 491528 | tf_op jit(solution)/shard_map/ppermute | solution.py:226
  62.3 1.9 %collective-permute-start.12 = (f32[320,256]{1,0:T(8,128)S(1)}, f32[320,256]{1,0:T(8,128)S(1)}, u32[]{:S(2)}, u32[]{:S(2)}) collective-permute-start(f32[320,256]{1,0:T(8,128)S(1)} %pad_maximum_fusion.1.refs_0_), channel_id=1, source_target_pairs={{0,14},{1,15},{2,0},{3,1},{4,2},{5,3},{6,4},{7,5},{8,6},{9,7},{10,... | collective-permute-start | bytes 983048 | tf_op jit(solution)/shard_map/ppermute | solution.py:222
  65.3 5.5 %collective-permute-start.23 = (f32[480,256]{1,0:T(8,128)S(1)}, f32[480,256]{1,0:T(8,128)S(1)}, u32[]{:S(2)}, u32[]{:S(2)}) collective-permute-start(f32[480,256]{1,0:T(8,128)S(1)} %pad_maximum_fusion.refs_5_.refs_9_), channel_id=1, source_target_pairs={{0,96},{16,176},{32,128},{48,208},{64,160},{80,240},{96,192},{112,... | collective-permute-start | bytes 1474568 | tf_op jit(solution)/shard_map/ppermute | solution.py:229
  70.8 2.8 %collective-permute-start.13 = (f32[320,256]{1,0:T(8,128)S(1)}, f32[320,256]{1,0:T(8,128)S(1)}, u32[]{:S(2)}, u32[]{:S(2)}) collective-permute-start(f32[320,256]{1,0:T(8,128)S(1)} %collective-permute-done.11.refs_1_), channel_id=1, source_target_pairs={{0,2},{1,3},{2,4},{3,5},{4,6},{5,7},{6,8},{7,9},{8,10},{9,11},{10,... | collective-permute-start | bytes 983048 | tf_op jit(solution)/shard_map/ppermute | solution.py:221
  73.6 3.1 %collective-permute-start.24 = (f32[320,256]{1,0:T(8,128)S(1)}, f32[320,256]{1,0:T(8,128)S(1)}, u32[]{:S(2)}, u32[]{:S(2)}) collective-permute-start(f32[320,256]{1,0:T(8,128)S(1)} %pad_maximum_fusion.2), channel_id=1, source_target_pairs={{0,192},{16,80},{32,224},{48,112},{64,0},{80,144},{96,32},{112,176... | collective-permute-start | bytes 983048 | tf_op jit(solution)/shard_map/ppermute | solution.py:230
  76.7 3.0 %collective-permute-start.14 = (f32[320,256]{1,0:T(8,128)S(1)}, f32[320,256]{1,0:T(8,128)S(1)}, u32[]{:S(2)}, u32[]{:S(2)}) collective-permute-start(f32[320,256]{1,0:T(8,128)S(1)} %collective-permute-done.12.refs_2_), channel_id=1, source_target_pairs={{0,14},{1,15},{2,0},{3,1},{4,2},{5,3},{6,4},{7,5},{8,6},{9,7},{10,... | collective-permute-start | bytes 983048 | tf_op jit(solution)/shard_map/ppermute | solution.py:222
  79.7 3.5 %collective-permute-start.15 = (f32[320,256]{1,0:T(8,128)S(1)}, f32[320,256]{1,0:T(8,128)S(1)}, u32[]{:S(2)}, u32[]{:S(2)}) collective-permute-start(f32[320,256]{1,0:T(8,128)S(1)} %collective-permute-done.13.refs_3_), channel_id=1, source_target_pairs={{0,2},{1,3},{2,4},{3,5},{4,6},{5,7},{6,8},{7,9},{8,10},{9,11},{10,... | collective-permute-start | bytes 983048 | tf_op jit(solution)/shard_map/ppermute | solution.py:221
  83.2 4.3 %collective-permute-start.26 = (f32[480,256]{1,0:T(8,128)S(1)}, f32[480,256]{1,0:T(8,128)S(1)}, u32[]{:S(2)}, u32[]{:S(2)}) collective-permute-start(f32[480,256]{1,0:T(8,128)S(1)} %pad_maximum_fusion.refs_5_.refs_9_), channel_id=1, source_target_pairs={{0,16},{16,0},{32,48},{48,32},{64,80},{80,64},{96,112},{112,96},{1... | collective-permute-start | bytes 1474568 | tf_op jit(solution)/shard_map/ppermute | solution.py:232
  87.5 4.4 %collective-permute-done.23.refs_8_ = f32[480,256]{1,0:T(8,128)S(1)} collective-permute-done((f32[480,256]{1,0:T(8,128)S(1)}, f32[480,256]{1,0:T(8,128)S(1)}, u32[]{:S(2)}, u32[]{:S(2)}) %collective-permute-start.23) | collective-permute-done | bytes 491552 | tf_op jit(solution)/shard_map/ppermute | solution.py:229
  91.8 8.1 %collective-permute-start.25 = (f32[480,256]{1,0:T(8,128)S(1)}, f32[480,256]{1,0:T(8,128)S(1)}, u32[]{:S(2)}, u32[]{:S(2)}) collective-permute-start(f32[480,256]{1,0:T(8,128)S(1)} %collective-permute-done.23.refs_8_), channel_id=1, source_target_pairs={{0,16},{16,0},{32,48},{48,32},{64,80},{80,64},{96,112},{112,96},{1... | collective-permute-start | bytes 1474568 | tf_op jit(solution)/shard_map/ppermute | solution.py:232
  99.9 1.9 %collective-permute-start.27 = (f32[320,256]{1,0:T(8,128)S(1)}, f32[320,256]{1,0:T(8,128)S(1)}, u32[]{:S(2)}, u32[]{:S(2)}) collective-permute-start(f32[320,256]{1,0:T(8,128)S(1)} %collective-permute-done.24.refs_10_), channel_id=1, source_target_pairs={{0,16},{16,0},{32,48},{48,32},{64,80},{80,64},{96,112},{112,96},{1... | collective-permute-start | bytes 983048 | tf_op jit(solution)/shard_map/ppermute | solution.py:232
  101.8 2.6 %collective-permute-start.16 = (f32[320,256]{1,0:T(8,128)S(1)}, f32[320,256]{1,0:T(8,128)S(1)}, u32[]{:S(2)}, u32[]{:S(2)}) collective-permute-start(f32[320,256]{1,0:T(8,128)S(1)} %collective-permute-done.14.refs_4_), channel_id=1, source_target_pairs={{0,14},{1,15},{2,0},{3,1},{4,2},{5,3},{6,4},{7,5},{8,6},{9,7},{10,... | collective-permute-start | bytes 983048 | tf_op jit(solution)/shard_map/ppermute | solution.py:222
  104.4 3.9 %collective-permute-start.17 = (f32[320,256]{1,0:T(8,128)S(1)}, f32[320,256]{1,0:T(8,128)S(1)}, u32[]{:S(2)}, u32[]{:S(2)}) collective-permute-start(f32[320,256]{1,0:T(8,128)S(1)} %collective-permute-done.15.refs_5_), channel_id=1, source_target_pairs={{0,2},{1,3},{2,4},{3,5},{4,6},{5,7},{6,8},{7,9},{8,10},{9,11},{10,... | collective-permute-start | bytes 983048 | tf_op jit(solution)/shard_map/ppermute | solution.py:224
  109.2 1.6 %collective-permute-done.16.refs_6_ = f32[320,256]{1,0:T(8,128)S(1)} collective-permute-done((f32[320,256]{1,0:T(8,128)S(1)}, f32[320,256]{1,0:T(8,128)S(1)}, u32[]{:S(2)}, u32[]{:S(2)}) %collective-permute-start.16) | collective-permute-done | bytes 327712 | tf_op jit(solution)/shard_map/ppermute | solution.py:222
  110.9 3.5 %collective-permute-done.17.refs_7_ = f32[320,256]{1,0:T(8,128)S(1)} collective-permute-done((f32[320,256]{1,0:T(8,128)S(1)}, f32[320,256]{1,0:T(8,128)S(1)}, u32[]{:S(2)}, u32[]{:S(2)}) %collective-permute-start.17) | collective-permute-done | bytes 327712 | tf_op jit(solution)/shard_map/ppermute | solution.py:224
  114.4 6.4 %multiply.1 = (f32[6,256,256]{2,1,0:T(8,128)}, bf16[2464,512]{1,0:T(8,128)(2,1)S(1)}, bf16[2464,512]{1,0:T(8,128)(2,1)S(1)}) custom-call(s32[85]{0:T(128)S(1)} %concatenate.12.ints, f32[320,256]{1,0:T(8,128)S(1)} %pad_maximum_fusion.1.refs_0_, f32[320,256]{1,0:T(8,128)S(1)} %collective-permute-done.11.refs_1_, ...), custom_call_target="tpu_custom_call", output_to_operand_aliasing={{1}: (15, {}), {2}: (16, {})} | custom-call | tf_op jit(solution)/shard_map/multiply/pallas_call | solution.py:183
  (47 shorter events, 6.6 us)
Async XLA Ops:
  0.0 13.2 %copy-start.3 = (s32[32]{0:T(128)S(1)}, s32[32]{0:T(128)}, u32[]{:S(2)}) copy-start(s32[32]{0:T(128)} %constant.17.clone) | copy-start | bytes 388
  0.0 12.8 %copy-start.1 = (s32[1,1,6,2]{2,3,1,0:T(2,128)S(1)}, s32[1,1,6,2]{2,3,1,0:T(2,128)}, u32[]{:S(2)}) copy-start(s32[1,1,6,2]{2,3,1,0:T(2,128)} %param.12) | copy-start | bytes 148
  0.0 12.9 %copy-start = (s32[1,1,3,6,2]{3,4,2,1,0:T(2,128)S(1)}, s32[1,1,3,6,2]{3,4,2,1,0:T(2,128)}, u32[]{:S(2)}) copy-start(s32[1,1,3,6,2]{3,4,2,1,0:T(2,128)} %param.13) | copy-start | bytes 436
  0.0 13.2 %copy-start.2 = (s32[1,1,3]{2,1,0:T(1,128)S(1)}, s32[1,1,3]{2,1,0:T(1,128)}, u32[]{:S(2)}) copy-start(s32[1,1,3]{2,1,0:T(1,128)} %param.14) | copy-start | bytes 40
  1.7 11.6 %collective-permute-start.6 = (f32[160,256]{1,0:T(8,128)S(1)}, f32[160,256]{1,0:T(8,128)S(1)}, u32[]{:S(2)}, u32[]{:S(2)}) collective-permute-start(f32[160,256]{1,0:T(8,128)S(1)} %get-tuple-element.15), channel_id=1, source_target_pairs={{0,1},{1,13},{2,3},{16,17},{17,29},{18,19},{32,33},{33,45},{34,35}... | collective-permute-start | bytes 491528 | tf_op jit(solution)/shard_map/ppermute | solution.py:70
  7.4 11.7 %collective-permute-start.9 = (f32[160,256]{1,0:T(8,128)S(1)}, f32[160,256]{1,0:T(8,128)S(1)}, u32[]{:S(2)}, u32[]{:S(2)}) collective-permute-start(f32[160,256]{1,0:T(8,128)S(1)} %get-tuple-element.16), channel_id=1, source_target_pairs={{0,10},{1,9},{2,8},{16,26},{17,25},{18,24},{32,42},{33,41},{34,40}... | collective-permute-start | bytes 491528 | tf_op jit(solution)/shard_map/ppermute | solution.py:70
  9.4 11.0 %collective-permute-start.8 = (f32[160,256]{1,0:T(8,128)S(1)}, f32[160,256]{1,0:T(8,128)S(1)}, u32[]{:S(2)}, u32[]{:S(2)}) collective-permute-start(f32[160,256]{1,0:T(8,128)S(1)} %get-tuple-element.17), channel_id=1, source_target_pairs={{0,12},{1,7},{2,6},{16,28},{17,23},{18,22},{32,44},{33,39},{34,38}... | collective-permute-start | bytes 491528 | tf_op jit(solution)/shard_map/ppermute | solution.py:70
  10.8 11.0 %collective-permute-start.7 = (f32[160,256]{1,0:T(8,128)S(1)}, f32[160,256]{1,0:T(8,128)S(1)}, u32[]{:S(2)}, u32[]{:S(2)}) collective-permute-start(f32[160,256]{1,0:T(8,128)S(1)} %get-tuple-element.18), channel_id=1, source_target_pairs={{0,14},{1,5},{2,4},{16,30},{17,21},{18,20},{32,46},{33,37},{34,36}... | collective-permute-start | bytes 491528 | tf_op jit(solution)/shard_map/ppermute | solution.py:70
  12.1 15.2 %collective-permute-start.5 = (f32[160,256]{1,0:T(8,128)S(1)}, f32[160,256]{1,0:T(8,128)S(1)}, u32[]{:S(2)}, u32[]{:S(2)}) collective-permute-start(f32[160,256]{1,0:T(8,128)S(1)} %get-tuple-element.19), channel_id=1, source_target_pairs={{1,15},{17,31},{33,47},{49,63},{65,79},{81,95},{97,111},{113,127},... | collective-permute-start | bytes 491528 | tf_op jit(solution)/shard_map/ppermute | solution.py:70
  13.3 16.9 %collective-permute-start = (f32[160,256]{1,0:T(8,128)S(1)}, f32[160,256]{1,0:T(8,128)S(1)}, u32[]{:S(2)}, u32[]{:S(2)}) collective-permute-start(f32[160,256]{1,0:T(8,128)S(1)} %get-tuple-element.25), channel_id=1, source_target_pairs={{16,240},{17,241},{18,242},{19,243},{20,244},{21,245},{22,246},{23... | collective-permute-start | bytes 491528 | tf_op jit(solution)/shard_map/ppermute | solution.py:70
  19.2 16.8 %collective-permute-start.2 = (f32[160,256]{1,0:T(8,128)S(1)}, f32[160,256]{1,0:T(8,128)S(1)}, u32[]{:S(2)}, u32[]{:S(2)}) collective-permute-start(f32[160,256]{1,0:T(8,128)S(1)} %get-tuple-element.26), channel_id=1, source_target_pairs={{0,224},{16,80},{32,64},{1,225},{17,81},{33,65},{2,226},{18,82},{3... | collective-permute-start | bytes 491528 | tf_op jit(solution)/shard_map/ppermute | solution.py:70
  20.5 15.5 %collective-permute-start.3 = (f32[160,256]{1,0:T(8,128)S(1)}, f32[160,256]{1,0:T(8,128)S(1)}, u32[]{:S(2)}, u32[]{:S(2)}) collective-permute-start(f32[160,256]{1,0:T(8,128)S(1)} %get-tuple-element.27), channel_id=1, source_target_pairs={{0,192},{16,112},{32,96},{1,193},{17,113},{33,97},{2,194},{18,114}... | collective-permute-start | bytes 491528 | tf_op jit(solution)/shard_map/ppermute | solution.py:70
  21.8 14.2 %collective-permute-start.4 = (f32[160,256]{1,0:T(8,128)S(1)}, f32[160,256]{1,0:T(8,128)S(1)}, u32[]{:S(2)}, u32[]{:S(2)}) collective-permute-start(f32[160,256]{1,0:T(8,128)S(1)} %get-tuple-element.28), channel_id=1, source_target_pairs={{0,160},{16,144},{32,128},{1,161},{17,145},{33,129},{2,162},{18,14... | collective-permute-start | bytes 491528 | tf_op jit(solution)/shard_map/ppermute | solution.py:70
  27.2 8.8 %collective-permute-start.1 = (f32[160,256]{1,0:T(8,128)S(1)}, f32[160,256]{1,0:T(8,128)S(1)}, u32[]{:S(2)}, u32[]{:S(2)}) collective-permute-start(f32[160,256]{1,0:T(8,128)S(1)} %get-tuple-element.29), channel_id=1, source_target_pairs={{0,16},{16,208},{32,48},{1,17},{17,209},{33,49},{2,18},{18,210},{3... | collective-permute-start | bytes 491528 | tf_op jit(solution)/shard_map/ppermute | solution.py:70
  30.2 16.2 %collective-permute-start.10 = (f32[160,256]{1,0:T(8,128)S(1)}, f32[160,256]{1,0:T(8,128)S(1)}, u32[]{:S(2)}, u32[]{:S(2)}) collective-permute-start(f32[160,256]{1,0:T(8,128)S(1)} %add_select_fusion), channel_id=1, source_target_pairs={{0,1},{1,0},{2,3},{3,2},{4,5},{5,4},{6,7},{7,6},{8,9},{9,8},{10,11... | collective-permute-start | bytes 491528 | tf_op jit(solution)/shard_map/ppermute | solution.py:218
  37.0 17.4 %collective-permute-start.20 = (f32[160,256]{1,0:T(8,128)S(1)}, f32[160,256]{1,0:T(8,128)S(1)}, u32[]{:S(2)}, u32[]{:S(2)}) collective-permute-start(f32[160,256]{1,0:T(8,128)S(1)} %add_select_fusion.1), channel_id=1, source_target_pairs={{0,768},{16,784},{32,800},{48,816},{64,832},{80,848},{96,864},{112... | collective-permute-start | bytes 491528 | tf_op jit(solution)/shard_map/ppermute | solution.py:216
  43.7 10.6 %collective-permute-start.19 = (f32[160,256]{1,0:T(8,128)S(1)}, f32[160,256]{1,0:T(8,128)S(1)}, u32[]{:S(2)}, u32[]{:S(2)}) collective-permute-start(f32[160,256]{1,0:T(8,128)S(1)} %add_select_fusion.1), channel_id=1, source_target_pairs={{0,512},{16,528},{32,544},{48,560},{64,576},{80,592},{96,608},{112... | collective-permute-start | bytes 491528 | tf_op jit(solution)/shard_map/ppermute | solution.py:216
  45.0 9.3 %collective-permute-start.18 = (f32[160,256]{1,0:T(8,128)S(1)}, f32[160,256]{1,0:T(8,128)S(1)}, u32[]{:S(2)}, u32[]{:S(2)}) collective-permute-start(f32[160,256]{1,0:T(8,128)S(1)} %add_select_fusion.1), channel_id=1, source_target_pairs={{0,256},{16,272},{32,288},{48,304},{64,320},{80,336},{96,352},{112... | collective-permute-start | bytes 491528 | tf_op jit(solution)/shard_map/ppermute | solution.py:216
  46.4 24.4 %collective-permute-start.11 = (f32[320,256]{1,0:T(8,128)S(1)}, f32[320,256]{1,0:T(8,128)S(1)}, u32[]{:S(2)}, u32[]{:S(2)}) collective-permute-start(f32[320,256]{1,0:T(8,128)S(1)} %pad_maximum_fusion.1.refs_0_), channel_id=1, source_target_pairs={{0,2},{1,3},{2,4},{3,5},{4,6},{5,7},{6,8},{7,9},{8,10},{9,11},{10,... | collective-permute-start | bytes 983048 | tf_op jit(solution)/shard_map/ppermute | solution.py:221
  54.4 9.8 %collective-permute-start.22 = (f32[160,256]{1,0:T(8,128)S(1)}, f32[160,256]{1,0:T(8,128)S(1)}, u32[]{:S(2)}, u32[]{:S(2)}) collective-permute-start(f32[160,256]{1,0:T(8,128)S(1)} %add_add_fusion), channel_id=1, source_target_pairs={{0,224},{16,48},{32,0},{48,80},{64,32},{80,112},{96,64},{112,144},... | collective-permute-start | bytes 491528 | tf_op jit(solution)/shard_map/ppermute | solution.py:227
  57.8 7.5 %collective-permute-start.21 = (f32[160,256]{1,0:T(8,128)S(1)}, f32[160,256]{1,0:T(8,128)S(1)}, u32[]{:S(2)}, u32[]{:S(2)}) collective-permute-start(f32[160,256]{1,0:T(8,128)S(1)} %add_add_fusion), channel_id=1, source_target_pairs={{0,32},{16,240},{32,64},{48,16},{64,96},{80,48},{96,128},{112,80},... | collective-permute-start | bytes 491528 | tf_op jit(solution)/shard_map/ppermute | solution.py:226
  62.3 14.4 %collective-permute-start.12 = (f32[320,256]{1,0:T(8,128)S(1)}, f32[320,256]{1,0:T(8,128)S(1)}, u32[]{:S(2)}, u32[]{:S(2)}) collective-permute-start(f32[320,256]{1,0:T(8,128)S(1)} %pad_maximum_fusion.1.refs_0_), channel_id=1, source_target_pairs={{0,14},{1,15},{2,0},{3,1},{4,2},{5,3},{6,4},{7,5},{8,6},{9,7},{10,... | collective-permute-start | bytes 983048 | tf_op jit(solution)/shard_map/ppermute | solution.py:222
  65.3 26.5 %collective-permute-start.23 = (f32[480,256]{1,0:T(8,128)S(1)}, f32[480,256]{1,0:T(8,128)S(1)}, u32[]{:S(2)}, u32[]{:S(2)}) collective-permute-start(f32[480,256]{1,0:T(8,128)S(1)} %pad_maximum_fusion.refs_5_.refs_9_), channel_id=1, source_target_pairs={{0,96},{16,176},{32,128},{48,208},{64,160},{80,240},{96,192},{112,... | collective-permute-start | bytes 1474568 | tf_op jit(solution)/shard_map/ppermute | solution.py:229
  70.8 8.9 %collective-permute-start.13 = (f32[320,256]{1,0:T(8,128)S(1)}, f32[320,256]{1,0:T(8,128)S(1)}, u32[]{:S(2)}, u32[]{:S(2)}) collective-permute-start(f32[320,256]{1,0:T(8,128)S(1)} %collective-permute-done.11.refs_1_), channel_id=1, source_target_pairs={{0,2},{1,3},{2,4},{3,5},{4,6},{5,7},{6,8},{7,9},{8,10},{9,11},{10,... | collective-permute-start | bytes 983048 | tf_op jit(solution)/shard_map/ppermute | solution.py:221
  73.6 26.3 %collective-permute-start.24 = (f32[320,256]{1,0:T(8,128)S(1)}, f32[320,256]{1,0:T(8,128)S(1)}, u32[]{:S(2)}, u32[]{:S(2)}) collective-permute-start(f32[320,256]{1,0:T(8,128)S(1)} %pad_maximum_fusion.2), channel_id=1, source_target_pairs={{0,192},{16,80},{32,224},{48,112},{64,0},{80,144},{96,32},{112,176... | collective-permute-start | bytes 983048 | tf_op jit(solution)/shard_map/ppermute | solution.py:230
  76.7 25.2 %collective-permute-start.14 = (f32[320,256]{1,0:T(8,128)S(1)}, f32[320,256]{1,0:T(8,128)S(1)}, u32[]{:S(2)}, u32[]{:S(2)}) collective-permute-start(f32[320,256]{1,0:T(8,128)S(1)} %collective-permute-done.12.refs_2_), channel_id=1, source_target_pairs={{0,14},{1,15},{2,0},{3,1},{4,2},{5,3},{6,4},{7,5},{8,6},{9,7},{10,... | collective-permute-start | bytes 983048 | tf_op jit(solution)/shard_map/ppermute | solution.py:222
  79.7 24.7 %collective-permute-start.15 = (f32[320,256]{1,0:T(8,128)S(1)}, f32[320,256]{1,0:T(8,128)S(1)}, u32[]{:S(2)}, u32[]{:S(2)}) collective-permute-start(f32[320,256]{1,0:T(8,128)S(1)} %collective-permute-done.13.refs_3_), channel_id=1, source_target_pairs={{0,2},{1,3},{2,4},{3,5},{4,6},{5,7},{6,8},{7,9},{8,10},{9,11},{10,... | collective-permute-start | bytes 983048 | tf_op jit(solution)/shard_map/ppermute | solution.py:221
  83.2 25.2 %collective-permute-start.26 = (f32[480,256]{1,0:T(8,128)S(1)}, f32[480,256]{1,0:T(8,128)S(1)}, u32[]{:S(2)}, u32[]{:S(2)}) collective-permute-start(f32[480,256]{1,0:T(8,128)S(1)} %pad_maximum_fusion.refs_5_.refs_9_), channel_id=1, source_target_pairs={{0,16},{16,0},{32,48},{48,32},{64,80},{80,64},{96,112},{112,96},{1... | collective-permute-start | bytes 1474568 | tf_op jit(solution)/shard_map/ppermute | solution.py:232
  91.8 19.0 %collective-permute-start.25 = (f32[480,256]{1,0:T(8,128)S(1)}, f32[480,256]{1,0:T(8,128)S(1)}, u32[]{:S(2)}, u32[]{:S(2)}) collective-permute-start(f32[480,256]{1,0:T(8,128)S(1)} %collective-permute-done.23.refs_8_), channel_id=1, source_target_pairs={{0,16},{16,0},{32,48},{48,32},{64,80},{80,64},{96,112},{112,96},{1... | collective-permute-start | bytes 1474568 | tf_op jit(solution)/shard_map/ppermute | solution.py:232
  99.9 9.3 %collective-permute-start.27 = (f32[320,256]{1,0:T(8,128)S(1)}, f32[320,256]{1,0:T(8,128)S(1)}, u32[]{:S(2)}, u32[]{:S(2)}) collective-permute-start(f32[320,256]{1,0:T(8,128)S(1)} %collective-permute-done.24.refs_10_), channel_id=1, source_target_pairs={{0,16},{16,0},{32,48},{48,32},{64,80},{80,64},{96,112},{112,96},{1... | collective-permute-start | bytes 983048 | tf_op jit(solution)/shard_map/ppermute | solution.py:232
  101.8 9.0 %collective-permute-start.16 = (f32[320,256]{1,0:T(8,128)S(1)}, f32[320,256]{1,0:T(8,128)S(1)}, u32[]{:S(2)}, u32[]{:S(2)}) collective-permute-start(f32[320,256]{1,0:T(8,128)S(1)} %collective-permute-done.14.refs_4_), channel_id=1, source_target_pairs={{0,14},{1,15},{2,0},{3,1},{4,2},{5,3},{6,4},{7,5},{8,6},{9,7},{10,... | collective-permute-start | bytes 983048 | tf_op jit(solution)/shard_map/ppermute | solution.py:222
  104.4 10.0 %collective-permute-start.17 = (f32[320,256]{1,0:T(8,128)S(1)}, f32[320,256]{1,0:T(8,128)S(1)}, u32[]{:S(2)}, u32[]{:S(2)}) collective-permute-start(f32[320,256]{1,0:T(8,128)S(1)} %collective-permute-done.15.refs_5_), channel_id=1, source_target_pairs={{0,2},{1,3},{2,4},{3,5},{4,6},{5,7},{6,8},{7,9},{8,10},{9,11},{10,... | collective-permute-start | bytes 983048 | tf_op jit(solution)/shard_map/ppermute | solution.py:224
